TPU v7x, 512 devices: a whole 4x4x16 slice. The times are simulated.
512 devices in a mesh: space: 256 (over y, z, x), feat: 2 (over core).
Axes of the slice: x: 4, y: 4, z: 16, core: 2. Of those that a mesh axis runs over, the one named last changes fastest.
Arguments:
- nodes: bfloat16 [40960, 512], P('space'), may hold values from -6 to 6
- edges: bfloat16 [196608, 512], P(('space', 'feat')), may hold values from -6 to 6
- senders: int32 [196608], P(('space', 'feat')), may hold values from 0 to 40959, as said below
- receivers: int32 [196608], P(('space', 'feat')), may hold values from 0 to 40959, as said below
- edge_proj: bfloat16 [512, 512], replicated, may hold values from -0.15625 to 0.15625
- send_proj: bfloat16 [512, 512], replicated, may hold values from -0.15625 to 0.15625
- recv_proj: bfloat16 [512, 512], replicated, may hold values from -0.15625 to 0.15625
- edge_bias: float32 [512], replicated, may hold values from -3 to 3
- edge_out: bfloat16 [512, 512], replicated, may hold values from -0.25 to 0.25
- edge_gain: float32 [512], replicated, may hold values from 0.25 to 1.75
- edge_shift: float32 [512], replicated, may hold values from -3 to 3
- node_in: bfloat16 [1024, 512], replicated, may hold values from -0.1875 to 0.1875
- node_bias: float32 [512], replicated, may hold values from -3 to 3
- node_out: bfloat16 [512, 512], replicated, may hold values from -0.25 to 0.25
- node_gain: float32 [512], replicated, may hold values from 0.25 to 1.75
- node_shift: float32 [512], replicated, may hold values from -3 to 3
- node_cot: bfloat16 [40960, 512], P('space'), may hold values from -6 to 6
Outputs:
- new_nodes: bfloat16 [40960, 512], P('space')
- node_grad: bfloat16 [40960, 512], P('space')
- edge_grad: bfloat16 [196608, 512], P(('space', 'feat'))
Inputs may be any that keep to these rules, and one draw needn't show every extreme that they name: `senders`: every edge of a block's 768 has its receiver in that block; its sender lies in the same block, in the last 48 rows of the previous block, in the first 48 rows of the next block, or among the first 2 rows of any block. `receivers`: every edge of a block's 768 has its receiver among that block's 160 nodes.
All inputs are finite; a program needn't handle non-finite values.
Results may differ from a plain program's by a relative error of at most 0.0077.
Values may be sent and summed in bfloat16 or wider, within the bound.
No kernel may reach another device: no remote copies, remote signals or barrier semaphores. Data moves between devices by JAX's collectives and lax.ppermute only.
A program may use at most 64 MiB of HBM per device.

v0:
```python
import jax
import jax.numpy as jnp
from jax import lax
from jax.sharding import PartitionSpec as P

RIM = 48
HUB_DEV = 2


epsilon = 1e-05


def padded(block, sides, width):
    for axis, dim in sides:
        count = lax.axis_size(axis)
        forward = [(i, i + 1) for i in range(count - 1)]
        backward = [(target, source) for source, target in forward]
        low = lax.ppermute(
            lax.slice_in_dim(block, block.shape[dim] - width, None, axis=dim), axis, forward
        )
        high = lax.ppermute(lax.slice_in_dim(block, 0, width, axis=dim), axis, backward)
        block = jnp.concatenate([low, block, high], axis=dim)
    return block


def layer_stats(values):
    average = jnp.mean(values, axis=-1, keepdims=True)
    centred = values - average
    inv_scale = lax.rsqrt(jnp.mean(centred * centred, axis=-1, keepdims=True) + epsilon)
    return (centred * inv_scale, inv_scale)


def norm_back(upstream, normed, inv_scale, gain_vec):
    scaled = upstream * gain_vec
    return inv_scale * (
        scaled
        - jnp.mean(scaled, axis=-1, keepdims=True)
        - normed * jnp.mean(scaled * normed, axis=-1, keepdims=True)
    )


def swish_slope(preact):
    sigmoid_val = jax.nn.sigmoid(preact)
    return sigmoid_val * (1.0 + preact * (1.0 - sigmoid_val))


def feat_total(partial_sum):
    return lax.psum(partial_sum, "feat")


def column_sums(onehot, values):
    return lax.dot_general(
        onehot, values, (((0,), (0,)), ((), ())), preferred_element_type=jnp.float32
    )


def exact_dot(left, right):
    return jnp.dot(left, right, precision=lax.Precision.HIGHEST)


def body(
    nodes,
    edges,
    senders,
    receivers,
    edge_proj,
    send_proj,
    recv_proj,
    edge_bias,
    edge_out,
    edge_gain,
    edge_shift,
    node_in,
    node_bias,
    node_out,
    node_gain,
    node_shift,
    node_cot,
):
    node_count = nodes.shape[0]
    width = nodes.shape[1]
    feat_count = lax.axis_size("feat")
    feat_index = lax.axis_index("feat")
    own_block = lax.axis_index("space")
    hub_total = HUB_DEV * lax.axis_size("space")
    table_count = 2 * RIM + node_count + hub_total
    edge_rows = lax.all_gather(edges, "feat", axis=0, tiled=True)
    send_ids, recv_ids = (
        lax.all_gather(senders, "feat", axis=0, tiled=True),
        lax.all_gather(receivers, "feat", axis=0, tiled=True),
    )
    half_width = width // feat_count
    col_start = feat_index * half_width
    w_edge = lax.dynamic_slice_in_dim(edge_proj, col_start, half_width, 1)
    w_send = lax.dynamic_slice_in_dim(send_proj, col_start, half_width, 1)
    w_recv = lax.dynamic_slice_in_dim(recv_proj, col_start, half_width, 1)
    bias_part = lax.dynamic_slice_in_dim(edge_bias, col_start, half_width, 0)
    w_out = lax.dynamic_slice_in_dim(edge_out, col_start, half_width, 0)
    edge_count = edge_rows.shape[0]
    sender_block = send_ids // node_count
    sender_row = send_ids - sender_block * node_count
    from_own = sender_block == own_block
    from_left = (sender_block == own_block - 1) & (sender_row >= node_count - RIM)
    from_right = (sender_block == own_block + 1) & (sender_row < RIM)
    slot_index = jnp.where(
        from_own,
        RIM + sender_row,
        jnp.where(
            from_left,
            sender_row - (node_count - RIM),
            jnp.where(
                from_right,
                RIM + node_count + sender_row,
                2 * RIM + node_count + sender_block * HUB_DEV + sender_row,
            ),
        ),
    )
    local_recv = recv_ids - own_block * node_count
    slot_onehot = (slot_index[:, None] == jnp.arange(table_count, dtype=jnp.int32)[None, :]).astype(
        jnp.bfloat16
    )
    recv_onehot = (local_recv[:, None] == jnp.arange(node_count, dtype=jnp.int32)[None, :]).astype(
        jnp.bfloat16
    )
    framed = padded(nodes, (("space", 0),), RIM)
    coarse = lax.all_gather(nodes[:HUB_DEV], "space", axis=0, tiled=True)
    table_rows = jnp.concatenate([framed, coarse], axis=0)
    send_terms = jnp.dot(table_rows, w_send, preferred_element_type=jnp.float32).astype(
        jnp.bfloat16
    )
    recv_terms = jnp.dot(nodes, w_recv, preferred_element_type=jnp.float32).astype(jnp.bfloat16)
    hidden_pre = (
        jnp.dot(edge_rows, w_edge, preferred_element_type=jnp.float32)
        + jnp.dot(slot_onehot, send_terms, preferred_element_type=jnp.float32)
        + jnp.dot(recv_onehot, recv_terms, preferred_element_type=jnp.float32)
        + bias_part
    )
    hidden_act = jax.nn.silu(hidden_pre).astype(jnp.bfloat16)
    edge_sum = jnp.dot(hidden_act, w_out, preferred_element_type=jnp.float32)
    edge_sum = feat_total(edge_sum)
    edge_normed, edge_scale = layer_stats(edge_sum)
    new_edges = (edge_rows.astype(jnp.float32) + edge_normed * edge_gain + edge_shift).astype(
        jnp.bfloat16
    )
    gathered_wide = column_sums(recv_onehot, new_edges)
    gathered = gathered_wide.astype(jnp.bfloat16)
    node_pre = (
        jnp.dot(nodes, node_in[:width], preferred_element_type=jnp.float32)
        + jnp.dot(gathered, node_in[width:], preferred_element_type=jnp.float32)
        + node_bias
    )
    node_act = jax.nn.silu(node_pre).astype(jnp.bfloat16)
    node_mix = jnp.dot(node_act, node_out, preferred_element_type=jnp.float32)
    node_normed, node_scale = layer_stats(node_mix)
    new_nodes = (nodes.astype(jnp.float32) + node_normed * node_gain + node_shift).astype(
        jnp.bfloat16
    )
    upstream = node_cot.astype(jnp.float32)
    node_dmix = norm_back(upstream, node_normed, node_scale, node_gain).astype(jnp.bfloat16)
    node_dact = jnp.dot(node_dmix, node_out.T, preferred_element_type=jnp.float32)
    node_dpre = (node_dact * swish_slope(node_pre)).astype(jnp.bfloat16)
    node_direct = upstream + jnp.dot(
        node_dpre, node_in[:width].T, preferred_element_type=jnp.float32
    )
    gathered_grad = jnp.dot(node_dpre, node_in[width:].T, preferred_element_type=jnp.float32)
    edge_upstream = exact_dot(recv_onehot.astype(jnp.float32), gathered_grad)
    edge_dsum = norm_back(edge_upstream, edge_normed, edge_scale, edge_gain).astype(jnp.bfloat16)
    edge_dact = jnp.dot(edge_dsum, w_out.T, preferred_element_type=jnp.float32)
    edge_dpre = (edge_dact * swish_slope(hidden_pre)).astype(jnp.bfloat16)
    edge_part = jnp.dot(edge_dpre, w_edge.T, preferred_element_type=jnp.float32)
    recv_sums = column_sums(recv_onehot, edge_dpre)
    slot_sums = column_sums(slot_onehot, edge_dpre)
    recv_part = exact_dot(recv_sums, w_recv.astype(jnp.float32).T)
    slot_sums = exact_dot(slot_sums, w_send.astype(jnp.float32).T)
    rim_terms = jnp.concatenate(
        [slot_sums[:RIM], slot_sums[RIM + node_count : 2 * RIM + node_count]], axis=0
    )
    rim_back = padded(rim_terms.astype(jnp.bfloat16), (("space", 0),), RIM).astype(rim_terms.dtype)
    hub_back = lax.psum_scatter(
        slot_sums[2 * RIM + node_count :], "space", scatter_dimension=0, tiled=True
    )
    own_terms = slot_sums[RIM : RIM + node_count]
    own_terms = own_terms + jnp.pad(rim_back[:RIM], ((0, node_count - RIM), (0, 0)))
    own_terms = own_terms + jnp.pad(rim_back[3 * RIM :], ((node_count - RIM, 0), (0, 0)))
    own_terms = own_terms + jnp.pad(hub_back, ((0, node_count - HUB_DEV), (0, 0)))
    totals = feat_total(jnp.concatenate([edge_part, own_terms + recv_part], axis=0))
    edge_full = edge_upstream + totals[:edge_count]
    node_extra = totals[edge_count:]
    own_edges = edge_count // feat_count
    edge_grad = lax.dynamic_slice_in_dim(edge_full, feat_index * own_edges, own_edges, 0).astype(
        jnp.bfloat16
    )
    node_grad = (node_direct + node_extra).astype(jnp.bfloat16)
    return (new_nodes, node_grad, edge_grad)


def solution(mesh):
    in_specs = (
        P("space", None),
        P(("space", "feat"), None),
        P(("space", "feat")),
        P(("space", "feat")),
        P(),
        P(),
        P(),
        P(),
        P(),
        P(),
        P(),
        P(),
        P(),
        P(),
        P(),
        P(),
        P("space", None),
    )
    out_specs = (P("space", None), P("space", None), P(("space", "feat"), None))
    return jax.shard_map(body, mesh=mesh, in_specs=in_specs, out_specs=out_specs, check_vma=False)
```

profile of v0, /device:TPU:1, one launch (start us, length us, event | category | flops | bytes accessed | tf_op | source)
XLA Modules:
  0.0 1228.4 jit_solution(10893948422444881251)
XLA Ops:
  7.2 0.9 fusion.104
  8.1 3.9 collective-permute-start
  12.1 1.3 collective-permute-start.1
  13.4 0.7 slice_bitcast_fusion
  14.1 0.7 reshape.54
  14.8 5.7 all-gather
  20.5 2.6 all_gather.13
  23.0 0.7 reshape.56
  23.7 1.8 all-gather.1
  25.6 579.3 %all-gather.2 = bf16[256,2,512]{2,1,0:T(2,128)(2,1)S(1)} all-gather(bf16[1,2,512]{2,1,0:T(2,128)(2,1)S(1)} %slice_bitcast_fusion), channel_id=1, replica_groups=mesh['space'=256,'feat'=2] {'space'}, dimensions={0}, use_global_device_ids=true | all-gather | bytes 526336 | tf_op jit(solution)/shard_map/all_gather | solution.py:126
  604.9 1.5 fusion.14
  606.4 2.2 convolution_bitcast_fusion
  608.8 1.0 reshape.59
  609.8 3.3 fusion.4
  613.1 2.7 fusion.52
  615.9 1.1 copy-done.6
  617.1 0.2 fusion.47
  617.4 137.1 %all-reduce.7.cloned.1.call-done = f32[768,512]{1,0:T(8,128)} async-done(((f32[768,512]{1,0:T(8,128)}), f32[768,512]{1,0:T(8,128)}) %all-reduce.7.cloned.1.call-update) | async-done | bytes 1572880 | tf_op jit(solution)/shard_map/psum | solution.py:48
  754.4 1.7 reduce_sum.72
  756.3 0.3 multiply_reduce_fusion.1
  756.7 2.7 fusion.6
  759.4 1.6 fusion.105
  761.2 0.8 fusion.51
  762.1 0.3 fusion.12
  762.5 0.7 copy-done.11
  763.3 0.3 fusion.43
  763.7 1.2 multiply_reduce_fusion.2
  764.9 1.3 fusion.5
  766.3 0.7 fusion.8
  766.9 0.8 fusion.106
  767.8 1.1 copy-done.2
  768.9 1.0 slice.63
  770.0 1.3 dynamic-slice
  772.0 2.1 collective-permute-start.2
  774.1 1.3 collective-permute-start.3
  775.4 1.4 fusion.77
  776.8 1.2 fusion.53
  778.0 1.0 collective-permute-done.3
  778.9 0.6 maximum_convert_fusion.1
  779.6 385.9 %all-reduce.11.cloned.1.call-done = f32[512,512]{1,0:T(8,128)} async-done(((f32[512,512]{1,0:T(8,128)}), f32[512,512]{1,0:T(8,128)}) %all-reduce.11.cloned.1.call-update) | async-done | bytes 1048592
  1165.5 0.7 constant_dynamic-slice_fusion
  1166.2 1.6 convolution_add_fusion
  1167.8 1.4 pad_maximum_fusion
  1169.2 48.5 %all-reduce.9.cloned.1.call-done = f32[928,512]{1,0:T(8,128)} async-done(((f32[928,512]{1,0:T(8,128)}), f32[928,512]{1,0:T(8,128)}) %all-reduce.9.cloned.1.call-update) | async-done | bytes 1900560 | tf_op jit(solution)/shard_map/psum | solution.py:48
  1217.8 1.4 slice-done
  1219.2 0.9 fusion.15
  1220.0 0.8 copy-done.5
  1220.8 1.0 fusion.13
  (74 shorter events, 1.1 us)
Async XLA Ops:
  7.2 602.6 %copy-start = (bf16[512,512]{1,0:T(8,128)(2,1)S(1)}, bf16[512,512]{1,0:T(8,128)(2,1)}, u32[]{:S(2)}) copy-start(bf16[512,512]{1,0:T(8,128)(2,1)} %param.22) | copy-start | bytes 1572868
  7.2 597.7 %copy-start.8 = (bf16[160,512]{1,0:T(8,128)(2,1)S(1)}, bf16[160,512]{1,0:T(8,128)(2,1)}, u32[]{:S(2)}) copy-start(bf16[160,512]{1,0:T(8,128)(2,1)} %param.17) | copy-start | bytes 491524
  7.2 747.2 %all-reduce.7.cloned.1.call-start = ((), (), s32[]{:S(2)}) async-start(), calls=%async_computation | async-start | bytes 3145728 | tf_op jit(solution)/shard_map/psum | solution.py:48
  8.1 601.6 %collective-permute-start = (bf16[48,512]{1,0:T(8,128)(2,1)S(1)}, bf16[48,512]{1,0:T(8,128)(2,1)S(1)}, u32[]{:S(2)}, u32[]{:S(2)}) collective-permute-start(bf16[48,512]{1,0:T(8,128)(2,1)S(1)} %get-tuple-element.10), channel_id=1, source_target_pairs={{0,2},{2,4},{4,6},{6,8},{8,10},{10,12},{12,14},{14,16},{16,18},{18... | collective-permute-start | bytes 147464 | tf_op jit(solution)/shard_map/ppermute | solution.py:18
  12.1 597.7 %collective-permute-start.1 = (bf16[48,512]{1,0:T(8,128)(2,1)S(1)}, bf16[48,512]{1,0:T(8,128)(2,1)S(1)}, u32[]{:S(2)}, u32[]{:S(2)}) collective-permute-start(bf16[48,512]{1,0:T(8,128)(2,1)S(1)} %get-tuple-element.11), channel_id=1, source_target_pairs={{2,0},{4,2},{6,4},{8,6},{10,8},{12,10},{14,12},{16,14},{18,16},{20... | collective-permute-start | bytes 147464 | tf_op jit(solution)/shard_map/ppermute | solution.py:21
  604.9 3.8 copy-start.18
  609.8 3.4 copy-start.20
  615.8 1.2 copy-start.6
  615.9 549.6 %all-reduce.11.cloned.1.call-start = ((), (), s32[]{:S(2)}) async-start(), calls=%async_computation.2 | async-start | bytes 2097152
  617.3 139.3 %copy-start.15 = (f32[512]{0:T(512)S(1)}, f32[512]{0:T(512)}, u32[]{:S(2)}) copy-start(f32[512]{0:T(512)} %param.26) | copy-start | bytes 6148
  617.3 139.3 %copy-start.22 = (f32[512]{0:T(512)S(1)}, f32[512]{0:T(512)}, u32[]{:S(2)}) copy-start(f32[512]{0:T(512)} %param.27) | copy-start | bytes 6148
  617.3 139.3 %copy-start.23 = (f32[512]{0:T(512)S(1)}, f32[512]{0:T(512)}, u32[]{:S(2)}) copy-start(f32[512]{0:T(512)} %param.29) | copy-start | bytes 6148
  754.4 1.9 copy-start.1
  759.4 1.8 copy-start.9
  759.4 1.8 copy-start.13
  759.4 1.9 copy-start.14
  759.4 2.7 copy-start.19
  759.4 2.7 copy-start.24
  762.1 1.2 copy-start.7
  762.4 0.7 copy-start.11
  763.6 1.3 copy-start.16
  763.6 1.3 copy-start.21
  763.6 1.3 copy-start.25
  764.9 1.4 copy-start.3
  767.8 1.1 copy-start.2
  770.0 447.8 %all-reduce.9.cloned.1.call-start = ((), (), s32[]{:S(2)}) async-start(), calls=%async_computation.1 | async-start | bytes 3801088 | tf_op jit(solution)/shard_map/psum | solution.py:48
  772.0 6.0 collective-permute-start.2
  774.1 392.1 %copy-start.17 = (pred[160]{0:T(512)(128)(4,1)S(1)}, pred[160]{0:T(512)(128)(4,1)}, u32[]{:S(2)}) copy-start(pred[160]{0:T(512)(128)(4,1)} %constant.65.clone.1) | copy-start | bytes 484
  774.1 4.8 collective-permute-start.3
  1169.2 50.8 %copy-start.10 = (bf16[160,512]{1,0:T(8,128)(2,1)S(1)}, bf16[160,512]{1,0:T(8,128)(2,1)}, u32[]{:S(2)}) copy-start(bf16[160,512]{1,0:T(8,128)(2,1)} %param.33) | copy-start | bytes 491524
  1169.2 50.8 %copy-start.12 = (bf16[160,512]{1,0:T(8,128)(2,1)S(1)}, bf16[160,512]{1,0:T(8,128)(2,1)}, u32[]{:S(2)}) copy-start(bf16[160,512]{1,0:T(8,128)(2,1)} %copy-done.11) | copy-start | bytes 491524
  1169.2 48.5 %copy-start.4 = (f32[768,512]{1,0:T(8,128)S(1)}, f32[768,512]{1,0:T(8,128)}, u32[]{:S(2)}) copy-start(f32[768,512]{1,0:T(8,128)} %copy-done.3) | copy-start | bytes 4718596
  1217.8 1.4 slice-start
  1219.2 1.7 copy-start.5
Sparse Core Ops, SparseCore 0:
  616.0 138.3 all-reduce.6
  770.1 395.3 all-reduce.10
  1169.4 48.3 all-reduce.8
where the time goes:
time: 1230 us
  blocking collectives  589 us (48%)
  waiting for transfers between devices  572 us (47%)
  matrix products  24.1 us (2%)
  between operations  14.8 us (1%)
  local copies, waits for them, and re-layouts  12.7 us (1%)
    all_gather x1, blocking collectives, body(): coarse = lax.all_gather(nodes[:HUB_DEV], 'space', axis=0, tiled=True)  579 us
    unnamed x4, waiting for transfers between devices  386 us
    psum x2, waiting for transfers between devices, feat_total(): return lax.psum(partial_sum, 'feat')  186 us
  transfers between devices with their start and end apart: 7, of which 4 were waited for; matrix products, arithmetic and copies ran while one was open for 1% of the time, Pallas kernels for 0%

commit v1 on v0

v1 whole, which is shorter than its diff:
```python
import math

import jax
import jax.numpy as jnp
import numpy as np
from jax import lax
from jax.sharding import Mesh, PartitionSpec as P

RIM = 48
HUB_DEV = 2
EPS = 1e-05
BF = jnp.bfloat16
F32 = jnp.float32
ALL = ("y", "z", "x", "c")
SPACE = ("y", "z", "x")
PLANE = ("y", "x", "c")


def dot(a, b):
    return jnp.dot(a, b, preferred_element_type=F32)


def dot_t(a, b):
    return lax.dot_general(a, b, (((1,), (1,)), ((), ())), preferred_element_type=F32)


def col_sums(onehot, values):
    return lax.dot_general(onehot, values, (((0,), (0,)), ((), ())), preferred_element_type=F32)


def split2(v):
    high = v.astype(BF)
    return high, (v - high.astype(F32)).astype(BF)


def layer_stats(values):
    average = jnp.mean(values, axis=-1, keepdims=True)
    centred = values - average
    inv_scale = lax.rsqrt(jnp.mean(centred * centred, axis=-1, keepdims=True) + EPS)
    return centred * inv_scale, inv_scale


def norm_back(upstream, normed, inv_scale, gain_vec):
    scaled = upstream * gain_vec
    return inv_scale * (
        scaled
        - jnp.mean(scaled, axis=-1, keepdims=True)
        - normed * jnp.mean(scaled * normed, axis=-1, keepdims=True)
    )


def swish_slope(preact):
    sigmoid_val = jax.nn.sigmoid(preact)
    return sigmoid_val * (1.0 + preact * (1.0 - sigmoid_val))


def along_space(x, step):
    count = math.prod(lax.axis_size(a) for a in SPACE)
    return lax.ppermute(x, SPACE, [(i, (i + step) % count) for i in range(count)])


def other_core(x):
    return lax.ppermute(x, "c", [(0, 1), (1, 0)])


def body(
    nodes,
    edges,
    senders,
    receivers,
    edge_proj,
    send_proj,
    recv_proj,
    edge_bias,
    edge_out,
    edge_gain,
    edge_shift,
    node_in,
    node_bias,
    node_out,
    node_gain,
    node_shift,
    node_cot,
):
    node_count, width = nodes.shape
    ny, nz, nx = (lax.axis_size(a) for a in SPACE)
    plane = ny * nx * HUB_DEV
    core = lax.axis_index("c")
    own_block = lax.axis_index(SPACE)
    hub_base = 2 * RIM + node_count
    slots = hub_base + plane * nz

    left_rows = along_space(nodes[node_count - RIM :], 1)
    right_rows = along_space(nodes[:RIM], -1)
    my_hub = lax.dynamic_slice_in_dim(nodes, core, 1, 0).astype(F32)
    by_z = lax.all_to_all(jnp.broadcast_to(my_hub[None], (nz, 1, width)), "z", 0, 0)
    by_z = by_z.reshape(nz, width).astype(BF)
    hubs = lax.all_to_all(jnp.broadcast_to(by_z[None], (plane, nz, width)), PLANE, 0, 0)
    hubs = hubs.reshape(plane * nz, width)

    block = senders // node_count
    row = senders - block * node_count
    hub_y, hub_zx = block // (nz * nx), block % (nz * nx)
    hub_z, hub_x = hub_zx // nx, hub_zx % nx
    hub_slot = ((hub_y * nx + hub_x) * HUB_DEV + row) * nz + hub_z
    slot = jnp.where(
        block == own_block,
        RIM + row,
        jnp.where(
            (block == own_block - 1) & (row >= node_count - RIM),
            row - (node_count - RIM),
            jnp.where(
                (block == own_block + 1) & (row < RIM),
                RIM + node_count + row,
                hub_base + hub_slot,
            ),
        ),
    )
    slot_hot = (slot[:, None] == jnp.arange(slots, dtype=jnp.int32)[None, :]).astype(BF)
    local_recv = receivers - own_block * node_count
    recv_hot = (local_recv[:, None] == jnp.arange(node_count, dtype=jnp.int32)[None, :]).astype(BF)

    table = jnp.concatenate([left_rows, nodes, right_rows, hubs], axis=0)
    send_terms = dot(table, send_proj).astype(BF)
    recv_terms = dot(nodes, recv_proj).astype(BF)
    hidden_pre = (
        dot(edges, edge_proj) + dot(slot_hot, send_terms) + dot(recv_hot, recv_terms) + edge_bias
    )
    hidden_act = jax.nn.silu(hidden_pre).astype(BF)
    edge_normed, edge_scale = layer_stats(dot(hidden_act, edge_out))
    new_edges = (edges.astype(F32) + edge_normed * edge_gain + edge_shift).astype(BF)
    gathered = col_sums(recv_hot, new_edges)
    gathered = (gathered + other_core(gathered)).astype(BF)

    node_pre = dot(nodes, node_in[:width]) + dot(gathered, node_in[width:]) + node_bias
    node_act = jax.nn.silu(node_pre).astype(BF)
    node_normed, node_scale = layer_stats(dot(node_act, node_out))
    new_nodes = (nodes.astype(F32) + node_normed * node_gain + node_shift).astype(BF)
    upstream = node_cot.astype(F32)
    node_dmix = norm_back(upstream, node_normed, node_scale, node_gain).astype(BF)
    node_dpre = (dot_t(node_dmix, node_out) * swish_slope(node_pre)).astype(BF)
    node_direct = upstream + dot_t(node_dpre, node_in[:width])
    gathered_grad = dot_t(node_dpre, node_in[width:])

    grad_high, grad_low = split2(gathered_grad)
    edge_upstream = dot(recv_hot, grad_high) + dot(recv_hot, grad_low)
    edge_dsum = norm_back(edge_upstream, edge_normed, edge_scale, edge_gain).astype(BF)
    edge_dpre = (dot_t(edge_dsum, edge_out) * swish_slope(hidden_pre)).astype(BF)
    slot_sums = col_sums(slot_hot, edge_dpre)
    recv_sums = col_sums(recv_hot, edge_dpre)
    edge_grad = (edge_upstream + dot_t(edge_dpre, edge_proj)).astype(BF)

    back_right = along_space(slot_sums[:RIM].astype(BF), -1)
    back_left = along_space(slot_sums[RIM + node_count : hub_base].astype(BF), 1)
    hub_sums = slot_sums[hub_base:].astype(BF).reshape(plane, nz, width)
    hub_sums = lax.all_to_all(hub_sums, PLANE, 0, 0).astype(F32).sum(0)
    hub_sums = lax.all_to_all(hub_sums.reshape(nz, 1, width), "z", 0, 0).sum(0)
    own_sums = slot_sums[RIM : RIM + node_count]
    own_sums = own_sums + jnp.pad(back_left.astype(F32), ((0, node_count - RIM), (0, 0)))
    own_sums = own_sums + jnp.pad(back_right.astype(F32), ((node_count - RIM, 0), (0, 0)))
    hub_row = (jnp.arange(node_count, dtype=jnp.int32) == core)[:, None]
    own_sums = own_sums + jnp.where(hub_row, hub_sums, 0.0)
    send_high, send_low = split2(own_sums)
    recv_high, recv_low = split2(recv_sums)
    extra = (
        dot_t(send_high, send_proj)
        + dot_t(send_low, send_proj)
        + dot_t(recv_high, recv_proj)
        + dot_t(recv_low, recv_proj)
    )
    extra = extra + other_core(extra)
    node_grad = (node_direct + extra).astype(BF)
    return new_nodes, node_grad, edge_grad


def solution(mesh):
    ny, nz, nx = SHAPE
    fine = Mesh(np.asarray(mesh.devices).reshape(ny, nz, nx, 2), ALL)
    rows, both = P(SPACE, None), P(ALL, None)
    whole = P()
    in_specs = (rows, both, P(ALL), P(ALL)) + (whole,) * 12 + (rows,)
    return jax.shard_map(
        body, mesh=fine, in_specs=in_specs, out_specs=(rows, rows, both), check_vma=False
    )


SHAPE = (4, 16, 4)
```

time: 1230 us -> 118 us (0.10)
  blocking collectives: 589 us -> 0 us
  waiting for transfers between devices: 572 us -> 22.1 us
  starting transfers between devices: 8.73 us -> 63.2 us
  between operations: 14.8 us -> 1.14 us
    all_gather x4 -> x0, blocking collectives: 589 us -> none  [the longest x1 579 us: body(): coarse = lax.all_gather(nodes[:HUB_DEV], 'space', axis=0, tiled=True)]
    unnamed x4 -> x0, waiting for transfers between devices: 386 us -> none
    psum x2 -> x0, waiting for transfers between devices: 186 us -> none  [feat_total(): return lax.psum(partial_sum, 'feat')]
    all_to_all x0 -> x4, starting transfers between devices: none -> 35.8 us  [the longest x1 15.7 us: body(): lax.all_to_all(jnp.broadcast_to(my_hub[None], (nz, 1, width)), 'z', 0, 0)]
    all_to_all x0 -> x4, waiting for transfers between devices: none -> 21.1 us  [the longest x1 10.4 us: body(): hub_sums = lax.all_to_all(hub_sums.reshape(nz, 1, width), 'z', 0, 0).sum(0)]
    ppermute x4 -> x6, starting transfers between devices: 8.61 us -> 27.4 us  [the longest x4 21.7 us: along_space(): lax.ppermute(x, SPACE, [(i, (i + step) % count) for i in range(count)])]
  transfers between devices with their start and end apart: 7 -> 10, of which waited for: 4 -> 5; matrix products, arithmetic and copies ran while one was open for 1% -> 8% of each run, Pallas kernels for 0% -> 0%
where the time goes in v1:
time: 118 us; the launch traced here: 117 us
  starting transfers between devices  63.2 us (54%)
  waiting for transfers between devices  22.1 us (19%)
  matrix products  18.6 us (16%)
  local copies, waits for them, and re-layouts  7.04 us (6%)
  other arithmetic  4.75 us (4%)
    ppermute x4, starting transfers between devices, along_space(): lax.ppermute(x, SPACE, [(i, (i + step) % count) for i in range(count)])  21.7 us
    all_to_all x1, starting transfers between devices, body(): lax.all_to_all(jnp.broadcast_to(my_hub[None], (nz, 1, width)), 'z', 0, 0)  15.7 us
    all_to_all x1, waiting for transfers between devices, body(): hub_sums = lax.all_to_all(hub_sums.reshape(nz, 1, width), 'z', 0, 0).sum(0)  10.4 us
    all_to_all x1, waiting for transfers between devices, body(): lax.all_to_all(jnp.broadcast_to(by_z[None], (plane, nz, width)), PLANE, 0...  9.57 us
    dot_general x9, matrix products, dot(): return jnp.dot(a, b, preferred_element_type=F32)  8.18 us
    all_to_all x1, starting transfers between devices, body(): lax.all_to_all(jnp.broadcast_to(by_z[None], (plane, nz, width)), PLANE, 0...  8 us
    all_to_all x1, starting transfers between devices, body(): hub_sums = lax.all_to_all(hub_sums.reshape(nz, 1, width), 'z', 0, 0).sum(0)  7.46 us
    dot_general x9, matrix products, dot_t(): lax.dot_general(a, b, (((1,), (1,)), ((), ())), preferred_element_type=F32)  6.92 us
  transfers between devices with their start and end apart: 10, of which 5 were waited for; matrix products, arithmetic and copies ran while one was open for 8% of the time, Pallas kernels for 0%

profile of v1, /device:TPU:1, one launch (start us, length us, event | category | flops | bytes accessed | tf_op | source)
XLA Modules:
  0.0 116.8 jit_solution(8739452714017775064)
XLA Ops:
  0.7 0.8 dynamic-slice_convert_fusion
  1.5 0.5 broadcast.135
  2.0 0.7 reduce.1
  2.7 0.6 reshape.84
  3.4 15.7 %all-to-all-start = ((bf16[16,2,256]{2,1,0:T(2,128)(2,1)}), bf16[16,2,256]{2,1,0:T(2,128)(2,1)S(1)}, u32[]{:S(2)}, u32[]{:S(2)}) async-start(bf16[16,2,256]{2,1,0:T(2,128)(2,1)} %reshape.84), calls=%async_computation | async-start | bytes 32768 | tf_op jit(solution)/shard_map/all_to_all | solution.py:96
  19.1 0.8 fusion.93
  19.9 3.1 %collective-permute-start = (bf16[48,512]{1,0:T(8,128)(2,1)S(1)}, bf16[48,512]{1,0:T(8,128)(2,1)}, u32[]{:S(2)}, u32[]{:S(2)}) collective-permute-start(bf16[48,512]{1,0:T(8,128)(2,1)S(1)} %get-tuple-element.10), channel_id=1, source_target_pairs={{0,2},{2,4},{4,6},{6,8},{8,10},{10,12},{12,14},{14,16},{16,18},{18... | collective-permute-start | bytes 147464 | tf_op jit(solution)/shard_map/ppermute | solution.py:59
  23.1 7.9 %collective-permute-start.1 = (bf16[48,512]{1,0:T(8,128)(2,1)S(1)}, bf16[48,512]{1,0:T(8,128)(2,1)}, u32[]{:S(2)}, u32[]{:S(2)}) collective-permute-start(bf16[48,512]{1,0:T(8,128)(2,1)S(1)} %get-tuple-element.11), channel_id=1, source_target_pairs={{0,510},{2,0},{4,2},{6,4},{8,6},{10,8},{12,10},{14,12},{16,14},{18... | collective-permute-start | bytes 147464 | tf_op jit(solution)/shard_map/ppermute | solution.py:59
  31.0 0.7 broadcast_subtract_fusion
  31.7 0.9 broadcast_in_dim.24
  32.6 8.0 %all-to-all-start.1 = ((bf16[32,16,512]{2,1,0:T(8,128)(2,1)}), bf16[32,16,512]{2,1,0:T(8,128)(2,1)}, u32[]{:S(2)}, u32[]{:S(2)}) async-start(bf16[32,16,512]{2,1,0:T(8,128)(2,1)} %broadcast_in_dim.24), calls=%async_computation.1 | async-start | bytes 1048576 | tf_op jit(solution)/shard_map/all_to_all | solution.py:98
  40.7 0.5 fusion.9
  41.2 1.3 %fusion.97 = f32[384,512]{1,0:T(8,128)} fusion(bf16[384,512]{1,0:T(8,128)(2,1)S(1)} %copy-done.10, bf16[512,512]{1,0:T(8,128)(2,1)S(1)} %copy-done.8), kind=kOutput, calls=%fused_computation.149 | convolution fusion | flops 201326592 | bytes 1703936 | tf_op jit(solution)/shard_map/dot_general | solution.py:20
  42.5 9.6 %all-to-all-done.1 = bf16[32,16,512]{2,1,0:T(8,128)(2,1)} async-done(((bf16[32,16,512]{2,1,0:T(8,128)(2,1)}), bf16[32,16,512]{2,1,0:T(8,128)(2,1)}, u32[]{:S(2)}, u32[]{:S(2)}) %all-to-all-start.1) | async-done | bytes 524320 | tf_op jit(solution)/shard_map/all_to_all | solution.py:98
  52.1 3.1 %fusion.3 = f32[384,512]{1,0:T(8,128)} fusion(f32[384,512]{1,0:T(8,128)S(1)} %fusion.9, f32[384,512]{1,0:T(8,128)} %fusion.97, bf16[512,512]{1,0:T(8,128)(2,1)S(1)} %copy-done.6, bf16[512,512]{1,0:T(8,128)(2,1)} %bitcast.2, bf16[48,512]{1,0:T(8,128)(2,1)} %collective-permute-done.1, bf16[160,512]{1,0:T(8,128)(2,1)S(1)} %copy-done.5, ...), kind=kOutput, calls=%fused_computation.7 | convolution fusion | flops 709066752 | bytes 3673600 | tf_op jit(solution)/shard_map/dot_general | solution.py:20
  55.2 1.6 %fusion.94 = (f32[384]{0:T(512)S(1)}, f32[384,512]{1,0:T(8,128)S(1)}) fusion(bf16[512,512]{1,0:T(8,128)(2,1)S(1)} %copy-done, f32[384,512]{1,0:T(8,128)} %fusion.3), kind=kOutput, calls=%fused_computation.146 | convolution fusion | flops 202505856 | bytes 2098688 | tf_op jit(solution)/shard_map/dot_general | solution.py:20
  57.1 0.5 fusion.42
  57.7 2.5 %collective-permute-start.2 = (f32[160,512]{1,0:T(8,128)S(1)}, f32[160,512]{1,0:T(8,128)S(1)}, u32[]{:S(2)}, u32[]{:S(2)}) collective-permute-start(f32[160,512]{1,0:T(8,128)S(1)} %fusion.42), channel_id=1, source_target_pairs={{0,1},{1,0},{2,3},{3,2},{4,5},{5,4},{6,7},{7,6},{8,9},{9,8},{10,11... | collective-permute-start | bytes 983048 | tf_op jit(solution)/shard_map/ppermute | solution.py:63
  60.4 1.0 collective-permute-done.2
  61.7 0.4 fusion.95
  62.3 0.3 copy-done.11
  62.6 0.8 fusion.34
  63.4 0.3 fusion.8
  63.8 0.3 fusion.26
  64.1 0.3 fusion.41
  64.4 0.5 multiply_reduce_fusion.2
  65.0 0.6 copy-done.23
  65.6 0.6 fusion.4
  66.2 1.9 %fusion.96 = (bf16[768,512]{1,0:T(8,128)(2,1)S(1)}, f32[768,512]{1,0:T(8,128)}) fusion(bf16[384,512]{1,0:T(8,128)(2,1)S(1)} %fusion.4, s32[384]{0:T(512)S(1)} %select_select_fusion), kind=kOutput, calls=%fused_computation.148 | convolution fusion | flops 302678016 | bytes 2754048 | tf_op jit(solution)/shard_map/dot_general | solution.py:28
  68.1 0.9 copy-done.4
  68.9 0.8 slice.40
  69.8 4.6 %all-to-all-start.2 = ((bf16[32,16,512]{2,1,0:T(8,128)(2,1)}), bf16[32,16,512]{2,1,0:T(8,128)(2,1)}, u32[]{:S(2)}, u32[]{:S(2)}) async-start(bf16[32,16,512]{2,1,0:T(8,128)(2,1)} %bitcast.26), calls=%async_computation.2 | async-start | bytes 1048576 | tf_op jit(solution)/shard_map/all_to_all | solution.py:156
  74.4 0.8 fusion.92
  75.2 3.3 %collective-permute-start.3 = (bf16[48,512]{1,0:T(8,128)(2,1)S(1)}, bf16[48,512]{1,0:T(8,128)(2,1)S(1)}, u32[]{:S(2)}, u32[]{:S(2)}) collective-permute-start(bf16[48,512]{1,0:T(8,128)(2,1)S(1)} %get-tuple-element.7), channel_id=1, source_target_pairs={{0,2},{2,4},{4,6},{6,8},{8,10},{10,12},{12,14},{14,16},{16,18},{18... | collective-permute-start | bytes 147464 | tf_op jit(solution)/shard_map/ppermute | solution.py:59
  78.5 7.4 %collective-permute-start.4 = (bf16[48,512]{1,0:T(8,128)(2,1)S(1)}, bf16[48,512]{1,0:T(8,128)(2,1)S(1)}, u32[]{:S(2)}, u32[]{:S(2)}) collective-permute-start(bf16[48,512]{1,0:T(8,128)(2,1)S(1)} %get-tuple-element.8), channel_id=1, source_target_pairs={{0,510},{2,0},{4,2},{6,4},{8,6},{10,8},{12,10},{14,12},{16,14},{18... | collective-permute-start | bytes 147464 | tf_op jit(solution)/shard_map/ppermute | solution.py:59
  85.9 1.1 all-to-all-done.2
  87.0 1.1 convert_reduce_fusion
  88.1 0.6 reshape.82
  88.7 7.5 %all-to-all-start.3 = ((f32[16,1,512]{2,1,0:T(1,128)}), f32[16,1,512]{2,1,0:T(1,128)S(1)}, u32[]{:S(2)}, u32[]{:S(2)}) async-start(f32[16,1,512]{2,1,0:T(1,128)} %reshape.82), calls=%async_computation.3 | async-start | bytes 65536 | tf_op jit(solution)/shard_map/all_to_all | solution.py:157
  96.2 1.1 fusion.40
  97.3 10.4 %all-to-all-done.3 = f32[16,1,512]{2,1,0:T(1,128)S(1)} async-done(((f32[16,1,512]{2,1,0:T(1,128)}), f32[16,1,512]{2,1,0:T(1,128)S(1)}, u32[]{:S(2)}, u32[]{:S(2)}) %all-to-all-start.3) | async-done | bytes 32800 | tf_op jit(solution)/shard_map/all_to_all | solution.py:157
  107.8 1.5 %fusion.66 = f32[160,512]{1,0:T(8,128)S(1)} fusion(bf16[512,512]{1,0:T(8,128)(2,1)} %param.22, f32[768,512]{1,0:T(8,128)} %get-tuple-element.18, f32[512]{0:T(512)S(1)} %reduce_sum.99, bf16[48,512]{1,0:T(8,128)(2,1)S(1)} %collective-permute-done.4, bf16[48,512]{1,0:T(8,128)(2,1)S(1)} %collective-permute-done.3, pred[160]{0:T(512)(128)(4,1)S(1)} %iota_compare_fusion.9), kind=kOutput, calls=%fused_computation.92 | convolution fusion | flops 84459520 | bytes 1280160 | tf_op jit(solution)/shard_map/dot_general | solution.py:24
  109.3 1.3 %convolution_add_fusion.4 = f32[160,512]{1,0:T(8,128)S(1)} fusion(f32[160,512]{1,0:T(8,128)S(1)} %fusion.66, bf16[512,512]{1,0:T(8,128)(2,1)S(1)} %copy-done.7, f32[768,512]{1,0:T(8,128)} %get-tuple-element.18, f32[512]{0:T(512)S(1)} %reduce_sum.99, bf16[48,512]{1,0:T(8,128)(2,1)S(1)} %collective-permute-done.4, ...), kind=kOutput, calls=%fused_computation.12 | convolution fusion | flops 84787200 | bytes 1607840 | tf_op jit(solution)/shard_map/dot_general | solution.py:24
  110.7 0.3 convolution_add_fusion.3
  111.0 0.3 convolution_add_fusion.2
  111.4 3.3 %collective-permute-start.5 = (f32[160,512]{1,0:T(8,128)S(1)}, f32[160,512]{1,0:T(8,128)S(1)}, u32[]{:S(2)}, u32[]{:S(2)}) collective-permute-start(f32[160,512]{1,0:T(8,128)S(1)} %convolution_add_fusion.2), channel_id=1, source_target_pairs={{0,1},{1,0},{2,3},{3,2},{4,5},{5,4},{6,7},{7,6},{8,9},{9,8},{10,11... | collective-permute-start | bytes 983048 | tf_op jit(solution)/shard_map/ppermute | solution.py:63
  114.6 1.1 fusion.5
  115.9 1.0 add_convert_fusion.2
  (68 shorter events, 1.4 us)
Async XLA Ops:
  0.6 54.6 %copy-start = (bf16[512,512]{1,0:T(8,128)(2,1)S(1)}, bf16[512,512]{1,0:T(8,128)(2,1)}, u32[]{:S(2)}) copy-start(bf16[512,512]{1,0:T(8,128)(2,1)} %param.25) | copy-start | bytes 1572868
  0.6 40.0 %copy-start.5 = (bf16[160,512]{1,0:T(8,128)(2,1)S(1)}, bf16[160,512]{1,0:T(8,128)(2,1)}, u32[]{:S(2)}) copy-start(bf16[160,512]{1,0:T(8,128)(2,1)} %param.17) | copy-start | bytes 491524
  0.7 40.0 %copy-start.1 = (bf16[512,512]{1,0:T(8,128)(2,1)S(1)}, bf16[512,512]{1,0:T(8,128)(2,1)}, u32[]{:S(2)}) copy-start(bf16[512,512]{1,0:T(8,128)(2,1)} %param.23) | copy-start | bytes 1572868
  3.4 28.3 %all-to-all-start = ((bf16[16,2,256]{2,1,0:T(2,128)(2,1)}), bf16[16,2,256]{2,1,0:T(2,128)(2,1)S(1)}, u32[]{:S(2)}, u32[]{:S(2)}) async-start(bf16[16,2,256]{2,1,0:T(2,128)(2,1)} %reshape.84), calls=%async_computation | async-start | bytes 32768 | tf_op jit(solution)/shard_map/all_to_all | solution.py:96
  19.9 22.6 %collective-permute-start = (bf16[48,512]{1,0:T(8,128)(2,1)S(1)}, bf16[48,512]{1,0:T(8,128)(2,1)}, u32[]{:S(2)}, u32[]{:S(2)}) collective-permute-start(bf16[48,512]{1,0:T(8,128)(2,1)S(1)} %get-tuple-element.10), channel_id=1, source_target_pairs={{0,2},{2,4},{4,6},{6,8},{8,10},{10,12},{12,14},{14,16},{16,18},{18... | collective-permute-start | bytes 147464 | tf_op jit(solution)/shard_map/ppermute | solution.py:59
  23.1 19.5 %collective-permute-start.1 = (bf16[48,512]{1,0:T(8,128)(2,1)S(1)}, bf16[48,512]{1,0:T(8,128)(2,1)}, u32[]{:S(2)}, u32[]{:S(2)}) collective-permute-start(bf16[48,512]{1,0:T(8,128)(2,1)S(1)} %get-tuple-element.11), channel_id=1, source_target_pairs={{0,510},{2,0},{4,2},{6,4},{8,6},{10,8},{12,10},{14,12},{16,14},{18... | collective-permute-start | bytes 147464 | tf_op jit(solution)/shard_map/ppermute | solution.py:59
  31.7 9.5 %copy-start.8 = (bf16[512,512]{1,0:T(8,128)(2,1)S(1)}, bf16[512,512]{1,0:T(8,128)(2,1)}, u32[]{:S(2)}) copy-start(bf16[512,512]{1,0:T(8,128)(2,1)} %param.21) | copy-start | bytes 1572868
  31.7 9.5 %copy-start.10 = (bf16[384,512]{1,0:T(8,128)(2,1)S(1)}, bf16[384,512]{1,0:T(8,128)(2,1)}, u32[]{:S(2)}) copy-start(bf16[384,512]{1,0:T(8,128)(2,1)} %param.18) | copy-start | bytes 1179652
  32.6 19.5 %all-to-all-start.1 = ((bf16[32,16,512]{2,1,0:T(8,128)(2,1)}), bf16[32,16,512]{2,1,0:T(8,128)(2,1)}, u32[]{:S(2)}, u32[]{:S(2)}) async-start(bf16[32,16,512]{2,1,0:T(8,128)(2,1)} %broadcast_in_dim.24), calls=%async_computation.1 | async-start | bytes 1048576 | tf_op jit(solution)/shard_map/all_to_all | solution.py:98
  40.6 1.8 %copy-start.19 = (s32[384]{0:T(512)S(1)}, s32[384]{0:T(512)}, u32[]{:S(2)}) copy-start(s32[384]{0:T(512)} %param.19) | copy-start | bytes 4612
  40.6 11.5 %copy-start.6 = (bf16[512,512]{1,0:T(8,128)(2,1)S(1)}, bf16[512,512]{1,0:T(8,128)(2,1)}, u32[]{:S(2)}) copy-start(bf16[512,512]{1,0:T(8,128)(2,1)} %param.22) | copy-start | bytes 1572868
  40.7 11.4 %copy-start.22 = (f32[512]{0:T(512)S(1)}, f32[512]{0:T(512)}, u32[]{:S(2)}) copy-start(f32[512]{0:T(512)} %param.24) | copy-start | bytes 6148
  55.2 1.9 %copy-start.15 = (f32[512]{0:T(512)S(1)}, f32[512]{0:T(512)}, u32[]{:S(2)}) copy-start(f32[512]{0:T(512)} %param.26) | copy-start | bytes 6148
  55.2 1.9 %copy-start.16 = (f32[512]{0:T(512)S(1)}, f32[512]{0:T(512)}, u32[]{:S(2)}) copy-start(f32[512]{0:T(512)} %param.27) | copy-start | bytes 6148
  56.8 3.3 %copy-start.2 = (bf16[1024,512]{1,0:T(8,128)(2,1)S(1)}, bf16[1024,512]{1,0:T(8,128)(2,1)}, u32[]{:S(2)}) copy-start(bf16[1024,512]{1,0:T(8,128)(2,1)} %param.28) | copy-start | bytes 3145732
  56.8 4.5 %copy-start.20 = (f32[512]{0:T(512)S(1)}, f32[512]{0:T(512)}, u32[]{:S(2)}) copy-start(f32[512]{0:T(512)} %param.29) | copy-start | bytes 6148
  57.7 4.0 %copy-start.21 = (bf16[512,512]{1,0:T(8,128)(2,1)S(1)}, bf16[512,512]{1,0:T(8,128)(2,1)}, u32[]{:S(2)}) copy-start(bf16[512,512]{1,0:T(8,128)(2,1)} %param.30) | copy-start | bytes 1572868
  57.7 3.7 %collective-permute-start.2 = (f32[160,512]{1,0:T(8,128)S(1)}, f32[160,512]{1,0:T(8,128)S(1)}, u32[]{:S(2)}, u32[]{:S(2)}) collective-permute-start(f32[160,512]{1,0:T(8,128)S(1)} %fusion.42), channel_id=1, source_target_pairs={{0,1},{1,0},{2,3},{3,2},{4,5},{5,4},{6,7},{7,6},{8,9},{9,8},{10,11... | collective-permute-start | bytes 983048 | tf_op jit(solution)/shard_map/ppermute | solution.py:63
  61.7 0.9 copy-start.11
  61.7 0.9 copy-start.17
  61.7 0.9 copy-start.18
  63.8 1.2 copy-start.13
  64.4 1.1 copy-start.23
  68.1 0.9 copy-start.4
  69.8 17.2 %all-to-all-start.2 = ((bf16[32,16,512]{2,1,0:T(8,128)(2,1)}), bf16[32,16,512]{2,1,0:T(8,128)(2,1)}, u32[]{:S(2)}, u32[]{:S(2)}) async-start(bf16[32,16,512]{2,1,0:T(8,128)(2,1)} %bitcast.26), calls=%async_computation.2 | async-start | bytes 1048576 | tf_op jit(solution)/shard_map/all_to_all | solution.py:156
  75.2 32.6 %collective-permute-start.3 = (bf16[48,512]{1,0:T(8,128)(2,1)S(1)}, bf16[48,512]{1,0:T(8,128)(2,1)S(1)}, u32[]{:S(2)}, u32[]{:S(2)}) collective-permute-start(bf16[48,512]{1,0:T(8,128)(2,1)S(1)} %get-tuple-element.7), channel_id=1, source_target_pairs={{0,2},{2,4},{4,6},{6,8},{8,10},{10,12},{12,14},{14,16},{16,18},{18... | collective-permute-start | bytes 147464 | tf_op jit(solution)/shard_map/ppermute | solution.py:59
  78.5 29.3 %collective-permute-start.4 = (bf16[48,512]{1,0:T(8,128)(2,1)S(1)}, bf16[48,512]{1,0:T(8,128)(2,1)S(1)}, u32[]{:S(2)}, u32[]{:S(2)}) collective-permute-start(bf16[48,512]{1,0:T(8,128)(2,1)S(1)} %get-tuple-element.8), channel_id=1, source_target_pairs={{0,510},{2,0},{4,2},{6,4},{8,6},{10,8},{12,10},{14,12},{16,14},{18... | collective-permute-start | bytes 147464 | tf_op jit(solution)/shard_map/ppermute | solution.py:59
  88.7 19.0 %all-to-all-start.3 = ((f32[16,1,512]{2,1,0:T(1,128)}), f32[16,1,512]{2,1,0:T(1,128)S(1)}, u32[]{:S(2)}, u32[]{:S(2)}) async-start(f32[16,1,512]{2,1,0:T(1,128)} %reshape.82), calls=%async_computation.3 | async-start | bytes 65536 | tf_op jit(solution)/shard_map/all_to_all | solution.py:157
  107.8 1.6 %copy-start.7 = (bf16[512,512]{1,0:T(8,128)(2,1)S(1)}, bf16[512,512]{1,0:T(8,128)(2,1)}, u32[]{:S(2)}) copy-start(bf16[512,512]{1,0:T(8,128)(2,1)} %param.22) | copy-start | bytes 1572868
  107.8 2.9 %copy-start.3 = (f32[160,512]{1,0:T(8,128)S(1)}, f32[160,512]{1,0:T(8,128)}, u32[]{:S(2)}) copy-start(f32[160,512]{1,0:T(8,128)} %fusion.40) | copy-start | bytes 983044
  110.7 4.0 %copy-start.9 = (bf16[512,512]{1,0:T(8,128)(2,1)S(1)}, bf16[512,512]{1,0:T(8,128)(2,1)}, u32[]{:S(2)}) copy-start(bf16[512,512]{1,0:T(8,128)(2,1)} %param.21) | copy-start | bytes 1572868
  111.0 4.8 %copy-start.12 = (bf16[160,512]{1,0:T(8,128)(2,1)S(1)}, bf16[160,512]{1,0:T(8,128)(2,1)}, u32[]{:S(2)}) copy-start(bf16[160,512]{1,0:T(8,128)(2,1)} %param.33) | copy-start | bytes 491524
  111.0 4.8 %copy-start.14 = (bf16[160,512]{1,0:T(8,128)(2,1)S(1)}, bf16[160,512]{1,0:T(8,128)(2,1)}, u32[]{:S(2)}) copy-start(bf16[160,512]{1,0:T(8,128)(2,1)} %copy-done.13) | copy-start | bytes 491524
  111.4 4.5 %collective-permute-start.5 = (f32[160,512]{1,0:T(8,128)S(1)}, f32[160,512]{1,0:T(8,128)S(1)}, u32[]{:S(2)}, u32[]{:S(2)}) collective-permute-start(f32[160,512]{1,0:T(8,128)S(1)} %convolution_add_fusion.2), channel_id=1, source_target_pairs={{0,1},{1,0},{2,3},{3,2},{4,5},{5,4},{6,7},{7,6},{8,9},{9,8},{10,11... | collective-permute-start | bytes 983048 | tf_op jit(solution)/shard_map/ppermute | solution.py:63

commit v2 on v1

v2 whole, which is shorter than its diff:
```python
import functools
import math

import jax
import jax.numpy as jnp
import numpy as np
from jax import lax
from jax.experimental import pallas as pl
from jax.experimental.pallas import tpu as pltpu
from jax.sharding import Mesh, PartitionSpec as P

RIM = 48
HUB_DEV = 2
EPS = 1e-05
BF = jnp.bfloat16
F32 = jnp.float32
I32 = jnp.int32
ALL = ("y", "z", "x", "c")
SPACE = ("y", "z", "x")
PLANE = ("y", "x")
LANES = 128
TILE = 256
SHAPE = (4, 16, 4)


def dot(a, b):
    return jnp.dot(a, b, preferred_element_type=F32)


def dot_t(a, b):
    return lax.dot_general(a, b, (((1,), (1,)), ((), ())), preferred_element_type=F32)


def split2(v):
    high = v.astype(BF)
    return high, (v - high.astype(F32)).astype(BF)


def row_mean(v):
    return jnp.mean(v, axis=-1, keepdims=True)


def layer_stats(values):
    centred = values - row_mean(values)
    inv_scale = lax.rsqrt(row_mean(centred * centred) + EPS)
    return centred * inv_scale, inv_scale


def norm_back(upstream, normed, inv_scale, gain_vec):
    scaled = upstream * gain_vec
    return inv_scale * (scaled - row_mean(scaled) - normed * row_mean(scaled * normed))


def hot_rows(ids, first, count):
    edges = ids.shape[1]
    column = jnp.broadcast_to(ids - first, (LANES, edges)).T
    lane = lax.broadcasted_iota(I32, (edges, LANES), 1)
    parts = [
        jnp.where(column == lane + k, 1.0, 0.0).astype(BF) for k in range(0, count, LANES)
    ]
    return jnp.concatenate(parts, axis=1)[:, :count]


def hot_cols(ids, first, count):
    edges = ids.shape[1]
    slot = lax.broadcasted_iota(I32, (count, edges), 0)
    return jnp.where(slot == ids - first, 1.0, 0.0).astype(BF)


def vmem_call(kernel, outs, args, scratch=(), smem=0, flops=0, name=None):
    spec = pl.BlockSpec(memory_space=pltpu.VMEM)
    ins = [pl.BlockSpec(memory_space=pltpu.SMEM)] * smem + [spec] * (len(args) - smem)
    moved = sum(math.prod(o.shape) * o.dtype.itemsize for o in outs)
    moved += sum(math.prod(a.shape) * a.dtype.itemsize for a in args)
    return pl.pallas_call(
        kernel,
        out_shape=outs,
        in_specs=ins,
        out_specs=[spec] * len(outs),
        scratch_shapes=list(scratch),
        compiler_params=pltpu.CompilerParams(vmem_limit_bytes=40 * 2**20),
        cost_estimate=pl.CostEstimate(flops=flops, bytes_accessed=moved, transcendentals=0),
        name=name,
    )(*args)


def spread_kernel(rows_ref, out_ref):
    nz = rows_ref.shape[0] // 8
    parts = []
    for r in range(HUB_DEV):
        lanes = [rows_ref[pl.ds(4 * r + j, nz, stride=8), :] for j in range(4)]
        parts.append(jnp.concatenate(lanes, axis=1))
    rows = jnp.concatenate(parts, axis=0).astype(BF)
    for p in range(out_ref.shape[0]):
        out_ref[p] = rows


def gather_kernel(sums_ref, out_ref):
    nz = out_ref.shape[0] // 8
    total = sums_ref[0].astype(F32)
    for p in range(1, sums_ref.shape[0]):
        total += sums_ref[p].astype(F32)
    for r in range(HUB_DEV):
        for j in range(4):
            out_ref[pl.ds(4 * r + j, nz, stride=8), :] = total[
                r * nz : (r + 1) * nz, j * LANES : (j + 1) * LANES
            ]


def near_kernel(
    edges_ref, ids_ref, nodes_ref, left_ref, right_ref, we_ref, ws_ref, wr_ref, bias_ref,
    pre_ref, frame_ref, send_ref, recv_ref,
):
    node_count = nodes_ref.shape[0]
    slots = 2 * RIM + node_count
    frame_ref[:RIM] = left_ref[...]
    frame_ref[RIM : RIM + node_count] = nodes_ref[...]
    frame_ref[RIM + node_count :] = right_ref[...]
    send_ref[...] = dot(frame_ref[...], ws_ref[...]).astype(BF)
    recv_ref[...] = dot(frame_ref[...], wr_ref[...]).astype(BF)

    def step(i, carry):
        rows = pl.ds(pl.multiple_of(i * TILE, TILE), TILE)
        pre = dot(edges_ref[rows, :], we_ref[...])
        pre += dot(hot_rows(ids_ref[0:1, rows], 0, slots), send_ref[...])
        pre += dot(hot_rows(ids_ref[1:2, rows], 0, slots), recv_ref[...])
        pre_ref[rows, :] = pre + bias_ref[...]
        return carry

    lax.fori_loop(0, edges_ref.shape[0] // TILE, step, 0)


def main_kernel(
    hubs_ref, pre_ref, edges_ref, ids_ref, nodes_ref, cot_ref, ws_ref, wo_ref, win_ref, wout_ref,
    egain_ref, eshift_ref, nbias_ref, ngain_ref, nshift_ref,
    new_ref, dpre_ref, hub_sums_ref, rim_l_ref, rim_r_ref, own_ref, gg_ref, ndpre_ref,
    terms_ref, slope_ref, normed_ref, scale_ref, gathered_ref, high_ref, low_ref,
):
    node_count, width = nodes_ref.shape
    hub_count = hubs_ref.shape[0]
    edge_count = edges_ref.shape[0]
    slots = 2 * RIM + node_count
    own = slice(RIM, RIM + node_count)
    terms_ref[...] = dot(hubs_ref[...], ws_ref[...]).astype(BF)
    gathered_ref[...] = jnp.zeros_like(gathered_ref)

    def forward(i, carry):
        rows = pl.ds(pl.multiple_of(i * TILE, TILE), TILE)
        pre = pre_ref[rows, :] + dot(hot_rows(ids_ref[0:1, rows], slots, hub_count), terms_ref[...])
        gate = jax.nn.sigmoid(pre)
        slope_ref[rows, :] = gate * (1.0 + pre * (1.0 - gate))
        edge_sum = dot((pre * gate).astype(BF), wo_ref[...])
        normed, scale = layer_stats(edge_sum)
        normed_ref[rows, :] = normed
        scale_ref[rows, :] = jnp.broadcast_to(scale, (TILE, LANES))
        new_edges = edges_ref[rows, :].astype(F32) + normed * egain_ref[...] + eshift_ref[...]
        gathered_ref[...] += dot(hot_cols(ids_ref[1:2, rows], 0, slots), new_edges.astype(BF))
        return carry

    lax.fori_loop(0, edge_count // TILE, forward, 0)

    nodes = nodes_ref[...]
    gathered = gathered_ref[own].astype(BF)
    node_pre = dot(nodes, win_ref[:width]) + dot(gathered, win_ref[width:]) + nbias_ref[...]
    gate = jax.nn.sigmoid(node_pre)
    node_mix = dot((node_pre * gate).astype(BF), wout_ref[...])
    normed, scale = layer_stats(node_mix)
    new_nodes = nodes.astype(F32) + normed * ngain_ref[...] + nshift_ref[...]
    new_ref[...] = new_nodes.astype(BF)
    dmix = norm_back(cot_ref[...].astype(F32), normed, scale, ngain_ref[...]).astype(BF)
    ndpre = dot_t(dmix, wout_ref[...]) * (gate * (1.0 + node_pre * (1.0 - gate)))
    ndpre = ndpre.astype(BF)
    ndpre_ref[...] = ndpre
    gathered_grad = dot_t(ndpre, win_ref[width:])
    gg_ref[...] = gathered_grad
    high, low = split2(gathered_grad)
    for ref, part in ((high_ref, high), (low_ref, low)):
        ref[...] = jnp.zeros_like(ref)
        ref[own] = part

    def backward(i, carry):
        rows = pl.ds(pl.multiple_of(i * TILE, TILE), TILE)
        hot = hot_rows(ids_ref[1:2, rows], 0, slots)
        upstream = dot(hot, high_ref[...]) + dot(hot, low_ref[...])
        dsum = norm_back(upstream, normed_ref[rows, :], scale_ref[rows, :1], egain_ref[...])
        dpre_ref[rows, :] = (dot_t(dsum.astype(BF), wo_ref[...]) * slope_ref[rows, :]).astype(BF)
        return carry

    lax.fori_loop(0, edge_count // TILE, backward, 0)

    dpre = dpre_ref[...]
    hub_sums_ref[...] = dot(hot_cols(ids_ref[0:1, :], slots, hub_count), dpre).astype(BF)
    frame = dot(hot_cols(ids_ref[0:1, :], 0, slots), dpre)
    rim_l_ref[...] = frame[:RIM].astype(BF)
    rim_r_ref[...] = frame[RIM + node_count :].astype(BF)
    own_ref[...] = frame[own]


def late_kernel(
    core_ref, dpre_ref, ids_ref, gg_ref, ndpre_ref, own_ref, cot_ref, we_ref, ws_ref, wr_ref, win_ref,
    egrad_ref, base_ref, high_ref, low_ref,
):
    node_count, width = cot_ref.shape
    slots = 2 * RIM + node_count
    own = slice(RIM, RIM + node_count)
    half = egrad_ref.shape[0]
    high, low = split2(gg_ref[...])
    for ref, part in ((high_ref, high), (low_ref, low)):
        ref[...] = jnp.zeros_like(ref)
        ref[own] = part
    rows = pl.ds(pl.multiple_of(core_ref[0] * half, half), half)
    hot = hot_rows(ids_ref[1:2, rows], 0, slots)
    upstream = dot(hot, high_ref[...]) + dot(hot, low_ref[...])
    egrad_ref[...] = (upstream + dot_t(dpre_ref[rows, :], we_ref[...])).astype(BF)
    base = cot_ref[...].astype(F32) + dot_t(ndpre_ref[...], win_ref[:width])
    recv = dot(hot_cols(ids_ref[1:2, :], RIM, node_count), dpre_ref[...])
    for sums, weight in ((own_ref[...], ws_ref), (recv, wr_ref)):
        high, low = split2(sums)
        base += dot_t(high, weight[...]) + dot_t(low, weight[...])
    base_ref[...] = base


def last_kernel(hub_ref, first_ref, final_ref, base_ref, ws_ref, out_ref, sums_ref):
    node_count = base_ref.shape[0]
    hub = hub_ref[0]
    for z in range(1, hub_ref.shape[0]):
        hub += hub_ref[z]
    rows = [
        jnp.concatenate([hub[4 * r + j : 4 * r + j + 1] for j in range(4)], axis=1)
        for r in range(HUB_DEV)
    ]
    sums_ref[...] = jnp.zeros_like(sums_ref)
    sums_ref[:RIM] = first_ref[...].astype(F32)
    for r in range(HUB_DEV):
        sums_ref[r : r + 1] += rows[r]
    sums_ref[node_count - RIM :] += final_ref[...].astype(F32)
    high, low = split2(sums_ref[...])
    extra = dot_t(high, ws_ref[...]) + dot_t(low, ws_ref[...])
    out_ref[...] = (base_ref[...] + extra).astype(BF)


def along_space(x, step):
    count = math.prod(lax.axis_size(a) for a in SPACE)
    pairs = [(i, i + step) for i in range(count) if 0 <= i + step < count]
    return lax.ppermute(x, SPACE, pairs)


def body(
    nodes,
    edges,
    senders,
    receivers,
    edge_proj,
    send_proj,
    recv_proj,
    edge_bias,
    edge_out,
    edge_gain,
    edge_shift,
    node_in,
    node_bias,
    node_out,
    node_gain,
    node_shift,
    node_cot,
):
    shape = jax.ShapeDtypeStruct
    node_count, width = nodes.shape
    ny, nz, nx = (lax.axis_size(a) for a in SPACE)
    plane = ny * nx
    hub_count = plane * HUB_DEV * nz
    slots = 2 * RIM + node_count
    core = lax.axis_index("c")
    own_block = lax.axis_index(SPACE)
    row = lambda v: v.reshape(1, width)

    my_hub = nodes[:HUB_DEV].astype(F32).reshape(1, 8, LANES)
    by_z = lax.all_to_all(jnp.broadcast_to(my_hub, (nz, 8, LANES)), "z", 0, 0)
    left_rows = along_space(nodes[node_count - RIM :], 1)
    right_rows = along_space(nodes[:RIM], -1)
    (spread,) = vmem_call(
        spread_kernel,
        [shape((plane, HUB_DEV * nz, width), BF)],
        [by_z.reshape(nz * 8, LANES)],
        name="spread",
    )
    hubs = lax.all_to_all(spread, PLANE, 0, 0).reshape(hub_count, width)

    all_edges = lax.all_gather(edges, "c", axis=0, tiled=True)
    ids = lax.all_gather(jnp.stack([senders, receivers]), "c", axis=1, tiled=True)
    edge_count = all_edges.shape[0]
    block = ids[0] // node_count
    line = ids[0] - block * node_count
    hub_y, hub_zx = block // (nz * nx), block % (nz * nx)
    hub_z, hub_x = hub_zx // nx, hub_zx % nx
    hub_slot = ((hub_y * nx + hub_x) * HUB_DEV + line) * nz + hub_z
    slot = jnp.where(
        block == own_block,
        RIM + line,
        jnp.where(
            (block == own_block - 1) & (line >= node_count - RIM),
            line - (node_count - RIM),
            jnp.where(
                (block == own_block + 1) & (line < RIM),
                RIM + node_count + line,
                slots + hub_slot,
            ),
        ),
    )
    ids = jnp.stack([slot, ids[1] - own_block * node_count + RIM])

    square = 2 * width * width
    (near,) = vmem_call(
        near_kernel,
        [shape((edge_count, width), F32)],
        [all_edges, ids, nodes, left_rows, right_rows, edge_proj, send_proj, recv_proj, row(edge_bias)],
        [pltpu.VMEM((slots, width), BF)] * 3,
        flops=square * (edge_count * 2 + 2 * slots),
        name="near",
    )
    new_nodes, dpre, hub_sums, rim_l, rim_r, own_sums, gathered_grad, node_dpre = vmem_call(
        main_kernel,
        [
            shape((node_count, width), BF),
            shape((edge_count, width), BF),
            shape((hub_count, width), BF),
            shape((RIM, width), BF),
            shape((RIM, width), BF),
            shape((node_count, width), F32),
            shape((node_count, width), F32),
            shape((node_count, width), BF),
        ],
        [
            hubs, near, all_edges, ids, nodes, node_cot, send_proj, edge_out, node_in, node_out,
            row(edge_gain), row(edge_shift), row(node_bias), row(node_gain), row(node_shift),
        ],
        [
            pltpu.VMEM((hub_count, width), BF),
            pltpu.VMEM((edge_count, width), F32),
            pltpu.VMEM((edge_count, width), F32),
            pltpu.VMEM((edge_count, LANES), F32),
            pltpu.VMEM((slots, width), F32),
            pltpu.VMEM((slots, width), BF),
            pltpu.VMEM((slots, width), BF),
        ],
        flops=square * (edge_count * 6 + hub_count),
        name="main",
    )

    hub_back = lax.all_to_all(hub_sums.reshape(plane, HUB_DEV * nz, width), PLANE, 0, 0)
    final_back = along_space(rim_l, -1)
    first_back = along_space(rim_r, 1)
    (by_z,) = vmem_call(
        gather_kernel, [shape((nz * 8, LANES), F32)], [hub_back], name="gather"
    )
    hub_back = lax.all_to_all(by_z.reshape(nz, 8, LANES), "z", 0, 0)
    edge_grad, base = vmem_call(
        late_kernel,
        [shape(edges.shape, BF), shape((node_count, width), F32)],
        [
            core.astype(I32).reshape(1), dpre, ids, gathered_grad, node_dpre, own_sums, node_cot,
            edge_proj, send_proj, recv_proj, node_in,
        ],
        [pltpu.VMEM((slots, width), BF)] * 2,
        smem=1,
        flops=square * edge_count * 2,
        name="late",
    )
    (node_grad,) = vmem_call(
        last_kernel,
        [shape((node_count, width), BF)],
        [hub_back, first_back, final_back, base, send_proj],
        [pltpu.VMEM((node_count, width), F32)],
        flops=square * node_count * 2,
        name="last",
    )
    return new_nodes, node_grad, edge_grad


def solution(mesh):
    fine = Mesh(np.asarray(mesh.devices).reshape(*SHAPE, 2), ALL)
    rows, both = P(SPACE, None), P(ALL, None)
    whole = P()
    in_specs = (rows, both, P(ALL), P(ALL)) + (whole,) * 12 + (rows,)
    return jax.shard_map(
        body, mesh=fine, in_specs=in_specs, out_specs=(rows, rows, both), check_vma=False
    )
```

time: 118 us -> 111 us (0.941)
  the two profiles are of different devices: /device:TPU:1 before, /device:TPU:8 now
where the time goes in v2:
time: 111 us; the launch traced here: 110 us
  starting transfers between devices  52.5 us (47%)
  blocking collectives  18.6 us (17%)
  local copies, waits for them, and re-layouts  18.2 us (16%)
  Pallas kernels  15.9 us (14%)
  waiting for transfers between devices  3.25 us (3%)
    ppermute x4, starting transfers between devices, along_space(): return lax.ppermute(x, SPACE, pairs)  19.1 us
    pallas_call x6, Pallas kernels, vmem_call(): pl.pallas_call(kernel, out_shape=outs, in_specs=ins, out_specs=[spec] * l...  15.9 us
    unnamed x64, local copies, waits for them, and re-layouts  15.2 us
    all_to_all x1, starting transfers between devices, body(): by_z = lax.all_to_all(jnp.broadcast_to(my_hub, (nz, 8, LANES)), 'z', 0, 0)  15.2 us
    all_to_all x1, blocking collectives, body(): lax.all_to_all(hub_sums.reshape(plane, HUB_DEV * nz, width), PLANE, 0, 0)  14.2 us
    all_to_all x1, starting transfers between devices, body(): hub_back = lax.all_to_all(by_z.reshape(nz, 8, LANES), 'z', 0, 0)  12.1 us
    all_to_all x1, starting transfers between devices, body(): hubs = lax.all_to_all(spread, PLANE, 0, 0).reshape(hub_count, width)  6.13 us
    all_to_all x1, waiting for transfers between devices, body(): hubs = lax.all_to_all(spread, PLANE, 0, 0).reshape(hub_count, width)  3.24 us
  transfers between devices with their start and end apart: 7, of which 1 were waited for; matrix products, arithmetic and copies ran while one was open for 2% of the time, Pallas kernels for 4%

profile of v2, /device:TPU:8, one launch (start us, length us, event | category | flops | bytes accessed | tf_op | source)
XLA Modules:
  0.0 110.2 jit_solution(11641099625905639837)
XLA Ops:
  0.6 0.7 slice_convert_fusion
  1.3 0.6 broadcast_in_dim.12
  2.0 15.2 %all-to-all-start = ((f32[16,8,128]{2,1,0:T(8,128)}), f32[16,8,128]{2,1,0:T(8,128)S(1)}, u32[]{:S(2)}, u32[]{:S(2)}) async-start(f32[16,8,128]{2,1,0:T(8,128)} %broadcast_in_dim.12), calls=%async_computation | async-start | bytes 131072 | tf_op jit(solution)/shard_map/all_to_all | solution.py:278
  17.2 0.0 copy-start
  17.2 0.0 copy-start.1
  17.2 0.0 copy-start.2
  17.2 0.0 copy-start.22
  17.2 0.9 fusion.2
  18.2 7.1 %collective-permute-start.1 = (bf16[48,512]{1,0:T(8,128)(2,1)S(1)}, bf16[48,512]{1,0:T(8,128)(2,1)S(1)}, u32[]{:S(2)}, u32[]{:S(2)}) collective-permute-start(bf16[48,512]{1,0:T(8,128)(2,1)S(1)} %get-tuple-element.23), channel_id=1, source_target_pairs={{2,0},{4,2},{6,4},{8,6},{10,8},{12,10},{14,12},{16,14},{18,16},{20... | collective-permute-start | bytes 147464 | tf_op jit(solution)/shard_map/ppermute | solution.py:245
  25.3 1.9 %collective-permute-start = (bf16[48,512]{1,0:T(8,128)(2,1)S(1)}, bf16[48,512]{1,0:T(8,128)(2,1)S(1)}, u32[]{:S(2)}, u32[]{:S(2)}) collective-permute-start(bf16[48,512]{1,0:T(8,128)(2,1)S(1)} %get-tuple-element.24), channel_id=1, source_target_pairs={{0,2},{2,4},{4,6},{6,8},{8,10},{10,12},{12,14},{14,16},{16,18},{18... | collective-permute-start | bytes 147464 | tf_op jit(solution)/shard_map/ppermute | solution.py:245
  27.2 0.7 stack.14
  27.9 0.7 stack.15
  28.6 2.6 %all_gather.6.edges_ref = bf16[768,512]{1,0:T(8,128)(2,1)S(1)} all-gather(bf16[384,512]{1,0:T(8,128)(2,1)} %param.18), channel_id=1, replica_groups=mesh['y'=4,'z'=16,'x'=4,'c'=2] {'c'}, dimensions={0}, use_global_device_ids=true | all-gather | bytes 1179648 | tf_op jit(solution)/shard_map/all_gather | solution.py:289
  31.2 0.0 all-to-all-done
  31.2 0.9 spread.1
  32.0 6.1 %all-to-all-start.1 = ((bf16[16,32,512]{2,1,0:T(8,128)(2,1)}), bf16[16,32,512]{2,1,0:T(8,128)(2,1)}, u32[]{:S(2)}, u32[]{:S(2)}) async-start(bf16[16,32,512]{2,1,0:T(8,128)(2,1)} %spread.1), calls=%async_computation.1 | async-start | bytes 1048576 | tf_op jit(solution)/shard_map/all_to_all | solution.py:287
  38.2 1.8 %all_gather.7 = s32[2,768]{1,0:T(2,128)S(1)} all-gather(s32[2,384]{1,0:T(2,128)S(1)} %pad_add_fusion.1), channel_id=1, replica_groups=mesh['y'=4,'z'=16,'x'=4,'c'=2] {'c'}, dimensions={1}, use_global_device_ids=true | all-gather | bytes 9216 | tf_op jit(solution)/shard_map/all_gather | solution.py:290
  40.0 0.1 compare_select_fusion
  40.1 0.0 collective-permute-done.1.right_ref
  40.2 0.0 copy-start.8
  40.2 0.9 copy-done.8
  41.1 0.0 copy-start.30
  41.1 0.0 copy-start.31
  41.1 1.9 %near.1.pre_ref = f32[768,512]{1,0:T(8,128)S(1)} custom-call(bf16[768,512]{1,0:T(8,128)(2,1)S(1)} %all_gather.6.edges_ref, s32[2,768]{1,0:T(2,128)S(1)} %pad_add_fusion.ids_ref, bf16[160,512]{1,0:T(8,128)(2,1)S(1)} %copy-done.8, bf16[48,512]{1,0:T(8,128)(2,1)S(1)} %collective-permute-done.left_ref, bf16[48,512]{1,0:T(8,128)(2,1)S(1)} %collective-permute-done.1.right_ref, ...), custom_call_target="tpu_custom_call" | custom-call | flops 1073741824 | bytes 4202496 | tf_op jit(solution)/shard_map/near/pallas_call | solution.py:75
  43.0 1.2 %copy-done.3 = f32[768,512]{1,0:T(8,128)} copy-done((f32[768,512]{1,0:T(8,128)}, f32[768,512]{1,0:T(8,128)S(1)}, u32[]{:S(2)}) %copy-start.3) | copy-done | bytes 1572888
  44.2 3.2 %all-to-all-done.1 = bf16[16,32,512]{2,1,0:T(8,128)(2,1)} async-done(((bf16[16,32,512]{2,1,0:T(8,128)(2,1)}), bf16[16,32,512]{2,1,0:T(8,128)(2,1)}, u32[]{:S(2)}, u32[]{:S(2)}) %all-to-all-start.1) | async-done | bytes 524320 | tf_op jit(solution)/shard_map/all_to_all | solution.py:287
  47.5 1.4 %copy-done.4 = f32[768,512]{1,0:T(8,128)S(1)} copy-done((f32[768,512]{1,0:T(8,128)S(1)}, f32[768,512]{1,0:T(8,128)}, u32[]{:S(2)}) %copy-start.4) | copy-done | bytes 1572888
  48.9 0.9 copy-done.9
  49.8 0.9 copy-done.16
  50.7 1.0 copy-done.23
  51.7 1.0 copy-done.24
  52.8 9.4 %main.1 = (bf16[160,512]{1,0:T(8,128)(2,1)}, bf16[768,512]{1,0:T(8,128)(2,1)S(1)}, bf16[512,512]{1,0:T(8,128)(2,1)S(1)}, bf16[48,512]{1,0:T(8,128)(2,1)S(1)}, bf...) custom-call(bf16[512,512]{1,0:T(8,128)(2,1)} %bitcast.1.hubs_ref, ...), custom_call_target="tpu_custom_call" | custom-call | flops 2684354560 | bytes 8241152 | tf_op jit(solution)/shard_map/main/pallas_call | solution.py:75
  62.2 0.9 copy-done.6
  63.1 14.2 %all_to_all.20.sums_ref = bf16[16,32,512]{2,1,0:T(8,128)(2,1)S(1)} all-to-all(bf16[16,32,512]{2,1,0:T(8,128)(2,1)S(1)} %bitcast.11), channel_id=1, replica_groups=mesh['y'=4,'z'=16,'x'=4,'c'=2] {'y','x'}, dimensions={0} | all-to-all | bytes 1048576 | tf_op jit(solution)/shard_map/all_to_all | solution.py:350
  77.3 0.7 gather.1
  78.0 12.1 %all-to-all-start.3 = ((f32[16,8,128]{2,1,0:T(8,128)}), f32[16,8,128]{2,1,0:T(8,128)S(1)}, u32[]{:S(2)}, u32[]{:S(2)}) async-start(f32[16,8,128]{2,1,0:T(8,128)} %bitcast.9), calls=%async_computation.3 | async-start | bytes 131072 | tf_op jit(solution)/shard_map/all_to_all | solution.py:356
  90.1 2.8 %collective-permute-start.2 = (bf16[48,512]{1,0:T(8,128)(2,1)}, bf16[48,512]{1,0:T(8,128)(2,1)S(1)}, u32[]{:S(2)}, u32[]{:S(2)}) collective-permute-start(bf16[48,512]{1,0:T(8,128)(2,1)} %copy-done.26), channel_id=1, source_target_pairs={{0,2},{2,4},{4,6},{6,8},{8,10},{10,12},{12,14},{14,16},{16,18},{18... | collective-permute-start | bytes 147464 | tf_op jit(solution)/shard_map/ppermute | solution.py:245
  92.9 7.2 %collective-permute-start.3 = (bf16[48,512]{1,0:T(8,128)(2,1)}, bf16[48,512]{1,0:T(8,128)(2,1)S(1)}, u32[]{:S(2)}, u32[]{:S(2)}) collective-permute-start(bf16[48,512]{1,0:T(8,128)(2,1)} %copy-done.25), channel_id=1, source_target_pairs={{2,0},{4,2},{6,4},{8,6},{10,8},{12,10},{14,12},{16,14},{18,16},{20... | collective-permute-start | bytes 147464 | tf_op jit(solution)/shard_map/ppermute | solution.py:245
  100.2 1.0 copy-done.11
  101.1 1.0 copy-done.13
  102.1 0.9 copy-done.17
  103.0 0.9 copy-done.19
  103.9 2.0 %late.1 = (bf16[384,512]{1,0:T(8,128)(2,1)}, f32[160,512]{1,0:T(8,128)S(1)}) custom-call(s32[1]{0:T(128)} %bitcast.10.core_ref, bf16[768,512]{1,0:T(8,128)(2,1)S(1)} %copy-done.7, s32[2,768]{1,0:T(2,128)S(1)} %pad_add_fusion.ids_ref, f32[160,512]{1,0:T(8,128)S(1)} %copy-done.13, bf16[160,512]{1,0:T(8,128)(2,1)S(1)} %copy-done.19, f32[160,512]{1,0:T(8,128)S(1)} %copy-done.11, ...), custom_call_target="tpu_custom_call" | custom-call | flops 805306368 | bytes 5117956 | tf_op jit(solution)/shard_map/late/pallas_call | solution.py:75
  105.9 0.7 copy-done.14
  106.6 0.6 copy-done.20
  107.3 1.0 copy-done.15
  108.2 0.8 copy-done.21
  109.0 1.2 %last.1 = bf16[160,512]{1,0:T(8,128)(2,1)} custom-call(f32[16,8,128]{2,1,0:T(8,128)S(1)} %all-to-all-done.3.hub_ref, bf16[48,512]{1,0:T(8,128)(2,1)S(1)} %collective-permute-done.2.first_ref, bf16[48,512]{1,0:T(8,128)(2,1)S(1)} %copy-done.21, f32[160,512]{1,0:T(8,128)S(1)} %copy-done.15, bf16[512,512]{1,0:T(8,128)(2,1)S(1)} %copy-done), custom_call_target="tpu_custom_call" | custom-call | flops 167772160 | bytes 1179648 | tf_op jit(solution)/shard_map/last/pallas_call | solution.py:75
  (48 shorter events, 0.1 us)
Async XLA Ops:
  2.0 29.2 %all-to-all-start = ((f32[16,8,128]{2,1,0:T(8,128)}), f32[16,8,128]{2,1,0:T(8,128)S(1)}, u32[]{:S(2)}, u32[]{:S(2)}) async-start(f32[16,8,128]{2,1,0:T(8,128)} %broadcast_in_dim.12), calls=%async_computation | async-start | bytes 131072 | tf_op jit(solution)/shard_map/all_to_all | solution.py:278
  17.2 23.0 %copy-start = (bf16[512,512]{1,0:T(8,128)(2,1)S(1)}, bf16[512,512]{1,0:T(8,128)(2,1)}, u32[]{:S(2)}) copy-start(bf16[512,512]{1,0:T(8,128)(2,1)} %ws_ref.7) | copy-start | bytes 1572868
  17.2 23.0 %copy-start.1 = (bf16[512,512]{1,0:T(8,128)(2,1)S(1)}, bf16[512,512]{1,0:T(8,128)(2,1)}, u32[]{:S(2)}) copy-start(bf16[512,512]{1,0:T(8,128)(2,1)} %we_ref.3) | copy-start | bytes 1572868
  17.2 23.0 %copy-start.2 = (bf16[512,512]{1,0:T(8,128)(2,1)S(1)}, bf16[512,512]{1,0:T(8,128)(2,1)}, u32[]{:S(2)}) copy-start(bf16[512,512]{1,0:T(8,128)(2,1)} %wr_ref.3) | copy-start | bytes 1572868
  17.2 22.9 %copy-start.22 = (f32[512]{0:T(512)S(1)}, f32[512]{0:T(512)}, u32[]{:S(2)}) copy-start(f32[512]{0:T(512)} %param.24) | copy-start | bytes 6148
  18.2 21.9 %collective-permute-start.1 = (bf16[48,512]{1,0:T(8,128)(2,1)S(1)}, bf16[48,512]{1,0:T(8,128)(2,1)S(1)}, u32[]{:S(2)}, u32[]{:S(2)}) collective-permute-start(bf16[48,512]{1,0:T(8,128)(2,1)S(1)} %get-tuple-element.23), channel_id=1, source_target_pairs={{2,0},{4,2},{6,4},{8,6},{10,8},{12,10},{14,12},{16,14},{18,16},{20... | collective-permute-start | bytes 147464 | tf_op jit(solution)/shard_map/ppermute | solution.py:245
  25.3 14.8 %collective-permute-start = (bf16[48,512]{1,0:T(8,128)(2,1)S(1)}, bf16[48,512]{1,0:T(8,128)(2,1)S(1)}, u32[]{:S(2)}, u32[]{:S(2)}) collective-permute-start(bf16[48,512]{1,0:T(8,128)(2,1)S(1)} %get-tuple-element.24), channel_id=1, source_target_pairs={{0,2},{2,4},{4,6},{6,8},{8,10},{10,12},{12,14},{14,16},{16,18},{18... | collective-permute-start | bytes 147464 | tf_op jit(solution)/shard_map/ppermute | solution.py:245
  32.0 15.4 %all-to-all-start.1 = ((bf16[16,32,512]{2,1,0:T(8,128)(2,1)}), bf16[16,32,512]{2,1,0:T(8,128)(2,1)}, u32[]{:S(2)}, u32[]{:S(2)}) async-start(bf16[16,32,512]{2,1,0:T(8,128)(2,1)} %spread.1), calls=%async_computation.1 | async-start | bytes 1048576 | tf_op jit(solution)/shard_map/all_to_all | solution.py:287
  40.2 0.9 copy-start.8
  41.1 6.3 %copy-start.5 = (bf16[1024,512]{1,0:T(8,128)(2,1)S(1)}, bf16[1024,512]{1,0:T(8,128)(2,1)}, u32[]{:S(2)}) copy-start(bf16[1024,512]{1,0:T(8,128)(2,1)} %win_ref.3) | copy-start | bytes 3145732
  41.1 6.3 %copy-start.27 = (f32[512]{0:T(512)S(1)}, f32[512]{0:T(512)}, u32[]{:S(2)}) copy-start(f32[512]{0:T(512)} %param.26) | copy-start | bytes 6148
  41.1 6.3 %copy-start.28 = (f32[512]{0:T(512)S(1)}, f32[512]{0:T(512)}, u32[]{:S(2)}) copy-start(f32[512]{0:T(512)} %param.27) | copy-start | bytes 6148
  41.1 6.3 %copy-start.29 = (f32[512]{0:T(512)S(1)}, f32[512]{0:T(512)}, u32[]{:S(2)}) copy-start(f32[512]{0:T(512)} %param.29) | copy-start | bytes 6148
  41.1 6.3 %copy-start.30 = (f32[512]{0:T(512)S(1)}, f32[512]{0:T(512)}, u32[]{:S(2)}) copy-start(f32[512]{0:T(512)} %param.31) | copy-start | bytes 6148
  41.1 6.3 %copy-start.31 = (f32[512]{0:T(512)S(1)}, f32[512]{0:T(512)}, u32[]{:S(2)}) copy-start(f32[512]{0:T(512)} %param.32) | copy-start | bytes 6148
  43.0 1.2 %copy-start.3 = (f32[768,512]{1,0:T(8,128)}, f32[768,512]{1,0:T(8,128)S(1)}, u32[]{:S(2)}) copy-start(f32[768,512]{1,0:T(8,128)S(1)} %near.1.pre_ref) | copy-start | bytes 4718596
  47.5 1.4 %copy-start.4 = (f32[768,512]{1,0:T(8,128)S(1)}, f32[768,512]{1,0:T(8,128)}, u32[]{:S(2)}) copy-start(f32[768,512]{1,0:T(8,128)} %copy-done.3) | copy-start | bytes 4718596
  48.9 0.9 copy-start.9
  49.8 0.9 copy-start.16
  50.7 1.0 copy-start.23
  51.7 1.0 copy-start.24
  62.2 0.9 copy-start.6
  63.1 14.9 %copy-start.10 = (f32[160,512]{1,0:T(8,128)}, f32[160,512]{1,0:T(8,128)S(1)}, u32[]{:S(2)}) copy-start(f32[160,512]{1,0:T(8,128)S(1)} %get-tuple-element.20.own_ref) | copy-start | bytes 983044
  63.1 14.9 %copy-start.12 = (f32[160,512]{1,0:T(8,128)}, f32[160,512]{1,0:T(8,128)S(1)}, u32[]{:S(2)}) copy-start(f32[160,512]{1,0:T(8,128)S(1)} %get-tuple-element.18.gg_ref) | copy-start | bytes 983044
  63.1 14.9 %copy-start.18 = (bf16[160,512]{1,0:T(8,128)(2,1)}, bf16[160,512]{1,0:T(8,128)(2,1)S(1)}, u32[]{:S(2)}) copy-start(bf16[160,512]{1,0:T(8,128)(2,1)S(1)} %get-tuple-element.19.ndpre_ref) | copy-start | bytes 491524
  63.1 14.9 %copy-start.26 = (bf16[48,512]{1,0:T(8,128)(2,1)}, bf16[48,512]{1,0:T(8,128)(2,1)S(1)}, u32[]{:S(2)}) copy-start(bf16[48,512]{1,0:T(8,128)(2,1)S(1)} %get-tuple-element.15) | copy-start | bytes 147460
  63.1 14.9 %copy-start.25 = (bf16[48,512]{1,0:T(8,128)(2,1)}, bf16[48,512]{1,0:T(8,128)(2,1)S(1)}, u32[]{:S(2)}) copy-start(bf16[48,512]{1,0:T(8,128)(2,1)S(1)} %get-tuple-element.16) | copy-start | bytes 147460
  63.1 37.1 %copy-start.7 = (bf16[768,512]{1,0:T(8,128)(2,1)S(1)}, bf16[768,512]{1,0:T(8,128)(2,1)}, u32[]{:S(2)}) copy-start(bf16[768,512]{1,0:T(8,128)(2,1)} %copy-done.6) | copy-start | bytes 2359300
  78.0 29.3 %all-to-all-start.3 = ((f32[16,8,128]{2,1,0:T(8,128)}), f32[16,8,128]{2,1,0:T(8,128)S(1)}, u32[]{:S(2)}, u32[]{:S(2)}) async-start(f32[16,8,128]{2,1,0:T(8,128)} %bitcast.9), calls=%async_computation.3 | async-start | bytes 131072 | tf_op jit(solution)/shard_map/all_to_all | solution.py:356
  90.1 16.5 %collective-permute-start.2 = (bf16[48,512]{1,0:T(8,128)(2,1)}, bf16[48,512]{1,0:T(8,128)(2,1)S(1)}, u32[]{:S(2)}, u32[]{:S(2)}) collective-permute-start(bf16[48,512]{1,0:T(8,128)(2,1)} %copy-done.26), channel_id=1, source_target_pairs={{0,2},{2,4},{4,6},{6,8},{8,10},{10,12},{12,14},{14,16},{16,18},{18... | collective-permute-start | bytes 147464 | tf_op jit(solution)/shard_map/ppermute | solution.py:245
  92.9 13.7 %collective-permute-start.3 = (bf16[48,512]{1,0:T(8,128)(2,1)}, bf16[48,512]{1,0:T(8,128)(2,1)S(1)}, u32[]{:S(2)}, u32[]{:S(2)}) collective-permute-start(bf16[48,512]{1,0:T(8,128)(2,1)} %copy-done.25), channel_id=1, source_target_pairs={{2,0},{4,2},{6,4},{8,6},{10,8},{12,10},{14,12},{16,14},{18,16},{20... | collective-permute-start | bytes 147464 | tf_op jit(solution)/shard_map/ppermute | solution.py:245
  100.2 1.0 copy-start.11
  101.1 1.0 copy-start.13
  102.1 0.9 copy-start.17
  103.0 0.9 copy-start.19
  105.9 0.7 copy-start.14
  106.6 0.6 copy-start.20
  107.3 1.0 copy-start.15
  108.2 0.8 copy-start.21

commit v3 on v2

v3 whole, which is shorter than its diff:
```python
import functools
import math

import jax
import jax.numpy as jnp
import numpy as np
from jax import lax
from jax.experimental import pallas as pl
from jax.experimental.pallas import tpu as pltpu
from jax.sharding import Mesh, PartitionSpec as P

RIM = 48
HUB_DEV = 2
EPS = 1e-05
BF = jnp.bfloat16
F32 = jnp.float32
I32 = jnp.int32
ALL = ("y", "z", "x", "c")
SPACE = ("y", "z", "x")
PLANE = ("y", "x")
LANES = 128
TILE = 256
SHAPE = (4, 16, 4)
GRANT = 60 * 1024 * 1024


def dot(a, b):
    return jnp.dot(a, b, preferred_element_type=F32)


def dot_t(a, b):
    return lax.dot_general(a, b, (((1,), (1,)), ((), ())), preferred_element_type=F32)


def split2(v):
    high = v.astype(BF)
    return high, (v - high.astype(F32)).astype(BF)


def row_mean(v):
    return jnp.mean(v, axis=-1, keepdims=True)


def layer_stats(values):
    centred = values - row_mean(values)
    inv_scale = lax.rsqrt(row_mean(centred * centred) + EPS)
    return centred * inv_scale, inv_scale


def norm_back(upstream, normed, inv_scale, gain_vec):
    scaled = upstream * gain_vec
    return inv_scale * (scaled - row_mean(scaled) - normed * row_mean(scaled * normed))


def hot_rows(ids, first, count):
    edges = ids.shape[1]
    column = jnp.broadcast_to(ids - first, (LANES, edges)).T
    lane = lax.broadcasted_iota(I32, (edges, LANES), 1)
    parts = [
        jnp.where(column == lane + k, 1.0, 0.0).astype(BF) for k in range(0, count, LANES)
    ]
    return jnp.concatenate(parts, axis=1)[:, :count]


def hot_cols(ids, first, count):
    edges = ids.shape[1]
    slot = lax.broadcasted_iota(I32, (count, edges), 0)
    return jnp.where(slot == ids - first, 1.0, 0.0).astype(BF)


VM = pl.BlockSpec(memory_space=pltpu.VMEM)
SM = pl.BlockSpec(memory_space=pltpu.SMEM)
HB = pl.BlockSpec(memory_space=pltpu.HBM)


def call(kernel, ins, outs, scratch=(), copies=0, flops=0, room=0, name=None):
    shapes = [jax.ShapeDtypeStruct(s, d) for s, d, _ in outs]
    args = [a for a, _ in ins]
    moved = sum(math.prod(o.shape) * o.dtype.itemsize for o in shapes + args)
    scratch = list(scratch)
    if copies:
        scratch.append(pltpu.SemaphoreType.DMA((copies,)))
    return pl.pallas_call(
        kernel,
        out_shape=shapes,
        in_specs=[spec for _, spec in ins],
        out_specs=[spec for _, _, spec in outs],
        scratch_shapes=scratch,
        compiler_params=pltpu.CompilerParams(vmem_limit_bytes=GRANT - room * 1024),
        cost_estimate=pl.CostEstimate(flops=flops, bytes_accessed=moved, transcendentals=0),
        name=name,
    )(*args)


def start_copies(pairs, sems, first=0):
    copies = [
        pltpu.make_async_copy(src, dst, sems.at[first + k]) for k, (src, dst) in enumerate(pairs)
    ]
    for copy in copies:
        copy.start()
    return copies


def prep_kernel(core_ref, nodes_ref, hub_ref, rim_ref, head_ref, sems):
    node_count = nodes_ref.shape[0]
    start = pl.multiple_of((1 - core_ref[0]) * (node_count - RIM), 16)
    head, rim = start_copies(
        [(nodes_ref.at[:16], head_ref), (nodes_ref.at[pl.ds(start, RIM)], rim_ref)], sems
    )
    head.wait()
    rows = head_ref[...].astype(F32)
    tile = jnp.concatenate(
        [rows[r : r + 1, j * LANES : (j + 1) * LANES] for r in range(HUB_DEV) for j in range(4)],
        axis=0,
    )
    for z in range(hub_ref.shape[0]):
        hub_ref[z] = tile
    rim.wait()


def spread_kernel(rows_ref, out_ref):
    nz = rows_ref.shape[0] // 8
    parts = []
    for r in range(HUB_DEV):
        lanes = [rows_ref[pl.ds(4 * r + j, nz, stride=8), :] for j in range(4)]
        parts.append(jnp.concatenate(lanes, axis=1))
    rows = jnp.concatenate(parts, axis=0).astype(BF)
    for p in range(out_ref.shape[0]):
        out_ref[p] = rows


def gather_kernel(sums_ref, rim_ref, flag_ref, out_ref, rim_out_ref, buf_ref, sems):
    del flag_ref
    planes = sums_ref.shape[0]
    nz = out_ref.shape[0] // 8
    quarter = planes // 4
    pairs = [
        (sums_ref.at[pl.ds(k * quarter, quarter)], buf_ref.at[pl.ds(k * quarter, quarter)])
        for k in range(4)
    ]
    *copies, rim = start_copies(pairs + [(rim_ref, rim_out_ref)], sems)
    total = jnp.zeros(buf_ref.shape[1:], F32)
    for p in range(planes):
        if p % quarter == 0:
            copies[p // quarter].wait()
        total += buf_ref[p].astype(F32)
    for r in range(HUB_DEV):
        for j in range(4):
            out_ref[pl.ds(4 * r + j, nz, stride=8), :] = total[
                r * nz : (r + 1) * nz, j * LANES : (j + 1) * LANES
            ]
    rim.wait()


def near_kernel(
    edges_in, ids_ref, nodes_in, rims_in, we_in, ws_in, wr_in, bias_ref,
    pre_out,
    edges_ref, frame_ref, we_ref, ws_ref, wr_ref, send_ref, recv_ref, pre_ref, sems,
):
    node_count = nodes_in.shape[0]
    slots = 2 * RIM + node_count
    copies = start_copies(
        [
            (nodes_in, frame_ref.at[pl.ds(RIM, node_count)]),
            (rims_in.at[pl.ds(0, RIM)], frame_ref.at[pl.ds(0, RIM)]),
            (rims_in.at[pl.ds(RIM, RIM)], frame_ref.at[pl.ds(RIM + node_count, RIM)]),
            (ws_in, ws_ref),
            (wr_in, wr_ref),
            (we_in, we_ref),
            (edges_in, edges_ref),
        ],
        sems,
    )
    for copy in copies[:4]:
        copy.wait()
    send_ref[...] = dot(frame_ref[...], ws_ref[...]).astype(BF)
    copies[4].wait()
    recv_ref[...] = dot(frame_ref[...], wr_ref[...]).astype(BF)
    copies[5].wait()
    copies[6].wait()
    back = []
    for i in range(edges_in.shape[0] // TILE):
        rows = pl.ds(i * TILE, TILE)
        pre = dot(edges_ref[rows, :], we_ref[...])
        pre += dot(hot_rows(ids_ref[0:1, rows], 0, slots), send_ref[...])
        pre += dot(hot_rows(ids_ref[1:2, rows], 0, slots), recv_ref[...])
        pre_ref[rows, :] = pre + bias_ref[...]
        back += start_copies([(pre_ref.at[rows], pre_out.at[rows])], sems, 7 + i)
    for copy in back:
        copy.wait()


def main_kernel(
    core_ref, hubs_in, pre_in, edges_in, ids_ref, nodes_in, cot_in, ws_in, wo_in, win_in, wout_in,
    egain_ref, eshift_ref, nbias_ref, ngain_ref, nshift_ref,
    new_ref, dpre_out, hub_sums_out, rim_ref, own_out, gg_out, ndpre_out,
    hubs_ref, pre_ref, edges_ref, nodes_ref, cot_ref, ws_ref, wo_ref, win_ref, wout_ref,
    dpre_ref, hub_sums_ref, gg_ref, ndpre_ref,
    terms_ref, normed_ref, scale_ref, gathered_ref, high_ref, low_ref, sems,
):
    node_count, width = nodes_in.shape
    hub_count = hubs_in.shape[0]
    edge_count = edges_in.shape[0]
    steps = edge_count // TILE
    slots = 2 * RIM + node_count
    own = slice(RIM, RIM + node_count)
    tiles = [pl.ds(i * TILE, TILE) for i in range(steps)]
    hubs, ws, wo, nodes, cot, win, wout, *rest = start_copies(
        [
            (hubs_in, hubs_ref),
            (ws_in, ws_ref),
            (wo_in, wo_ref),
            (nodes_in, nodes_ref),
            (cot_in, cot_ref),
            (win_in, win_ref),
            (wout_in, wout_ref),
        ]
        + [(pre_in.at[rows], pre_ref.at[rows]) for rows in tiles]
        + [(edges_in.at[rows], edges_ref.at[rows]) for rows in tiles],
        sems,
    )
    done = 7 + 2 * steps
    gathered_ref[...] = jnp.zeros_like(gathered_ref)
    hubs.wait()
    ws.wait()
    terms_ref[...] = dot(hubs_ref[...], ws_ref[...]).astype(BF)
    wo.wait()
    for copy in rest:
        copy.wait()

    def forward(i, carry):
        rows = pl.ds(pl.multiple_of(i * TILE, TILE), TILE)
        pre = pre_ref[rows, :] + dot(hot_rows(ids_ref[0:1, rows], slots, hub_count), terms_ref[...])
        gate = jax.nn.sigmoid(pre)
        pre_ref[rows, :] = gate * (1.0 + pre * (1.0 - gate))
        edge_sum = dot((pre * gate).astype(BF), wo_ref[...])
        normed, scale = layer_stats(edge_sum)
        normed_ref[rows, :] = normed
        scale_ref[rows, :] = jnp.broadcast_to(scale, (TILE, LANES))
        new_edges = edges_ref[rows, :].astype(F32) + normed * egain_ref[...] + eshift_ref[...]
        gathered_ref[...] += dot(hot_cols(ids_ref[1:2, rows], 0, slots), new_edges.astype(BF))
        return carry

    lax.fori_loop(0, steps, forward, 0)

    for copy in (nodes, cot, win, wout):
        copy.wait()
    nodes = nodes_ref[...]
    gathered = gathered_ref[own].astype(BF)
    node_pre = dot(nodes, win_ref[:width]) + dot(gathered, win_ref[width:]) + nbias_ref[...]
    gate = jax.nn.sigmoid(node_pre)
    node_mix = dot((node_pre * gate).astype(BF), wout_ref[...])
    normed, scale = layer_stats(node_mix)
    new_nodes = nodes.astype(F32) + normed * ngain_ref[...] + nshift_ref[...]
    new_ref[...] = new_nodes.astype(BF)
    dmix = norm_back(cot_ref[...].astype(F32), normed, scale, ngain_ref[...]).astype(BF)
    ndpre = dot_t(dmix, wout_ref[...]) * (gate * (1.0 + node_pre * (1.0 - gate)))
    ndpre = ndpre.astype(BF)
    ndpre_ref[...] = ndpre
    gathered_grad = dot_t(ndpre, win_ref[width:])
    gg_ref[...] = gathered_grad
    back = start_copies([(ndpre_ref, ndpre_out), (gg_ref, gg_out)], sems, done)
    high, low = split2(gathered_grad)
    for ref, part in ((high_ref, high), (low_ref, low)):
        ref[...] = jnp.zeros_like(ref)
        ref[own] = part

    def backward(i, carry):
        rows = pl.ds(pl.multiple_of(i * TILE, TILE), TILE)
        hot = hot_rows(ids_ref[1:2, rows], 0, slots)
        upstream = dot(hot, high_ref[...]) + dot(hot, low_ref[...])
        dsum = norm_back(upstream, normed_ref[rows, :], scale_ref[rows, :1], egain_ref[...])
        dpre_ref[rows, :] = (dot_t(dsum.astype(BF), wo_ref[...]) * pre_ref[rows, :]).astype(BF)
        return carry

    lax.fori_loop(0, steps, backward, 0)

    back += start_copies([(dpre_ref, dpre_out)], sems, done + 2)
    dpre = dpre_ref[...]
    hub_sums_ref[...] = dot(hot_cols(ids_ref[0:1, :], slots, hub_count), dpre).astype(BF)
    back += start_copies([(hub_sums_ref, hub_sums_out)], sems, done + 3)
    gathered_ref[...] = dot(hot_cols(ids_ref[0:1, :], 0, slots), dpre)
    back += start_copies([(gathered_ref.at[pl.ds(RIM, node_count)], own_out)], sems, done + 4)
    start = pl.multiple_of(core_ref[0] * (RIM + node_count), 16)
    rim_ref[...] = gathered_ref[pl.ds(start, RIM), :].astype(BF)
    for copy in back:
        copy.wait()


def late_kernel(
    core_ref, dpre_in, ids_ref, gg_in, ndpre_in, own_in, cot_in, we_in, ws_in, wr_in, win_in,
    egrad_ref, base_ref, flag_ref,
    dpre_ref, gg_ref, ndpre_ref, own_ref, cot_ref, we_ref, ws_ref, wr_ref, win_ref,
    high_ref, low_ref, sems,
):
    node_count, width = cot_in.shape
    slots = 2 * RIM + node_count
    own = slice(RIM, RIM + node_count)
    half = egrad_ref.shape[0]
    copies = start_copies(
        [
            (gg_in, gg_ref),
            (dpre_in, dpre_ref),
            (we_in, we_ref),
            (ndpre_in, ndpre_ref),
            (own_in, own_ref),
            (cot_in, cot_ref),
            (win_in.at[pl.ds(0, width)], win_ref),
            (ws_in, ws_ref),
            (wr_in, wr_ref),
        ],
        sems,
    )
    for copy in copies:
        copy.wait()
    high, low = split2(gg_ref[...])
    for ref, part in ((high_ref, high), (low_ref, low)):
        ref[...] = jnp.zeros_like(ref)
        ref[own] = part
    rows = pl.ds(pl.multiple_of(core_ref[0] * half, half), half)
    hot = hot_rows(ids_ref[1:2, rows], 0, slots)
    upstream = dot(hot, high_ref[...]) + dot(hot, low_ref[...])
    egrad_ref[...] = (upstream + dot_t(dpre_ref[rows, :], we_ref[...])).astype(BF)
    base = cot_ref[...].astype(F32) + dot_t(ndpre_ref[...], win_ref[...])
    recv = dot(hot_cols(ids_ref[1:2, :], RIM, node_count), dpre_ref[...])
    for sums, weight in ((own_ref[...], ws_ref), (recv, wr_ref)):
        high, low = split2(sums)
        base += dot_t(high, weight[...]) + dot_t(low, weight[...])
    base_ref[...] = base
    flag_ref[...] = jnp.zeros_like(flag_ref)


def last_kernel(hub_ref, rims_in, base_in, ws_in, out_ref, rims_ref, base_ref, ws_ref, sums_ref, sems):
    node_count = base_in.shape[0]
    copies = start_copies([(rims_in, rims_ref), (ws_in, ws_ref), (base_in, base_ref)], sems)
    hub = hub_ref[0]
    for z in range(1, hub_ref.shape[0]):
        hub += hub_ref[z]
    rows = [
        jnp.concatenate([hub[4 * r + j : 4 * r + j + 1] for j in range(4)], axis=1)
        for r in range(HUB_DEV)
    ]
    sums_ref[...] = jnp.zeros_like(sums_ref)
    copies[0].wait()
    sums_ref[:RIM] = rims_ref[RIM:].astype(F32)
    for r in range(HUB_DEV):
        sums_ref[r : r + 1] += rows[r]
    sums_ref[node_count - RIM :] += rims_ref[:RIM].astype(F32)
    high, low = split2(sums_ref[...])
    copies[1].wait()
    extra = dot_t(high, ws_ref[...]) + dot_t(low, ws_ref[...])
    copies[2].wait()
    out_ref[...] = (base_ref[...] + extra).astype(BF)


def both_ways(x, step):
    count = math.prod(lax.axis_size(a) for a in SPACE)
    pairs = [
        (2 * i + c, 2 * (i + d) + c)
        for i in range(count)
        for c, d in ((0, step), (1, -step))
        if 0 <= i + d < count
    ]
    return lax.ppermute(x, ALL, pairs)


def body(
    nodes,
    edges,
    senders,
    receivers,
    edge_proj,
    send_proj,
    recv_proj,
    edge_bias,
    edge_out,
    edge_gain,
    edge_shift,
    node_in,
    node_bias,
    node_out,
    node_gain,
    node_shift,
    node_cot,
):
    node_count, width = nodes.shape
    half = edges.shape[0]
    edge_count = 2 * half
    steps = edge_count // TILE
    ny, nz, nx = (lax.axis_size(a) for a in SPACE)
    plane = ny * nx
    hub_count = plane * HUB_DEV * nz
    slots = 2 * RIM + node_count
    core = lax.axis_index("c").astype(I32)
    own_block = lax.axis_index(SPACE)
    row = lambda v: (v.reshape(1, width), VM)
    wide = lambda rows, kind=BF: pltpu.VMEM((rows, width), kind)
    square = 2 * width * width

    my_hub, my_rim = call(
        prep_kernel,
        [(core.reshape(1), SM), (nodes, HB)],
        [((nz, 8, LANES), F32, VM), ((RIM, width), BF, VM)],
        [wide(16)],
        copies=2,
        name="prep",
    )
    by_z = lax.all_to_all(my_hub, "z", 0, 0)
    rim = both_ways(my_rim, 1)
    (spread,) = call(
        spread_kernel,
        [(by_z.reshape(nz * 8, LANES), VM)],
        [((plane, HUB_DEV * nz, width), BF, VM)],
        room=54000,
        name="spread",
    )
    hubs = lax.all_to_all(spread, PLANE, 0, 0).reshape(hub_count, width)

    rims = lax.all_gather(rim, "c", axis=0, tiled=True)
    all_edges = lax.all_gather(edges, "c", axis=0, tiled=True)
    ids = lax.all_gather(jnp.stack([senders, receivers]), "c", axis=1, tiled=True)
    block = ids[0] // node_count
    line = ids[0] - block * node_count
    hub_y, hub_zx = block // (nz * nx), block % (nz * nx)
    hub_z, hub_x = hub_zx // nx, hub_zx % nx
    hub_slot = ((hub_y * nx + hub_x) * HUB_DEV + line) * nz + hub_z
    slot = jnp.where(
        block == own_block,
        RIM + line,
        jnp.where(
            (block == own_block - 1) & (line >= node_count - RIM),
            line - (node_count - RIM),
            jnp.where(
                (block == own_block + 1) & (line < RIM),
                RIM + node_count + line,
                slots + hub_slot,
            ),
        ),
    )
    ids = jnp.stack([slot, ids[1] - own_block * node_count + RIM])

    (near,) = call(
        near_kernel,
        [
            (all_edges, HB), (ids, VM), (nodes, HB), (rims, HB),
            (edge_proj, HB), (send_proj, HB), (recv_proj, HB), row(edge_bias),
        ],
        [((edge_count, width), F32, HB)],
        [wide(edge_count)] + [wide(slots)] + [wide(width)] * 3 + [wide(slots)] * 2
        + [wide(edge_count, F32)],
        copies=7 + steps,
        flops=square * (edge_count * 2 + 2 * slots),
        name="near",
    )
    new_nodes, dpre, hub_sums, my_rim, own_sums, gathered_grad, node_dpre = call(
        main_kernel,
        [
            (core.reshape(1), SM), (hubs, HB), (near, HB), (all_edges, HB), (ids, VM), (nodes, HB),
            (node_cot, HB), (send_proj, HB), (edge_out, HB), (node_in, HB), (node_out, HB),
            row(edge_gain), row(edge_shift), row(node_bias), row(node_gain), row(node_shift),
        ],
        [
            ((node_count, width), BF, VM),
            ((edge_count, width), BF, HB),
            ((hub_count, width), BF, HB),
            ((RIM, width), BF, VM),
            ((node_count, width), F32, HB),
            ((node_count, width), F32, HB),
            ((node_count, width), BF, HB),
        ],
        [wide(hub_count), wide(edge_count, F32), wide(edge_count)]
        + [wide(node_count)] * 2 + [wide(width)] * 2 + [wide(2 * width), wide(width)]
        + [wide(edge_count), wide(hub_count), wide(node_count, F32), wide(node_count)]
        + [wide(hub_count), wide(edge_count, F32), pltpu.VMEM((edge_count, LANES), F32)]
        + [wide(slots, F32), wide(slots), wide(slots)],
        copies=12 + 2 * steps,
        flops=square * (edge_count * 6 + hub_count),
        room=0,
        name="main",
    )

    hub_back = lax.all_to_all(hub_sums.reshape(plane, HUB_DEV * nz, width), PLANE, 0, 0)
    rim = both_ways(my_rim, -1)
    edge_grad, base, flag = call(
        late_kernel,
        [
            (core.reshape(1), SM), (dpre, HB), (ids, VM), (gathered_grad, HB), (node_dpre, HB),
            (own_sums, HB), (node_cot, HB), (edge_proj, HB), (send_proj, HB), (recv_proj, HB),
            (node_in, HB),
        ],
        [((half, width), BF, VM), ((node_count, width), F32, VM), ((8, LANES), F32, VM)],
        [wide(edge_count), wide(node_count, F32), wide(node_count), wide(node_count, F32)]
        + [wide(node_count)] + [wide(width)] * 4 + [wide(slots)] * 2,
        copies=9,
        flops=square * edge_count * 2,
        name="late",
    )
    by_z, rim = call(
        gather_kernel,
        [(hub_back, HB), (rim, HB), (flag, HB)],
        [((nz * 8, LANES), F32, VM), ((RIM, width), BF, VM)],
        [pltpu.VMEM((plane, HUB_DEV * nz, width), BF)],
        copies=5,
        room=54000,
        name="gather",
    )
    hub_back = lax.all_to_all(by_z.reshape(nz, 8, LANES), "z", 0, 0)
    rims = lax.all_gather(rim, "c", axis=0, tiled=True)
    (node_grad,) = call(
        last_kernel,
        [(hub_back, VM), (rims, HB), (base, HB), (send_proj, HB)],
        [((node_count, width), BF, VM)],
        [wide(2 * RIM), wide(node_count, F32), wide(width), wide(node_count, F32)],
        copies=3,
        flops=square * node_count * 2,
        room=0,
        name="last",
    )
    return new_nodes, node_grad, edge_grad


def solution(mesh):
    fine = Mesh(np.asarray(mesh.devices).reshape(*SHAPE, 2), ALL)
    rows, both = P(SPACE, None), P(ALL, None)
    whole = P()
    in_specs = (rows, both, P(ALL), P(ALL)) + (whole,) * 12 + (rows,)
    return jax.shard_map(
        body, mesh=fine, in_specs=in_specs, out_specs=(rows, rows, both), check_vma=False
    )
```

time: 111 us -> 106 us (0.955)
  the two profiles are of different devices: /device:TPU:8 before, /device:TPU:1 now
where the time goes in v3:
time: 106 us; the launch traced here: 104 us
  starting transfers between devices  41.8 us (39%)
  Pallas kernels  28.8 us (27%)
  blocking collectives  16.7 us (16%)
  waiting for transfers between devices  11.9 us (11%)
  local copies, waits for them, and re-layouts  3.46 us (3%)
    pallas_call x7, Pallas kernels, call(): pl.pallas_call(kernel, out_shape=shapes, in_specs=[spec for _, spec in in...  28.8 us
    all_to_all x1, starting transfers between devices, body(): by_z = lax.all_to_all(my_hub, 'z', 0, 0)  15.7 us
    all_to_all x1, starting transfers between devices, body(): hub_back = lax.all_to_all(by_z.reshape(nz, 8, LANES), 'z', 0, 0)  7.76 us
    all_to_all x1, waiting for transfers between devices, body(): hub_back = lax.all_to_all(by_z.reshape(nz, 8, LANES), 'z', 0, 0)  7.59 us
    all_to_all x1, starting transfers between devices, body(): lax.all_to_all(hub_sums.reshape(plane, HUB_DEV * nz, width), PLANE, 0, 0)  6.94 us
    all_gather x1, blocking collectives, body(): all_edges = lax.all_gather(edges, 'c', axis=0, tiled=True)  6.92 us
    all_to_all x1, starting transfers between devices, body(): hubs = lax.all_to_all(spread, PLANE, 0, 0).reshape(hub_count, width)  6.75 us
    all_gather x2, blocking collectives, body(): rims = lax.all_gather(rim, 'c', axis=0, tiled=True)  5.98 us
  transfers between devices with their start and end apart: 6, of which 3 were waited for; matrix products, arithmetic and copies ran while one was open for 2% of the time, Pallas kernels for 10%

profile of v3, /device:TPU:1, one launch (start us, length us, event | category | flops | bytes accessed | tf_op | source)
XLA Modules:
  0.0 104.2 jit_solution(18249949071874367560)
XLA Ops:
  0.6 1.5 %prep.1 = (f32[16,8,128]{2,1,0:T(8,128)}, bf16[48,512]{1,0:T(8,128)(2,1)}) custom-call(s32[1]{0:T(128)} %bitcast.core_ref, bf16[160,512]{1,0:T(8,128)(2,1)} %nodes_in.3), custom_call_target="tpu_custom_call" | custom-call | bytes 278532 | tf_op jit(solution)/shard_map/prep/pallas_call | solution.py:83
  2.2 15.7 %all-to-all-start = ((f32[16,8,128]{2,1,0:T(8,128)}), f32[16,8,128]{2,1,0:T(8,128)S(1)}, u32[]{:S(2)}, u32[]{:S(2)}) async-start(f32[16,8,128]{2,1,0:T(8,128)} %get-tuple-element.17), calls=%async_computation | async-start | bytes 131072 | tf_op jit(solution)/shard_map/all_to_all | solution.py:408
  17.9 1.3 %collective-permute-start = (bf16[48,512]{1,0:T(8,128)(2,1)}, bf16[48,512]{1,0:T(8,128)(2,1)S(1)}, u32[]{:S(2)}, u32[]{:S(2)}) collective-permute-start(bf16[48,512]{1,0:T(8,128)(2,1)} %get-tuple-element.18), channel_id=1, source_target_pairs={{0,2},{2,4},{3,1},{4,6},{5,3},{6,8},{7,5},{8,10},{9,7},{10,12},{11... | collective-permute-start | bytes 147464 | tf_op jit(solution)/shard_map/ppermute | solution.py:364
  19.2 0.7 stack.14
  19.9 0.7 stack.15
  20.6 6.9 %all_gather.12.edges_in = bf16[768,512]{1,0:T(8,128)(2,1)} all-gather(bf16[384,512]{1,0:T(8,128)(2,1)} %param.18), channel_id=1, replica_groups=mesh['y'=4,'z'=16,'x'=4,'c'=2] {'c'}, dimensions={0}, use_global_device_ids=true | all-gather | bytes 1179648 | tf_op jit(solution)/shard_map/all_gather | solution.py:420
  27.5 2.0 %all-to-all-done = f32[16,8,128]{2,1,0:T(8,128)S(1)} async-done(((f32[16,8,128]{2,1,0:T(8,128)}), f32[16,8,128]{2,1,0:T(8,128)S(1)}, u32[]{:S(2)}, u32[]{:S(2)}) %all-to-all-start) | async-done | bytes 65568 | tf_op jit(solution)/shard_map/all_to_all | solution.py:408
  29.5 0.9 spread.1
  30.4 6.8 %all-to-all-start.1 = ((bf16[16,32,512]{2,1,0:T(8,128)(2,1)}), bf16[16,32,512]{2,1,0:T(8,128)(2,1)S(1)}, u32[]{:S(2)}, u32[]{:S(2)}) async-start(bf16[16,32,512]{2,1,0:T(8,128)(2,1)} %spread.1), calls=%async_computation.1 | async-start | bytes 1048576 | tf_op jit(solution)/shard_map/all_to_all | solution.py:417
  37.1 3.8 %all_gather.13 = s32[2,768]{1,0:T(2,128)S(1)} all-gather(s32[2,384]{1,0:T(2,128)S(1)} %pad_add_fusion.1), channel_id=1, replica_groups=mesh['y'=4,'z'=16,'x'=4,'c'=2] {'c'}, dimensions={1}, use_global_device_ids=true | all-gather | bytes 9216 | tf_op jit(solution)/shard_map/all_gather | solution.py:421
  41.0 0.1 compare_select_fusion
  41.1 0.6 pad_add_fusion.ids_ref
  41.7 0.0 collective-permute-done
  41.7 2.0 %all_gather.14.rims_in = bf16[96,512]{1,0:T(8,128)(2,1)} all-gather(bf16[48,512]{1,0:T(8,128)(2,1)S(1)} %collective-permute-done), channel_id=1, replica_groups=mesh['y'=4,'z'=16,'x'=4,'c'=2] {'c'}, dimensions={0}, use_global_device_ids=true | all-gather | bytes 147456 | tf_op jit(solution)/shard_map/all_gather | solution.py:419
  43.7 4.4 %near.1.pre_in = f32[768,512]{1,0:T(8,128)} custom-call(bf16[768,512]{1,0:T(8,128)(2,1)} %all_gather.12.edges_in, s32[2,768]{1,0:T(2,128)} %pad_add_fusion.ids_ref, bf16[160,512]{1,0:T(8,128)(2,1)} %nodes_in.3, bf16[96,512]{1,0:T(8,128)(2,1)} %all_gather.14.rims_in, bf16[512,512]{1,0:T(8,128)(2,1)} %we_in.3, bf16[512,512]{1,0:T(8,128)(2,1)} %ws_in.7, ...), custom_call_target="tpu_custom_call" | custom-call | flops 1073741824 | bytes 4202496 | tf_op jit(solution)/shard_map/near/pallas_call | solution.py:83
  48.1 0.0 all-to-all-done.1
  48.1 0.0 copy-start.1
  48.1 0.8 copy-done.1
  48.9 12.3 %main.1 = (bf16[160,512]{1,0:T(8,128)(2,1)}, bf16[768,512]{1,0:T(8,128)(2,1)}, bf16[512,512]{1,0:T(8,128)(2,1)}, bf16[48,512]{1,0:T(8,128)(2,1)}, f32[160,512]{1...) custom-call(s32[1]{0:T(128)} %bitcast.core_ref, bf16[512,512]{1,0:T(8,128)(2,1)} %bitcast.12, ...), custom_call_target="tpu_custom_call" | custom-call | flops 2684354560 | bytes 8192004 | tf_op jit(solution)/shard_map/main/pallas_call | solution.py:83
  61.2 6.9 %all-to-all-start.2 = ((bf16[16,32,512]{2,1,0:T(8,128)(2,1)}), bf16[16,32,512]{2,1,0:T(8,128)(2,1)S(1)}, u32[]{:S(2)}, u32[]{:S(2)}) async-start(bf16[16,32,512]{2,1,0:T(8,128)(2,1)} %bitcast.13), calls=%async_computation.2 | async-start | bytes 1048576 | tf_op jit(solution)/shard_map/all_to_all | solution.py:482
  68.2 3.3 %collective-permute-start.1 = (bf16[48,512]{1,0:T(8,128)(2,1)}, bf16[48,512]{1,0:T(8,128)(2,1)S(1)}, u32[]{:S(2)}, u32[]{:S(2)}) collective-permute-start(bf16[48,512]{1,0:T(8,128)(2,1)} %get-tuple-element.21), channel_id=1, source_target_pairs={{1,3},{2,0},{3,5},{4,2},{5,7},{6,4},{7,9},{8,6},{9,11},{10,8},{11,... | collective-permute-start | bytes 147464 | tf_op jit(solution)/shard_map/ppermute | solution.py:364
  71.4 5.1 %late.1 = (bf16[384,512]{1,0:T(8,128)(2,1)}, f32[160,512]{1,0:T(8,128)}, f32[8,128]{1,0:T(8,128)}) custom-call(s32[1]{0:T(128)} %bitcast.core_ref, bf16[768,512]{1,0:T(8,128)(2,1)} %get-tuple-element.22.dpre_in, s32[2,768]{1,0:T(2,128)} %pad_add_fusion.ids_ref, f32[160,512]{1,0:T(8,128)} %get-tuple-element.23.gg_in, ...), custom_call_target="tpu_custom_call" | custom-call | flops 805306368 | bytes 5122052 | tf_op jit(solution)/shard_map/late/pallas_call | solution.py:83
  76.6 0.0 collective-permute-done.1.rim_ref
  76.6 2.4 %all-to-all-done.2.sums_ref = bf16[16,32,512]{2,1,0:T(8,128)(2,1)S(1)} async-done(((bf16[16,32,512]{2,1,0:T(8,128)(2,1)}), bf16[16,32,512]{2,1,0:T(8,128)(2,1)S(1)}, u32[]{:S(2)}, u32[]{:S(2)}) %all-to-all-start.2) | async-done | bytes 524320 | tf_op jit(solution)/shard_map/all_to_all | solution.py:482
  78.9 0.0 copy-start
  78.9 0.7 copy-done
  79.6 1.5 %gather.1 = (f32[128,128]{1,0:T(8,128)}, bf16[48,512]{1,0:T(8,128)(2,1)S(1)}) custom-call(bf16[16,32,512]{2,1,0:T(8,128)(2,1)S(1)} %all-to-all-done.2.sums_ref, bf16[48,512]{1,0:T(8,128)(2,1)S(1)} %collective-permute-done.1.rim_ref, f32[8,128]{1,0:T(8,128)S(1)} %copy-done), custom_call_target="tpu_custom_call" | custom-call | bytes 692224 | tf_op jit(solution)/shard_map/gather/pallas_call | solution.py:83
  81.1 7.8 %all-to-all-start.3 = ((f32[16,8,128]{2,1,0:T(8,128)}), f32[16,8,128]{2,1,0:T(8,128)S(1)}, u32[]{:S(2)}, u32[]{:S(2)}) async-start(f32[16,8,128]{2,1,0:T(8,128)} %bitcast.10), calls=%async_computation.3 | async-start | bytes 131072 | tf_op jit(solution)/shard_map/all_to_all | solution.py:507
  88.8 4.0 %all_gather.15.rims_in = bf16[96,512]{1,0:T(8,128)(2,1)} all-gather(bf16[48,512]{1,0:T(8,128)(2,1)S(1)} %get-tuple-element.28), channel_id=1, replica_groups=mesh['y'=4,'z'=16,'x'=4,'c'=2] {'c'}, dimensions={0}, use_global_device_ids=true | all-gather | bytes 147456 | tf_op jit(solution)/shard_map/all_gather | solution.py:508
  92.8 7.6 %all-to-all-done.3.hub_ref = f32[16,8,128]{2,1,0:T(8,128)S(1)} async-done(((f32[16,8,128]{2,1,0:T(8,128)}), f32[16,8,128]{2,1,0:T(8,128)S(1)}, u32[]{:S(2)}, u32[]{:S(2)}) %all-to-all-start.3) | async-done | bytes 65568 | tf_op jit(solution)/shard_map/all_to_all | solution.py:507
  100.4 0.0 copy-start.2
  100.4 0.6 copy-done.2
  101.0 3.1 %last.1 = bf16[160,512]{1,0:T(8,128)(2,1)} custom-call(f32[16,8,128]{2,1,0:T(8,128)} %copy-done.2, bf16[96,512]{1,0:T(8,128)(2,1)} %all_gather.15.rims_in, f32[160,512]{1,0:T(8,128)} %get-tuple-element.29.base_in, bf16[512,512]{1,0:T(8,128)(2,1)} %ws_in.7), custom_call_target="tpu_custom_call" | custom-call | flops 167772160 | bytes 1179648 | tf_op jit(solution)/shard_map/last/pallas_call | solution.py:83
  (1 shorter events, 0.0 us)
Async XLA Ops:
  2.2 27.3 %all-to-all-start = ((f32[16,8,128]{2,1,0:T(8,128)}), f32[16,8,128]{2,1,0:T(8,128)S(1)}, u32[]{:S(2)}, u32[]{:S(2)}) async-start(f32[16,8,128]{2,1,0:T(8,128)} %get-tuple-element.17), calls=%async_computation | async-start | bytes 131072 | tf_op jit(solution)/shard_map/all_to_all | solution.py:408
  17.9 23.7 %collective-permute-start = (bf16[48,512]{1,0:T(8,128)(2,1)}, bf16[48,512]{1,0:T(8,128)(2,1)S(1)}, u32[]{:S(2)}, u32[]{:S(2)}) collective-permute-start(bf16[48,512]{1,0:T(8,128)(2,1)} %get-tuple-element.18), channel_id=1, source_target_pairs={{0,2},{2,4},{3,1},{4,6},{5,3},{6,8},{7,5},{8,10},{9,7},{10,12},{11... | collective-permute-start | bytes 147464 | tf_op jit(solution)/shard_map/ppermute | solution.py:364
  30.4 17.7 %all-to-all-start.1 = ((bf16[16,32,512]{2,1,0:T(8,128)(2,1)}), bf16[16,32,512]{2,1,0:T(8,128)(2,1)S(1)}, u32[]{:S(2)}, u32[]{:S(2)}) async-start(bf16[16,32,512]{2,1,0:T(8,128)(2,1)} %spread.1), calls=%async_computation.1 | async-start | bytes 1048576 | tf_op jit(solution)/shard_map/all_to_all | solution.py:417
  48.1 0.8 copy-start.1
  61.2 17.7 %all-to-all-start.2 = ((bf16[16,32,512]{2,1,0:T(8,128)(2,1)}), bf16[16,32,512]{2,1,0:T(8,128)(2,1)S(1)}, u32[]{:S(2)}, u32[]{:S(2)}) async-start(bf16[16,32,512]{2,1,0:T(8,128)(2,1)} %bitcast.13), calls=%async_computation.2 | async-start | bytes 1048576 | tf_op jit(solution)/shard_map/all_to_all | solution.py:482
  68.2 8.4 %collective-permute-start.1 = (bf16[48,512]{1,0:T(8,128)(2,1)}, bf16[48,512]{1,0:T(8,128)(2,1)S(1)}, u32[]{:S(2)}, u32[]{:S(2)}) collective-permute-start(bf16[48,512]{1,0:T(8,128)(2,1)} %get-tuple-element.21), channel_id=1, source_target_pairs={{1,3},{2,0},{3,5},{4,2},{5,7},{6,4},{7,9},{8,6},{9,11},{10,8},{11,... | collective-permute-start | bytes 147464 | tf_op jit(solution)/shard_map/ppermute | solution.py:364
  78.9 0.7 copy-start
  81.1 19.3 %all-to-all-start.3 = ((f32[16,8,128]{2,1,0:T(8,128)}), f32[16,8,128]{2,1,0:T(8,128)S(1)}, u32[]{:S(2)}, u32[]{:S(2)}) async-start(f32[16,8,128]{2,1,0:T(8,128)} %bitcast.10), calls=%async_computation.3 | async-start | bytes 131072 | tf_op jit(solution)/shard_map/all_to_all | solution.py:507
  100.4 0.6 copy-start.2

commit v4 on v3

--- a/solution.py
+++ b/solution.py
@@ -17,7 +17,6 @@
 I32 = jnp.int32
 ALL = ("y", "z", "x", "c")
 SPACE = ("y", "z", "x")
-PLANE = ("y", "x")
 LANES = 128
 TILE = 256
 SHAPE = (4, 16, 4)
@@ -112,43 +111,9 @@
     tile = jnp.concatenate(
         [rows[r : r + 1, j * LANES : (j + 1) * LANES] for r in range(HUB_DEV) for j in range(4)],
         axis=0,
-    )
-    for z in range(hub_ref.shape[0]):
-        hub_ref[z] = tile
-    rim.wait()
-
-
-def spread_kernel(rows_ref, out_ref):
-    nz = rows_ref.shape[0] // 8
-    parts = []
-    for r in range(HUB_DEV):
-        lanes = [rows_ref[pl.ds(4 * r + j, nz, stride=8), :] for j in range(4)]
-        parts.append(jnp.concatenate(lanes, axis=1))
-    rows = jnp.concatenate(parts, axis=0).astype(BF)
-    for p in range(out_ref.shape[0]):
-        out_ref[p] = rows
-
-
-def gather_kernel(sums_ref, rim_ref, flag_ref, out_ref, rim_out_ref, buf_ref, sems):
-    del flag_ref
-    planes = sums_ref.shape[0]
-    nz = out_ref.shape[0] // 8
-    quarter = planes // 4
-    pairs = [
-        (sums_ref.at[pl.ds(k * quarter, quarter)], buf_ref.at[pl.ds(k * quarter, quarter)])
-        for k in range(4)
-    ]
-    *copies, rim = start_copies(pairs + [(rim_ref, rim_out_ref)], sems)
-    total = jnp.zeros(buf_ref.shape[1:], F32)
-    for p in range(planes):
-        if p % quarter == 0:
-            copies[p // quarter].wait()
-        total += buf_ref[p].astype(F32)
-    for r in range(HUB_DEV):
-        for j in range(4):
-            out_ref[pl.ds(4 * r + j, nz, stride=8), :] = total[
-                r * nz : (r + 1) * nz, j * LANES : (j + 1) * LANES
-            ]
+    ).astype(BF)
+    for b in range(hub_ref.shape[0]):
+        hub_ref[b] = tile
     rim.wait()
 
 
@@ -159,6 +124,7 @@
 ):
     node_count = nodes_in.shape[0]
     slots = 2 * RIM + node_count
+    tiles = [pl.ds(i * TILE, TILE) for i in range(edges_in.shape[0] // TILE)]
     copies = start_copies(
         [
             (nodes_in, frame_ref.at[pl.ds(RIM, node_count)]),
@@ -167,8 +133,8 @@
             (ws_in, ws_ref),
             (wr_in, wr_ref),
             (we_in, we_ref),
-            (edges_in, edges_ref),
-        ],
+        ]
+        + [(edges_in.at[rows], edges_ref.at[rows]) for rows in tiles],
         sems,
     )
     for copy in copies[:4]:
@@ -177,15 +143,14 @@
     copies[4].wait()
     recv_ref[...] = dot(frame_ref[...], wr_ref[...]).astype(BF)
     copies[5].wait()
-    copies[6].wait()
     back = []
-    for i in range(edges_in.shape[0] // TILE):
-        rows = pl.ds(i * TILE, TILE)
+    for i, rows in enumerate(tiles):
+        copies[6 + i].wait()
         pre = dot(edges_ref[rows, :], we_ref[...])
         pre += dot(hot_rows(ids_ref[0:1, rows], 0, slots), send_ref[...])
         pre += dot(hot_rows(ids_ref[1:2, rows], 0, slots), recv_ref[...])
         pre_ref[rows, :] = pre + bias_ref[...]
-        back += start_copies([(pre_ref.at[rows], pre_out.at[rows])], sems, 7 + i)
+        back += start_copies([(pre_ref.at[rows], pre_out.at[rows])], sems, len(copies) + i)
     for copy in back:
         copy.wait()
 
@@ -196,10 +161,11 @@
     new_ref, dpre_out, hub_sums_out, rim_ref, own_out, gg_out, ndpre_out,
     hubs_ref, pre_ref, edges_ref, nodes_ref, cot_ref, ws_ref, wo_ref, win_ref, wout_ref,
     dpre_ref, hub_sums_ref, gg_ref, ndpre_ref,
-    terms_ref, normed_ref, scale_ref, gathered_ref, high_ref, low_ref, sems,
+    wide_ref, rows_ref, terms_ref, normed_ref, scale_ref, gathered_ref, high_ref, low_ref, sems,
 ):
     node_count, width = nodes_in.shape
-    hub_count = hubs_in.shape[0]
+    blocks = hubs_in.shape[0] // 8
+    hub_count = HUB_DEV * blocks
     edge_count = edges_in.shape[0]
     steps = edge_count // TILE
     slots = 2 * RIM + node_count
@@ -221,15 +187,25 @@
     )
     done = 7 + 2 * steps
     gathered_ref[...] = jnp.zeros_like(gathered_ref)
+    spots = [
+        (
+            pl.ds(4 * r + j, blocks, stride=8),
+            slice(r * blocks, (r + 1) * blocks),
+            slice(j * LANES, (j + 1) * LANES),
+        )
+        for r in range(HUB_DEV)
+        for j in range(4)
+    ]
     hubs.wait()
+    wide_ref[...] = hubs_ref[...].astype(F32)
+    for spot, line, lane in spots:
+        rows_ref[line, lane] = wide_ref[spot, :].astype(BF)
     ws.wait()
-    terms_ref[...] = dot(hubs_ref[...], ws_ref[...]).astype(BF)
+    terms_ref[...] = dot(rows_ref[...], ws_ref[...]).astype(BF)
     wo.wait()
-    for copy in rest:
-        copy.wait()
-
-    def forward(i, carry):
-        rows = pl.ds(pl.multiple_of(i * TILE, TILE), TILE)
+    for i, rows in enumerate(tiles):
+        rest[i].wait()
+        rest[steps + i].wait()
         pre = pre_ref[rows, :] + dot(hot_rows(ids_ref[0:1, rows], slots, hub_count), terms_ref[...])
         gate = jax.nn.sigmoid(pre)
         pre_ref[rows, :] = gate * (1.0 + pre * (1.0 - gate))
@@ -239,9 +215,6 @@
         scale_ref[rows, :] = jnp.broadcast_to(scale, (TILE, LANES))
         new_edges = edges_ref[rows, :].astype(F32) + normed * egain_ref[...] + eshift_ref[...]
         gathered_ref[...] += dot(hot_cols(ids_ref[1:2, rows], 0, slots), new_edges.astype(BF))
-        return carry
-
-    lax.fori_loop(0, steps, forward, 0)
 
     for copy in (nodes, cot, win, wout):
         copy.wait()
@@ -265,19 +238,18 @@
         ref[...] = jnp.zeros_like(ref)
         ref[own] = part
 
-    def backward(i, carry):
-        rows = pl.ds(pl.multiple_of(i * TILE, TILE), TILE)
+    for rows in tiles:
         hot = hot_rows(ids_ref[1:2, rows], 0, slots)
         upstream = dot(hot, high_ref[...]) + dot(hot, low_ref[...])
         dsum = norm_back(upstream, normed_ref[rows, :], scale_ref[rows, :1], egain_ref[...])
         dpre_ref[rows, :] = (dot_t(dsum.astype(BF), wo_ref[...]) * pre_ref[rows, :]).astype(BF)
-        return carry
-
-    lax.fori_loop(0, steps, backward, 0)
 
     back += start_copies([(dpre_ref, dpre_out)], sems, done + 2)
     dpre = dpre_ref[...]
-    hub_sums_ref[...] = dot(hot_cols(ids_ref[0:1, :], slots, hub_count), dpre).astype(BF)
+    hub_sums = dot(hot_cols(ids_ref[0:1, :], slots, hub_count), dpre)
+    for spot, line, lane in spots:
+        wide_ref[spot, :] = hub_sums[line, lane]
+    hub_sums_ref[...] = wide_ref[...].astype(BF)
     back += start_copies([(hub_sums_ref, hub_sums_out)], sems, done + 3)
     gathered_ref[...] = dot(hot_cols(ids_ref[0:1, :], 0, slots), dpre)
     back += start_copies([(gathered_ref.at[pl.ds(RIM, node_count)], own_out)], sems, done + 4)
@@ -289,7 +261,7 @@
 
 def late_kernel(
     core_ref, dpre_in, ids_ref, gg_in, ndpre_in, own_in, cot_in, we_in, ws_in, wr_in, win_in,
-    egrad_ref, base_ref, flag_ref,
+    egrad_ref, base_ref,
     dpre_ref, gg_ref, ndpre_ref, own_ref, cot_ref, we_ref, ws_ref, wr_ref, win_ref,
     high_ref, low_ref, sems,
 ):
@@ -327,29 +299,32 @@
         high, low = split2(sums)
         base += dot_t(high, weight[...]) + dot_t(low, weight[...])
     base_ref[...] = base
-    flag_ref[...] = jnp.zeros_like(flag_ref)
-
-
-def last_kernel(hub_ref, rims_in, base_in, ws_in, out_ref, rims_ref, base_ref, ws_ref, sums_ref, sems):
+
+
+def last_kernel(
+    hub_in, rims_in, base_in, ws_in, out_ref, hub_ref, rims_ref, base_ref, ws_ref, sums_ref, sems
+):
     node_count = base_in.shape[0]
-    copies = start_copies([(rims_in, rims_ref), (ws_in, ws_ref), (base_in, base_ref)], sems)
-    hub = hub_ref[0]
-    for z in range(1, hub_ref.shape[0]):
-        hub += hub_ref[z]
+    copies = start_copies(
+        [(hub_in, hub_ref), (rims_in, rims_ref), (ws_in, ws_ref), (base_in, base_ref)], sems
+    )
+    blocks = hub_ref.shape[0] // 8
+    sums_ref[...] = jnp.zeros_like(sums_ref)
+    copies[0].wait()
+    hub = hub_ref[...].astype(F32).reshape(blocks, 8, LANES).sum(0)
     rows = [
         jnp.concatenate([hub[4 * r + j : 4 * r + j + 1] for j in range(4)], axis=1)
         for r in range(HUB_DEV)
     ]
-    sums_ref[...] = jnp.zeros_like(sums_ref)
-    copies[0].wait()
+    copies[1].wait()
     sums_ref[:RIM] = rims_ref[RIM:].astype(F32)
     for r in range(HUB_DEV):
         sums_ref[r : r + 1] += rows[r]
     sums_ref[node_count - RIM :] += rims_ref[:RIM].astype(F32)
     high, low = split2(sums_ref[...])
-    copies[1].wait()
+    copies[2].wait()
     extra = dot_t(high, ws_ref[...]) + dot_t(low, ws_ref[...])
-    copies[2].wait()
+    copies[3].wait()
     out_ref[...] = (base_ref[...] + extra).astype(BF)
 
 
@@ -387,9 +362,8 @@
     half = edges.shape[0]
     edge_count = 2 * half
     steps = edge_count // TILE
-    ny, nz, nx = (lax.axis_size(a) for a in SPACE)
-    plane = ny * nx
-    hub_count = plane * HUB_DEV * nz
+    blocks = math.prod(lax.axis_size(a) for a in SPACE)
+    hub_count = HUB_DEV * blocks
     slots = 2 * RIM + node_count
     core = lax.axis_index("c").astype(I32)
     own_block = lax.axis_index(SPACE)
@@ -400,30 +374,19 @@
     my_hub, my_rim = call(
         prep_kernel,
         [(core.reshape(1), SM), (nodes, HB)],
-        [((nz, 8, LANES), F32, VM), ((RIM, width), BF, VM)],
+        [((blocks, 8, LANES), BF, VM), ((RIM, width), BF, VM)],
         [wide(16)],
         copies=2,
         name="prep",
     )
-    by_z = lax.all_to_all(my_hub, "z", 0, 0)
+    hubs = lax.all_to_all(my_hub, SPACE, 0, 0).reshape(blocks * 8, LANES)
     rim = both_ways(my_rim, 1)
-    (spread,) = call(
-        spread_kernel,
-        [(by_z.reshape(nz * 8, LANES), VM)],
-        [((plane, HUB_DEV * nz, width), BF, VM)],
-        room=54000,
-        name="spread",
-    )
-    hubs = lax.all_to_all(spread, PLANE, 0, 0).reshape(hub_count, width)
 
     rims = lax.all_gather(rim, "c", axis=0, tiled=True)
     all_edges = lax.all_gather(edges, "c", axis=0, tiled=True)
     ids = lax.all_gather(jnp.stack([senders, receivers]), "c", axis=1, tiled=True)
     block = ids[0] // node_count
     line = ids[0] - block * node_count
-    hub_y, hub_zx = block // (nz * nx), block % (nz * nx)
-    hub_z, hub_x = hub_zx // nx, hub_zx % nx
-    hub_slot = ((hub_y * nx + hub_x) * HUB_DEV + line) * nz + hub_z
     slot = jnp.where(
         block == own_block,
         RIM + line,
@@ -433,7 +396,7 @@
             jnp.where(
                 (block == own_block + 1) & (line < RIM),
                 RIM + node_count + line,
-                slots + hub_slot,
+                slots + line * blocks + block,
             ),
         ),
     )
@@ -448,7 +411,7 @@
         [((edge_count, width), F32, HB)],
         [wide(edge_count)] + [wide(slots)] + [wide(width)] * 3 + [wide(slots)] * 2
         + [wide(edge_count, F32)],
-        copies=7 + steps,
+        copies=6 + 2 * steps,
         flops=square * (edge_count * 2 + 2 * slots),
         name="near",
     )
@@ -462,15 +425,16 @@
         [
             ((node_count, width), BF, VM),
             ((edge_count, width), BF, HB),
-            ((hub_count, width), BF, HB),
+            ((blocks * 8, LANES), BF, HB),
             ((RIM, width), BF, VM),
             ((node_count, width), F32, HB),
             ((node_count, width), F32, HB),
             ((node_count, width), BF, HB),
         ],
-        [wide(hub_count), wide(edge_count, F32), wide(edge_count)]
+        [pltpu.VMEM((blocks * 8, LANES), BF), wide(edge_count, F32), wide(edge_count)]
         + [wide(node_count)] * 2 + [wide(width)] * 2 + [wide(2 * width), wide(width)]
-        + [wide(edge_count), wide(hub_count), wide(node_count, F32), wide(node_count)]
+        + [wide(edge_count), pltpu.VMEM((blocks * 8, LANES), BF), wide(node_count, F32)]
+        + [wide(node_count), pltpu.VMEM((blocks * 8, LANES), F32), wide(hub_count)]
         + [wide(hub_count), wide(edge_count, F32), pltpu.VMEM((edge_count, LANES), F32)]
         + [wide(slots, F32), wide(slots), wide(slots)],
         copies=12 + 2 * steps,
@@ -479,39 +443,31 @@
         name="main",
     )
 
-    hub_back = lax.all_to_all(hub_sums.reshape(plane, HUB_DEV * nz, width), PLANE, 0, 0)
+    hub_back = lax.all_to_all(hub_sums.reshape(blocks, 8, LANES), SPACE, 0, 0)
+    hub_back = hub_back.reshape(blocks * 8, LANES)
     rim = both_ways(my_rim, -1)
-    edge_grad, base, flag = call(
+    edge_grad, base = call(
         late_kernel,
         [
             (core.reshape(1), SM), (dpre, HB), (ids, VM), (gathered_grad, HB), (node_dpre, HB),
             (own_sums, HB), (node_cot, HB), (edge_proj, HB), (send_proj, HB), (recv_proj, HB),
             (node_in, HB),
         ],
-        [((half, width), BF, VM), ((node_count, width), F32, VM), ((8, LANES), F32, VM)],
+        [((half, width), BF, VM), ((node_count, width), F32, VM)],
         [wide(edge_count), wide(node_count, F32), wide(node_count), wide(node_count, F32)]
         + [wide(node_count)] + [wide(width)] * 4 + [wide(slots)] * 2,
         copies=9,
         flops=square * edge_count * 2,
         name="late",
     )
-    by_z, rim = call(
-        gather_kernel,
-        [(hub_back, HB), (rim, HB), (flag, HB)],
-        [((nz * 8, LANES), F32, VM), ((RIM, width), BF, VM)],
-        [pltpu.VMEM((plane, HUB_DEV * nz, width), BF)],
-        copies=5,
-        room=54000,
-        name="gather",
-    )
-    hub_back = lax.all_to_all(by_z.reshape(nz, 8, LANES), "z", 0, 0)
     rims = lax.all_gather(rim, "c", axis=0, tiled=True)
     (node_grad,) = call(
         last_kernel,
-        [(hub_back, VM), (rims, HB), (base, HB), (send_proj, HB)],
+        [(hub_back, HB), (rims, HB), (base, HB), (send_proj, HB)],
         [((node_count, width), BF, VM)],
-        [wide(2 * RIM), wide(node_count, F32), wide(width), wide(node_count, F32)],
-        copies=3,
+        [pltpu.VMEM((blocks * 8, LANES), BF), wide(2 * RIM), wide(node_count, F32), wide(width)]
+        + [wide(node_count, F32)],
+        copies=4,
         flops=square * node_count * 2,
         room=0,
         name="last",

time: 106 us -> 129 us (1.22)
  waiting for transfers between devices: 11.9 us -> 42.1 us
  blocking collectives: 16.7 us -> 11.5 us
  Pallas kernels: 28.8 us -> 25.6 us
  starting transfers between devices: 41.8 us -> 44.1 us
    all_to_all x4 -> x2, waiting for transfers between devices: 11.9 us -> 42.1 us  [the longest x1 25.8 us: body(): hub_back = lax.all_to_all(hub_sums.reshape(blocks, 8, LANES), SPACE, 0, 0)]
    all_to_all x4 -> x2, starting transfers between devices: 37.2 us -> 41.2 us  [the longest x1 25.3 us: body(): hubs = lax.all_to_all(my_hub, SPACE, 0, 0).reshape(blocks * 8, LANES)]
    pallas_call x7 -> x5, Pallas kernels: 28.8 us -> 25.6 us  [call(): pl.pallas_call(kernel, out_shape=shapes, in_specs=[spec for _, spec in in...]
    all_gather x1, blocking collectives: 6.92 us -> 4.25 us  [body(): all_edges = lax.all_gather(edges, 'c', axis=0, tiled=True)]
    all_gather x2, blocking collectives: 5.98 us -> 4.01 us  [body(): rims = lax.all_gather(rim, 'c', axis=0, tiled=True)]
    ppermute x2, starting transfers between devices: 4.55 us -> 2.89 us  [both_ways(): return lax.ppermute(x, ALL, pairs)]
  transfers between devices with their start and end apart: 6 -> 4, of which waited for: 3 -> 2; matrix products, arithmetic and copies ran while one was open for 2% -> 2% of each run, Pallas kernels for 10% -> 8%
where the time goes in v4:
time: 129 us; the launch traced here: 128 us
  starting transfers between devices  44.1 us (34%)
  waiting for transfers between devices  42.1 us (33%)
  Pallas kernels  25.6 us (20%)
  blocking collectives  11.5 us (9%)
  local copies, waits for them, and re-layouts  2.95 us (2%)
    all_to_all x1, waiting for transfers between devices, body(): hub_back = lax.all_to_all(hub_sums.reshape(blocks, 8, LANES), SPACE, 0, 0)  25.8 us
    pallas_call x5, Pallas kernels, call(): pl.pallas_call(kernel, out_shape=shapes, in_specs=[spec for _, spec in in...  25.6 us
    all_to_all x1, starting transfers between devices, body(): hubs = lax.all_to_all(my_hub, SPACE, 0, 0).reshape(blocks * 8, LANES)  25.3 us
    all_to_all x1, waiting for transfers between devices, body(): hubs = lax.all_to_all(my_hub, SPACE, 0, 0).reshape(blocks * 8, LANES)  16.4 us
    all_to_all x1, starting transfers between devices, body(): hub_back = lax.all_to_all(hub_sums.reshape(blocks, 8, LANES), SPACE, 0, 0)  15.8 us
    all_gather x1, blocking collectives, body(): all_edges = lax.all_gather(edges, 'c', axis=0, tiled=True)  4.25 us
    all_gather x2, blocking collectives, body(): rims = lax.all_gather(rim, 'c', axis=0, tiled=True)  4.01 us
    all_gather x1, blocking collectives, body(): lax.all_gather(jnp.stack([senders, receivers]), 'c', axis=1, tiled=True)  3.24 us
  transfers between devices with their start and end apart: 4, of which 2 were waited for; matrix products, arithmetic and copies ran while one was open for 2% of the time, Pallas kernels for 8%

profile of v4, /device:TPU:1, one launch (start us, length us, event | category | flops | bytes accessed | tf_op | source)
XLA Modules:
  0.0 127.7 jit_solution(14197649778567090531)
XLA Ops:
  0.6 1.7 %prep.1 = (bf16[256,8,128]{2,1,0:T(8,128)(2,1)}, bf16[48,512]{1,0:T(8,128)(2,1)}) custom-call(s32[1]{0:T(128)} %bitcast.core_ref, bf16[160,512]{1,0:T(8,128)(2,1)} %nodes_in.3), custom_call_target="tpu_custom_call" | custom-call | bytes 737284 | tf_op jit(solution)/shard_map/prep/pallas_call | solution.py:82
  2.3 25.3 %all-to-all-start = ((bf16[256,8,128]{2,1,0:T(8,128)(2,1)}), bf16[256,8,128]{2,1,0:T(8,128)(2,1)S(1)}, u32[]{:S(2)}, u32[]{:S(2)}) async-start(bf16[256,8,128]{2,1,0:T(8,128)(2,1)} %get-tuple-element.14), calls=%async_computation | async-start | bytes 1048576 | tf_op jit(solution)/shard_map/all_to_all | solution.py:382
  27.7 1.3 %collective-permute-start = (bf16[48,512]{1,0:T(8,128)(2,1)}, bf16[48,512]{1,0:T(8,128)(2,1)S(1)}, u32[]{:S(2)}, u32[]{:S(2)}) collective-permute-start(bf16[48,512]{1,0:T(8,128)(2,1)} %get-tuple-element.15), channel_id=1, source_target_pairs={{0,2},{2,4},{3,1},{4,6},{5,3},{6,8},{7,5},{8,10},{9,7},{10,12},{11... | collective-permute-start | bytes 147464 | tf_op jit(solution)/shard_map/ppermute | solution.py:339
  29.0 0.7 stack.14
  29.7 0.7 stack.15
  30.4 3.2 %all_gather.13 = s32[2,768]{1,0:T(2,128)S(1)} all-gather(s32[2,384]{1,0:T(2,128)S(1)} %pad_add_fusion.1), channel_id=1, replica_groups=mesh['y'=4,'z'=16,'x'=4,'c'=2] {'c'}, dimensions={1}, use_global_device_ids=true | all-gather | bytes 9216 | tf_op jit(solution)/shard_map/all_gather | solution.py:387
  33.6 4.2 %all_gather.12.edges_in = bf16[768,512]{1,0:T(8,128)(2,1)} all-gather(bf16[384,512]{1,0:T(8,128)(2,1)} %param.18), channel_id=1, replica_groups=mesh['y'=4,'z'=16,'x'=4,'c'=2] {'c'}, dimensions={0}, use_global_device_ids=true | all-gather | bytes 1179648 | tf_op jit(solution)/shard_map/all_gather | solution.py:386
  37.9 0.6 pad_add_fusion.ids_ref
  38.5 0.0 collective-permute-done
  38.5 2.0 %all_gather.14.rims_in = bf16[96,512]{1,0:T(8,128)(2,1)} all-gather(bf16[48,512]{1,0:T(8,128)(2,1)S(1)} %collective-permute-done), channel_id=1, replica_groups=mesh['y'=4,'z'=16,'x'=4,'c'=2] {'c'}, dimensions={0}, use_global_device_ids=true | all-gather | bytes 147456 | tf_op jit(solution)/shard_map/all_gather | solution.py:385
  40.5 4.9 %near.1.pre_in = f32[768,512]{1,0:T(8,128)} custom-call(bf16[768,512]{1,0:T(8,128)(2,1)} %all_gather.12.edges_in, s32[2,768]{1,0:T(2,128)} %pad_add_fusion.ids_ref, bf16[160,512]{1,0:T(8,128)(2,1)} %nodes_in.3, bf16[96,512]{1,0:T(8,128)(2,1)} %all_gather.14.rims_in, bf16[512,512]{1,0:T(8,128)(2,1)} %we_in.3, bf16[512,512]{1,0:T(8,128)(2,1)} %ws_in.7, ...), custom_call_target="tpu_custom_call" | custom-call | flops 1073741824 | bytes 4202496 | tf_op jit(solution)/shard_map/near/pallas_call | solution.py:82
  45.4 16.4 %all-to-all-done = bf16[256,8,128]{2,1,0:T(8,128)(2,1)S(1)} async-done(((bf16[256,8,128]{2,1,0:T(8,128)(2,1)}), bf16[256,8,128]{2,1,0:T(8,128)(2,1)S(1)}, u32[]{:S(2)}, u32[]{:S(2)}) %all-to-all-start) | async-done | bytes 524320 | tf_op jit(solution)/shard_map/all_to_all | solution.py:382
  61.8 0.0 copy-start.1
  61.8 0.8 copy-done.1
  62.6 11.3 %main.1 = (bf16[160,512]{1,0:T(8,128)(2,1)}, bf16[768,512]{1,0:T(8,128)(2,1)}, bf16[2048,128]{1,0:T(8,128)(2,1)}, bf16[48,512]{1,0:T(8,128)(2,1)}, f32[160,512]{...) custom-call(s32[1]{0:T(128)} %bitcast.core_ref, bf16[2048,128]{1,0:T(8,128)(2,1)} %bitcast.11, ...), custom_call_target="tpu_custom_call" | custom-call | flops 2684354560 | bytes 8192004 | tf_op jit(solution)/shard_map/main/pallas_call | solution.py:82
  73.8 15.8 %all-to-all-start.1 = ((bf16[256,8,128]{2,1,0:T(8,128)(2,1)}), bf16[256,8,128]{2,1,0:T(8,128)(2,1)S(1)}, u32[]{:S(2)}, u32[]{:S(2)}) async-start(bf16[256,8,128]{2,1,0:T(8,128)(2,1)} %bitcast.12), calls=%async_computation.1 | async-start | bytes 1048576 | tf_op jit(solution)/shard_map/all_to_all | solution.py:446
  89.7 1.6 %collective-permute-start.1 = (bf16[48,512]{1,0:T(8,128)(2,1)}, bf16[48,512]{1,0:T(8,128)(2,1)S(1)}, u32[]{:S(2)}, u32[]{:S(2)}) collective-permute-start(bf16[48,512]{1,0:T(8,128)(2,1)} %get-tuple-element.18), channel_id=1, source_target_pairs={{1,3},{2,0},{3,5},{4,2},{5,7},{6,4},{7,9},{8,6},{9,11},{10,8},{11,... | collective-permute-start | bytes 147464 | tf_op jit(solution)/shard_map/ppermute | solution.py:339
  91.3 5.1 %late.1 = (bf16[384,512]{1,0:T(8,128)(2,1)}, f32[160,512]{1,0:T(8,128)}) custom-call(s32[1]{0:T(128)} %bitcast.core_ref, bf16[768,512]{1,0:T(8,128)(2,1)} %get-tuple-element.19.dpre_in, s32[2,768]{1,0:T(2,128)} %pad_add_fusion.ids_ref, f32[160,512]{1,0:T(8,128)} %get-tuple-element.20.gg_in, bf16[160,512]{1,0:T(8,128)(2,1)} %get-tuple-element.21.ndpre_in, ...), custom_call_target="tpu_custom_call" | custom-call | flops 805306368 | bytes 5117956 | tf_op jit(solution)/shard_map/late/pallas_call | solution.py:82
  96.4 0.0 collective-permute-done.1
  96.4 2.0 %all_gather.15.rims_in = bf16[96,512]{1,0:T(8,128)(2,1)} all-gather(bf16[48,512]{1,0:T(8,128)(2,1)S(1)} %collective-permute-done.1), channel_id=1, replica_groups=mesh['y'=4,'z'=16,'x'=4,'c'=2] {'c'}, dimensions={0}, use_global_device_ids=true | all-gather | bytes 147456 | tf_op jit(solution)/shard_map/all_gather | solution.py:463
  98.4 25.8 %all-to-all-done.1 = bf16[256,8,128]{2,1,0:T(8,128)(2,1)S(1)} async-done(((bf16[256,8,128]{2,1,0:T(8,128)(2,1)}), bf16[256,8,128]{2,1,0:T(8,128)(2,1)S(1)}, u32[]{:S(2)}, u32[]{:S(2)}) %all-to-all-start.1) | async-done | bytes 524320 | tf_op jit(solution)/shard_map/all_to_all | solution.py:446
  124.2 0.0 copy-start
  124.2 0.8 copy-done
  125.0 2.6 %last.1 = bf16[160,512]{1,0:T(8,128)(2,1)} custom-call(bf16[2048,128]{1,0:T(8,128)(2,1)} %bitcast.10, bf16[96,512]{1,0:T(8,128)(2,1)} %all_gather.15.rims_in, f32[160,512]{1,0:T(8,128)} %get-tuple-element.23.base_in, bf16[512,512]{1,0:T(8,128)(2,1)} %ws_in.7), custom_call_target="tpu_custom_call" | custom-call | flops 167772160 | bytes 1638400 | tf_op jit(solution)/shard_map/last/pallas_call | solution.py:82
  (2 shorter events, 0.1 us)
Async XLA Ops:
  2.3 59.4 %all-to-all-start = ((bf16[256,8,128]{2,1,0:T(8,128)(2,1)}), bf16[256,8,128]{2,1,0:T(8,128)(2,1)S(1)}, u32[]{:S(2)}, u32[]{:S(2)}) async-start(bf16[256,8,128]{2,1,0:T(8,128)(2,1)} %get-tuple-element.14), calls=%async_computation | async-start | bytes 1048576 | tf_op jit(solution)/shard_map/all_to_all | solution.py:382
  27.7 10.8 %collective-permute-start = (bf16[48,512]{1,0:T(8,128)(2,1)}, bf16[48,512]{1,0:T(8,128)(2,1)S(1)}, u32[]{:S(2)}, u32[]{:S(2)}) collective-permute-start(bf16[48,512]{1,0:T(8,128)(2,1)} %get-tuple-element.15), channel_id=1, source_target_pairs={{0,2},{2,4},{3,1},{4,6},{5,3},{6,8},{7,5},{8,10},{9,7},{10,12},{11... | collective-permute-start | bytes 147464 | tf_op jit(solution)/shard_map/ppermute | solution.py:339
  61.8 0.8 copy-start.1
  73.8 50.4 %all-to-all-start.1 = ((bf16[256,8,128]{2,1,0:T(8,128)(2,1)}), bf16[256,8,128]{2,1,0:T(8,128)(2,1)S(1)}, u32[]{:S(2)}, u32[]{:S(2)}) async-start(bf16[256,8,128]{2,1,0:T(8,128)(2,1)} %bitcast.12), calls=%async_computation.1 | async-start | bytes 1048576 | tf_op jit(solution)/shard_map/all_to_all | solution.py:446
  89.7 6.7 %collective-permute-start.1 = (bf16[48,512]{1,0:T(8,128)(2,1)}, bf16[48,512]{1,0:T(8,128)(2,1)S(1)}, u32[]{:S(2)}, u32[]{:S(2)}) collective-permute-start(bf16[48,512]{1,0:T(8,128)(2,1)} %get-tuple-element.18), channel_id=1, source_target_pairs={{1,3},{2,0},{3,5},{4,2},{5,7},{6,4},{7,9},{8,6},{9,11},{10,8},{11,... | collective-permute-start | bytes 147464 | tf_op jit(solution)/shard_map/ppermute | solution.py:339
  124.2 0.8 copy-start

commit v5 on v3

--- a/solution.py
+++ b/solution.py
@@ -1,4 +1,3 @@
-import functools
 import math
 
 import jax
@@ -37,6 +36,11 @@
     return high, (v - high.astype(F32)).astype(BF)
 
 
+def times(sums, weight_ref):
+    high, low = split2(sums)
+    return (dot_t(high, weight_ref[...]) + dot_t(low, weight_ref[...])).astype(BF)
+
+
 def row_mean(v):
     return jnp.mean(v, axis=-1, keepdims=True)
 
@@ -73,7 +77,7 @@
 HB = pl.BlockSpec(memory_space=pltpu.HBM)
 
 
-def call(kernel, ins, outs, scratch=(), copies=0, flops=0, room=0, name=None):
+def call(kernel, ins, outs, scratch=(), copies=0, flops=0, room=0):
     shapes = [jax.ShapeDtypeStruct(s, d) for s, d, _ in outs]
     args = [a for a, _ in ins]
     moved = sum(math.prod(o.shape) * o.dtype.itemsize for o in shapes + args)
@@ -88,8 +92,15 @@
         scratch_shapes=scratch,
         compiler_params=pltpu.CompilerParams(vmem_limit_bytes=GRANT - room * 1024),
         cost_estimate=pl.CostEstimate(flops=flops, bytes_accessed=moved, transcendentals=0),
-        name=name,
     )(*args)
+
+
+def edge_pairs(core_ref, own_in, other_in, edges_ref):
+    half = own_in.shape[0]
+    return [
+        (src, edges_ref.at[pl.ds(pl.multiple_of(at * half, half), half)])
+        for src, at in ((own_in, core_ref[0]), (other_in, 1 - core_ref[0]))
+    ]
 
 
 def start_copies(pairs, sems, first=0):
@@ -129,8 +140,7 @@
         out_ref[p] = rows
 
 
-def gather_kernel(sums_ref, rim_ref, flag_ref, out_ref, rim_out_ref, buf_ref, sems):
-    del flag_ref
+def gather_kernel(sums_ref, out_ref, buf_ref, sems):
     planes = sums_ref.shape[0]
     nz = out_ref.shape[0] // 8
     quarter = planes // 4
@@ -138,7 +148,7 @@
         (sums_ref.at[pl.ds(k * quarter, quarter)], buf_ref.at[pl.ds(k * quarter, quarter)])
         for k in range(4)
     ]
-    *copies, rim = start_copies(pairs + [(rim_ref, rim_out_ref)], sems)
+    copies = start_copies(pairs, sems)
     total = jnp.zeros(buf_ref.shape[1:], F32)
     for p in range(planes):
         if p % quarter == 0:
@@ -149,11 +159,10 @@
             out_ref[pl.ds(4 * r + j, nz, stride=8), :] = total[
                 r * nz : (r + 1) * nz, j * LANES : (j + 1) * LANES
             ]
-    rim.wait()
 
 
 def near_kernel(
-    edges_in, ids_ref, nodes_in, rims_in, we_in, ws_in, wr_in, bias_ref,
+    core_ref, own_in, other_in, ids_ref, nodes_in, rims_in, we_in, ws_in, wr_in, bias_ref,
     pre_out,
     edges_ref, frame_ref, we_ref, ws_ref, wr_ref, send_ref, recv_ref, pre_ref, sems,
 ):
@@ -167,8 +176,8 @@
             (ws_in, ws_ref),
             (wr_in, wr_ref),
             (we_in, we_ref),
-            (edges_in, edges_ref),
-        ],
+        ]
+        + edge_pairs(core_ref, own_in, other_in, edges_ref),
         sems,
     )
     for copy in copies[:4]:
@@ -176,22 +185,22 @@
     send_ref[...] = dot(frame_ref[...], ws_ref[...]).astype(BF)
     copies[4].wait()
     recv_ref[...] = dot(frame_ref[...], wr_ref[...]).astype(BF)
-    copies[5].wait()
-    copies[6].wait()
+    for copy in copies[5:]:
+        copy.wait()
     back = []
-    for i in range(edges_in.shape[0] // TILE):
+    for i in range(edges_ref.shape[0] // TILE):
         rows = pl.ds(i * TILE, TILE)
         pre = dot(edges_ref[rows, :], we_ref[...])
         pre += dot(hot_rows(ids_ref[0:1, rows], 0, slots), send_ref[...])
         pre += dot(hot_rows(ids_ref[1:2, rows], 0, slots), recv_ref[...])
         pre_ref[rows, :] = pre + bias_ref[...]
-        back += start_copies([(pre_ref.at[rows], pre_out.at[rows])], sems, 7 + i)
+        back += start_copies([(pre_ref.at[rows], pre_out.at[rows])], sems, len(copies) + i)
     for copy in back:
         copy.wait()
 
 
 def main_kernel(
-    core_ref, hubs_in, pre_in, edges_in, ids_ref, nodes_in, cot_in, ws_in, wo_in, win_in, wout_in,
+    core_ref, hubs_in, pre_in, own_in, other_in, ids_ref, nodes_in, cot_in, ws_in, wo_in, win_in, wout_in,
     egain_ref, eshift_ref, nbias_ref, ngain_ref, nshift_ref,
     new_ref, dpre_out, hub_sums_out, rim_ref, own_out, gg_out, ndpre_out,
     hubs_ref, pre_ref, edges_ref, nodes_ref, cot_ref, ws_ref, wo_ref, win_ref, wout_ref,
@@ -200,36 +209,29 @@
 ):
     node_count, width = nodes_in.shape
     hub_count = hubs_in.shape[0]
-    edge_count = edges_in.shape[0]
+    edge_count = edges_ref.shape[0]
     steps = edge_count // TILE
     slots = 2 * RIM + node_count
     own = slice(RIM, RIM + node_count)
     tiles = [pl.ds(i * TILE, TILE) for i in range(steps)]
-    hubs, ws, wo, nodes, cot, win, wout, *rest = start_copies(
-        [
-            (hubs_in, hubs_ref),
-            (ws_in, ws_ref),
-            (wo_in, wo_ref),
-            (nodes_in, nodes_ref),
-            (cot_in, cot_ref),
-            (win_in, win_ref),
-            (wout_in, wout_ref),
-        ]
+    hubs, ws, wo, *rest = start_copies(
+        [(hubs_in, hubs_ref), (ws_in, ws_ref), (wo_in, wo_ref)]
         + [(pre_in.at[rows], pre_ref.at[rows]) for rows in tiles]
-        + [(edges_in.at[rows], edges_ref.at[rows]) for rows in tiles],
+        + edge_pairs(core_ref, own_in, other_in, edges_ref)
+        + [(nodes_in, nodes_ref), (cot_in, cot_ref), (win_in, win_ref), (wout_in, wout_ref)],
         sems,
     )
-    done = 7 + 2 * steps
+    done = 3 + len(rest)
     gathered_ref[...] = jnp.zeros_like(gathered_ref)
     hubs.wait()
     ws.wait()
     terms_ref[...] = dot(hubs_ref[...], ws_ref[...]).astype(BF)
-    wo.wait()
-    for copy in rest:
-        copy.wait()
-
-    def forward(i, carry):
-        rows = pl.ds(pl.multiple_of(i * TILE, TILE), TILE)
+    for i, rows in enumerate(tiles):
+        rest[i].wait()
+        if i == 0:
+            wo.wait()
+            rest[steps].wait()
+            rest[steps + 1].wait()
         pre = pre_ref[rows, :] + dot(hot_rows(ids_ref[0:1, rows], slots, hub_count), terms_ref[...])
         gate = jax.nn.sigmoid(pre)
         pre_ref[rows, :] = gate * (1.0 + pre * (1.0 - gate))
@@ -239,11 +241,8 @@
         scale_ref[rows, :] = jnp.broadcast_to(scale, (TILE, LANES))
         new_edges = edges_ref[rows, :].astype(F32) + normed * egain_ref[...] + eshift_ref[...]
         gathered_ref[...] += dot(hot_cols(ids_ref[1:2, rows], 0, slots), new_edges.astype(BF))
-        return carry
-
-    lax.fori_loop(0, steps, forward, 0)
-
-    for copy in (nodes, cot, win, wout):
+
+    for copy in rest[steps + 2 :]:
         copy.wait()
     nodes = nodes_ref[...]
     gathered = gathered_ref[own].astype(BF)
@@ -265,31 +264,27 @@
         ref[...] = jnp.zeros_like(ref)
         ref[own] = part
 
-    def backward(i, carry):
-        rows = pl.ds(pl.multiple_of(i * TILE, TILE), TILE)
+    for rows in tiles:
         hot = hot_rows(ids_ref[1:2, rows], 0, slots)
         upstream = dot(hot, high_ref[...]) + dot(hot, low_ref[...])
         dsum = norm_back(upstream, normed_ref[rows, :], scale_ref[rows, :1], egain_ref[...])
         dpre_ref[rows, :] = (dot_t(dsum.astype(BF), wo_ref[...]) * pre_ref[rows, :]).astype(BF)
-        return carry
-
-    lax.fori_loop(0, steps, backward, 0)
 
     back += start_copies([(dpre_ref, dpre_out)], sems, done + 2)
     dpre = dpre_ref[...]
-    hub_sums_ref[...] = dot(hot_cols(ids_ref[0:1, :], slots, hub_count), dpre).astype(BF)
+    hub_sums_ref[...] = times(dot(hot_cols(ids_ref[0:1, :], slots, hub_count), dpre), ws_ref)
     back += start_copies([(hub_sums_ref, hub_sums_out)], sems, done + 3)
     gathered_ref[...] = dot(hot_cols(ids_ref[0:1, :], 0, slots), dpre)
     back += start_copies([(gathered_ref.at[pl.ds(RIM, node_count)], own_out)], sems, done + 4)
     start = pl.multiple_of(core_ref[0] * (RIM + node_count), 16)
-    rim_ref[...] = gathered_ref[pl.ds(start, RIM), :].astype(BF)
+    rim_ref[...] = times(gathered_ref[pl.ds(start, RIM), :], ws_ref)
     for copy in back:
         copy.wait()
 
 
 def late_kernel(
     core_ref, dpre_in, ids_ref, gg_in, ndpre_in, own_in, cot_in, we_in, ws_in, wr_in, win_in,
-    egrad_ref, base_ref, flag_ref,
+    egrad_ref, base_ref,
     dpre_ref, gg_ref, ndpre_ref, own_ref, cot_ref, we_ref, ws_ref, wr_ref, win_ref,
     high_ref, low_ref, sems,
 ):
@@ -327,30 +322,23 @@
         high, low = split2(sums)
         base += dot_t(high, weight[...]) + dot_t(low, weight[...])
     base_ref[...] = base
-    flag_ref[...] = jnp.zeros_like(flag_ref)
-
-
-def last_kernel(hub_ref, rims_in, base_in, ws_in, out_ref, rims_ref, base_ref, ws_ref, sums_ref, sems):
+
+
+def last_kernel(hub_ref, rims_in, base_in, out_ref, rims_ref, base_ref, sems):
     node_count = base_in.shape[0]
-    copies = start_copies([(rims_in, rims_ref), (ws_in, ws_ref), (base_in, base_ref)], sems)
+    copies = start_copies([(rims_in, rims_ref), (base_in, base_ref)], sems)
     hub = hub_ref[0]
     for z in range(1, hub_ref.shape[0]):
         hub += hub_ref[z]
-    rows = [
-        jnp.concatenate([hub[4 * r + j : 4 * r + j + 1] for j in range(4)], axis=1)
-        for r in range(HUB_DEV)
-    ]
-    sums_ref[...] = jnp.zeros_like(sums_ref)
-    copies[0].wait()
-    sums_ref[:RIM] = rims_ref[RIM:].astype(F32)
+    for copy in copies:
+        copy.wait()
+    base_ref[:RIM] += rims_ref[RIM:].astype(F32)
+    base_ref[node_count - RIM :] += rims_ref[:RIM].astype(F32)
     for r in range(HUB_DEV):
-        sums_ref[r : r + 1] += rows[r]
-    sums_ref[node_count - RIM :] += rims_ref[:RIM].astype(F32)
-    high, low = split2(sums_ref[...])
-    copies[1].wait()
-    extra = dot_t(high, ws_ref[...]) + dot_t(low, ws_ref[...])
-    copies[2].wait()
-    out_ref[...] = (base_ref[...] + extra).astype(BF)
+        base_ref[r : r + 1] += jnp.concatenate(
+            [hub[4 * r + j : 4 * r + j + 1] for j in range(4)], axis=1
+        )
+    out_ref[...] = base_ref[...].astype(BF)
 
 
 def both_ways(x, step):
@@ -364,7 +352,7 @@
     return lax.ppermute(x, ALL, pairs)
 
 
-def body(
+def layer(
     nodes,
     edges,
     senders,
@@ -403,21 +391,19 @@
         [((nz, 8, LANES), F32, VM), ((RIM, width), BF, VM)],
         [wide(16)],
         copies=2,
-        name="prep",
-    )
+    )
+    rim = both_ways(my_rim, 1)
     by_z = lax.all_to_all(my_hub, "z", 0, 0)
-    rim = both_ways(my_rim, 1)
     (spread,) = call(
         spread_kernel,
         [(by_z.reshape(nz * 8, LANES), VM)],
         [((plane, HUB_DEV * nz, width), BF, VM)],
         room=54000,
-        name="spread",
     )
     hubs = lax.all_to_all(spread, PLANE, 0, 0).reshape(hub_count, width)
 
     rims = lax.all_gather(rim, "c", axis=0, tiled=True)
-    all_edges = lax.all_gather(edges, "c", axis=0, tiled=True)
+    other = lax.ppermute(edges, "c", [(0, 1), (1, 0)])
     ids = lax.all_gather(jnp.stack([senders, receivers]), "c", axis=1, tiled=True)
     block = ids[0] // node_count
     line = ids[0] - block * node_count
@@ -442,21 +428,20 @@
     (near,) = call(
         near_kernel,
         [
-            (all_edges, HB), (ids, VM), (nodes, HB), (rims, HB),
+            (core.reshape(1), SM), (edges, HB), (other, HB), (ids, VM), (nodes, HB), (rims, HB),
             (edge_proj, HB), (send_proj, HB), (recv_proj, HB), row(edge_bias),
         ],
         [((edge_count, width), F32, HB)],
         [wide(edge_count)] + [wide(slots)] + [wide(width)] * 3 + [wide(slots)] * 2
         + [wide(edge_count, F32)],
-        copies=7 + steps,
+        copies=8 + steps,
         flops=square * (edge_count * 2 + 2 * slots),
-        name="near",
     )
     new_nodes, dpre, hub_sums, my_rim, own_sums, gathered_grad, node_dpre = call(
         main_kernel,
         [
-            (core.reshape(1), SM), (hubs, HB), (near, HB), (all_edges, HB), (ids, VM), (nodes, HB),
-            (node_cot, HB), (send_proj, HB), (edge_out, HB), (node_in, HB), (node_out, HB),
+            (core.reshape(1), SM), (hubs, HB), (near, HB), (edges, HB), (other, HB), (ids, VM),
+            (nodes, HB), (node_cot, HB), (send_proj, HB), (edge_out, HB), (node_in, HB), (node_out, HB),
             row(edge_gain), row(edge_shift), row(node_bias), row(node_gain), row(node_shift),
         ],
         [
@@ -473,48 +458,43 @@
         + [wide(edge_count), wide(hub_count), wide(node_count, F32), wide(node_count)]
         + [wide(hub_count), wide(edge_count, F32), pltpu.VMEM((edge_count, LANES), F32)]
         + [wide(slots, F32), wide(slots), wide(slots)],
-        copies=12 + 2 * steps,
+        copies=14 + steps,
         flops=square * (edge_count * 6 + hub_count),
         room=0,
-        name="main",
     )
 
     hub_back = lax.all_to_all(hub_sums.reshape(plane, HUB_DEV * nz, width), PLANE, 0, 0)
     rim = both_ways(my_rim, -1)
-    edge_grad, base, flag = call(
+    edge_grad, base = call(
         late_kernel,
         [
             (core.reshape(1), SM), (dpre, HB), (ids, VM), (gathered_grad, HB), (node_dpre, HB),
             (own_sums, HB), (node_cot, HB), (edge_proj, HB), (send_proj, HB), (recv_proj, HB),
             (node_in, HB),
         ],
-        [((half, width), BF, VM), ((node_count, width), F32, VM), ((8, LANES), F32, VM)],
+        [((half, width), BF, VM), ((node_count, width), F32, VM)],
         [wide(edge_count), wide(node_count, F32), wide(node_count), wide(node_count, F32)]
         + [wide(node_count)] + [wide(width)] * 4 + [wide(slots)] * 2,
         copies=9,
         flops=square * edge_count * 2,
-        name="late",
-    )
-    by_z, rim = call(
+    )
+    (by_z,) = call(
         gather_kernel,
-        [(hub_back, HB), (rim, HB), (flag, HB)],
-        [((nz * 8, LANES), F32, VM), ((RIM, width), BF, VM)],
+        [(hub_back, HB)],
+        [((nz * 8, LANES), F32, VM)],
         [pltpu.VMEM((plane, HUB_DEV * nz, width), BF)],
-        copies=5,
+        copies=4,
         room=54000,
-        name="gather",
     )
     hub_back = lax.all_to_all(by_z.reshape(nz, 8, LANES), "z", 0, 0)
     rims = lax.all_gather(rim, "c", axis=0, tiled=True)
     (node_grad,) = call(
         last_kernel,
-        [(hub_back, VM), (rims, HB), (base, HB), (send_proj, HB)],
+        [(hub_back, VM), (rims, HB), (base, HB)],
         [((node_count, width), BF, VM)],
-        [wide(2 * RIM), wide(node_count, F32), wide(width), wide(node_count, F32)],
-        copies=3,
-        flops=square * node_count * 2,
+        [wide(2 * RIM), wide(node_count, F32)],
+        copies=2,
         room=0,
-        name="last",
     )
     return new_nodes, node_grad, edge_grad
 
@@ -525,5 +505,5 @@
     whole = P()
     in_specs = (rows, both, P(ALL), P(ALL)) + (whole,) * 12 + (rows,)
     return jax.shard_map(
-        body, mesh=fine, in_specs=in_specs, out_specs=(rows, rows, both), check_vma=False
-    )
+        layer, mesh=fine, in_specs=in_specs, out_specs=(rows, rows, both), check_vma=False
+    )

time: 106 us -> 103 us (0.972)
  the two profiles are of different devices: /device:TPU:1 before, /device:TPU:9 now
where the time goes in v5:
time: 103 us; the launch traced here: 102 us
  starting transfers between devices  37.8 us (37%)
  blocking collectives  27.9 us (27%)
  Pallas kernels  27.1 us (26%)
  waiting for transfers between devices  3.76 us (4%)
  local copies, waits for them, and re-layouts  3.54 us (3%)
    pallas_call x7, Pallas kernels, call(): pl.pallas_call(kernel, out_shape=shapes, in_specs=[spec for _, spec in in...  27.1 us
    all_to_all x1, blocking collectives, layer(): lax.all_to_all(hub_sums.reshape(plane, HUB_DEV * nz, width), PLANE, 0, 0)  15.6 us
    all_to_all x1, starting transfers between devices, layer(): by_z = lax.all_to_all(my_hub, 'z', 0, 0)  14.9 us
    ppermute x2, starting transfers between devices, both_ways(): return lax.ppermute(x, ALL, pairs)  8.75 us
    all_gather x2, blocking collectives, layer(): rims = lax.all_gather(rim, 'c', axis=0, tiled=True)  8.24 us
    all_to_all x1, starting transfers between devices, layer(): hubs = lax.all_to_all(spread, PLANE, 0, 0).reshape(hub_count, width)  6.83 us
    all_to_all x1, starting transfers between devices, layer(): hub_back = lax.all_to_all(by_z.reshape(nz, 8, LANES), 'z', 0, 0)  5.4 us
    all_gather x1, blocking collectives, layer(): lax.all_gather(jnp.stack([senders, receivers]), 'c', axis=1, tiled=True)  4.1 us
  transfers between devices with their start and end apart: 6, of which 2 were waited for; matrix products, arithmetic and copies ran while one was open for 2% of the time, Pallas kernels for 10%

profile of v5, /device:TPU:9, one launch (start us, length us, event | category | flops | bytes accessed | tf_op | source)
XLA Modules:
  0.0 101.7 jit_solution(12431129994806977510)
XLA Ops:
  0.6 1.5 %shard_map.184 = (f32[16,8,128]{2,1,0:T(8,128)}, bf16[48,512]{1,0:T(8,128)(2,1)}) custom-call(s32[1]{0:T(128)} %bitcast.core_ref, bf16[160,512]{1,0:T(8,128)(2,1)} %nodes_in.3), custom_call_target="tpu_custom_call" | custom-call | bytes 278532 | tf_op jit(solution)/shard_map/pallas_call | solution.py:87
  2.2 14.9 %all-to-all-start = ((f32[16,8,128]{2,1,0:T(8,128)}), f32[16,8,128]{2,1,0:T(8,128)S(1)}, u32[]{:S(2)}, u32[]{:S(2)}) async-start(f32[16,8,128]{2,1,0:T(8,128)} %get-tuple-element.14), calls=%async_computation | async-start | bytes 131072 | tf_op jit(solution)/shard_map/all_to_all | solution.py:396
  17.1 6.6 %collective-permute-start.1 = (bf16[48,512]{1,0:T(8,128)(2,1)}, bf16[48,512]{1,0:T(8,128)(2,1)S(1)}, u32[]{:S(2)}, u32[]{:S(2)}) collective-permute-start(bf16[48,512]{1,0:T(8,128)(2,1)} %get-tuple-element.15), channel_id=1, source_target_pairs={{0,2},{2,4},{3,1},{4,6},{5,3},{6,8},{7,5},{8,10},{9,7},{10,12},{11... | collective-permute-start | bytes 147464 | tf_op jit(solution)/shard_map/ppermute | solution.py:352
  23.7 1.9 %collective-permute-start = (bf16[384,512]{1,0:T(8,128)(2,1)}, bf16[384,512]{1,0:T(8,128)(2,1)S(1)}, u32[]{:S(2)}, u32[]{:S(2)}) collective-permute-start(bf16[384,512]{1,0:T(8,128)(2,1)} %own_in.3), channel_id=1, source_target_pairs={{0,1},{1,0},{2,3},{3,2},{4,5},{5,4},{6,7},{7,6},{8,9},{9,8},{10,11... | collective-permute-start | bytes 1179656 | tf_op jit(solution)/shard_map/ppermute | solution.py:406
  25.6 0.7 stack.14
  26.3 0.7 stack.15
  27.0 1.7 %all-to-all-done = f32[16,8,128]{2,1,0:T(8,128)S(1)} async-done(((f32[16,8,128]{2,1,0:T(8,128)}), f32[16,8,128]{2,1,0:T(8,128)S(1)}, u32[]{:S(2)}, u32[]{:S(2)}) %all-to-all-start) | async-done | bytes 65568 | tf_op jit(solution)/shard_map/all_to_all | solution.py:396
  28.7 0.9 shard_map.185
  29.6 6.8 %all-to-all-start.1 = ((bf16[16,32,512]{2,1,0:T(8,128)(2,1)}), bf16[16,32,512]{2,1,0:T(8,128)(2,1)S(1)}, u32[]{:S(2)}, u32[]{:S(2)}) async-start(bf16[16,32,512]{2,1,0:T(8,128)(2,1)} %shard_map.185), calls=%async_computation.1 | async-start | bytes 1048576 | tf_op jit(solution)/shard_map/all_to_all | solution.py:403
  36.4 4.1 %all_gather.9 = s32[2,768]{1,0:T(2,128)S(1)} all-gather(s32[2,384]{1,0:T(2,128)S(1)} %pad_add_fusion.1), channel_id=1, replica_groups=mesh['y'=4,'z'=16,'x'=4,'c'=2] {'c'}, dimensions={1}, use_global_device_ids=true | all-gather | bytes 9216 | tf_op jit(solution)/shard_map/all_gather | solution.py:407
  40.5 0.1 compare_select_fusion
  40.6 0.6 pad_add_fusion.ids_ref
  41.2 0.0 collective-permute-done.1
  41.2 2.0 %all_gather.10.rims_in = bf16[96,512]{1,0:T(8,128)(2,1)} all-gather(bf16[48,512]{1,0:T(8,128)(2,1)S(1)} %collective-permute-done.1), channel_id=1, replica_groups=mesh['y'=4,'z'=16,'x'=4,'c'=2] {'c'}, dimensions={0}, use_global_device_ids=true | all-gather | bytes 147456 | tf_op jit(solution)/shard_map/all_gather | solution.py:405
  43.2 0.0 collective-permute-done.other_in
  43.2 0.0 copy-start.1
  43.2 0.7 copy-done.1
  44.0 4.4 %shard_map.186.pre_in = f32[768,512]{1,0:T(8,128)} custom-call(s32[1]{0:T(128)} %bitcast.core_ref, bf16[384,512]{1,0:T(8,128)(2,1)} %own_in.3, bf16[384,512]{1,0:T(8,128)(2,1)} %copy-done.1, s32[2,768]{1,0:T(2,128)} %pad_add_fusion.ids_ref, bf16[160,512]{1,0:T(8,128)(2,1)} %nodes_in.3, bf16[96,512]{1,0:T(8,128)(2,1)} %all_gather.10.rims_in, ...), custom_call_target="tpu_custom_call" | custom-call | flops 1073741824 | bytes 4202500 | tf_op jit(solution)/shard_map/pallas_call | solution.py:87
  48.4 0.0 all-to-all-done.1
  48.4 0.0 copy-start
  48.4 0.8 copy-done
  49.2 11.2 %shard_map.187 = (bf16[160,512]{1,0:T(8,128)(2,1)}, bf16[768,512]{1,0:T(8,128)(2,1)}, bf16[512,512]{1,0:T(8,128)(2,1)}, bf16[48,512]{1,0:T(8,128)(2,1)}, f32[160...) custom-call(s32[1]{0:T(128)} %bitcast.core_ref, bf16[512,512]{1,0:T(8,128)(2,1)} %bitcast.12, ...), custom_call_target="tpu_custom_call" | custom-call | flops 2684354560 | bytes 8192004 | tf_op jit(solution)/shard_map/pallas_call | solution.py:87
  60.5 0.0 copy-start.3
  60.5 15.6 %all_to_all.20.sums_ref = bf16[16,32,512]{2,1,0:T(8,128)(2,1)S(1)} all-to-all(bf16[16,32,512]{2,1,0:T(8,128)(2,1)} %bitcast.13), channel_id=1, replica_groups=mesh['y'=4,'z'=16,'x'=4,'c'=2] {'y','x'}, dimensions={0} | all-to-all | bytes 1048576 | tf_op jit(solution)/shard_map/all_to_all | solution.py:466
  76.0 1.4 %shard_map.188 = f32[128,128]{1,0:T(8,128)} custom-call(bf16[16,32,512]{2,1,0:T(8,128)(2,1)S(1)} %all_to_all.20.sums_ref), custom_call_target="tpu_custom_call" | custom-call | bytes 589824 | tf_op jit(solution)/shard_map/pallas_call | solution.py:87
  77.4 5.4 %all-to-all-start.3 = ((f32[16,8,128]{2,1,0:T(8,128)}), f32[16,8,128]{2,1,0:T(8,128)S(1)}, u32[]{:S(2)}, u32[]{:S(2)}) async-start(f32[16,8,128]{2,1,0:T(8,128)} %bitcast.10), calls=%async_computation.3 | async-start | bytes 131072 | tf_op jit(solution)/shard_map/all_to_all | solution.py:489
  82.8 0.0 copy-done.3
  82.8 2.2 %collective-permute-start.2 = (bf16[48,512]{1,0:T(8,128)(2,1)S(1)}, bf16[48,512]{1,0:T(8,128)(2,1)S(1)}, u32[]{:S(2)}, u32[]{:S(2)}) collective-permute-start(bf16[48,512]{1,0:T(8,128)(2,1)S(1)} %copy-done.3), channel_id=1, source_target_pairs={{1,3},{2,0},{3,5},{4,2},{5,7},{6,4},{7,9},{8,6},{9,11},{10,8},{11,... | collective-permute-start | bytes 147464 | tf_op jit(solution)/shard_map/ppermute | solution.py:352
  85.0 5.1 %shard_map.189 = (bf16[384,512]{1,0:T(8,128)(2,1)}, f32[160,512]{1,0:T(8,128)}) custom-call(s32[1]{0:T(128)} %bitcast.core_ref, bf16[768,512]{1,0:T(8,128)(2,1)} %get-tuple-element.19.dpre_in, s32[2,768]{1,0:T(2,128)} %pad_add_fusion.ids_ref, f32[160,512]{1,0:T(8,128)} %get-tuple-element.20.gg_in, bf16[160,512]{1,0:T(8,128)(2,1)} %get-tuple-element.21.ndpre_in, ...), custom_call_target="tpu_custom_call" | custom-call | flops 805306368 | bytes 5117956 | tf_op jit(solution)/shard_map/pallas_call | solution.py:87
  90.1 2.0 %collective-permute-done.2 = bf16[48,512]{1,0:T(8,128)(2,1)S(1)} collective-permute-done((bf16[48,512]{1,0:T(8,128)(2,1)S(1)}, bf16[48,512]{1,0:T(8,128)(2,1)S(1)}, u32[]{:S(2)}, u32[]{:S(2)}) %collective-permute-start.2) | collective-permute-done | bytes 49184 | tf_op jit(solution)/shard_map/ppermute | solution.py:352
  92.2 6.2 %all_gather.11.rims_in = bf16[96,512]{1,0:T(8,128)(2,1)} all-gather(bf16[48,512]{1,0:T(8,128)(2,1)S(1)} %collective-permute-done.2), channel_id=1, replica_groups=mesh['y'=4,'z'=16,'x'=4,'c'=2] {'c'}, dimensions={0}, use_global_device_ids=true | all-gather | bytes 147456 | tf_op jit(solution)/shard_map/all_gather | solution.py:490
  98.4 0.0 all-to-all-done.3.hub_ref
  98.4 0.0 copy-start.2
  98.5 0.6 copy-done.2
  99.1 2.6 %shard_map.190 = bf16[160,512]{1,0:T(8,128)(2,1)} custom-call(f32[16,8,128]{2,1,0:T(8,128)} %copy-done.2, bf16[96,512]{1,0:T(8,128)(2,1)} %all_gather.11.rims_in, f32[160,512]{1,0:T(8,128)} %get-tuple-element.23.base_in), custom_call_target="tpu_custom_call" | custom-call | bytes 655360 | tf_op jit(solution)/shard_map/pallas_call | solution.py:87
  (1 shorter events, 0.0 us)
Async XLA Ops:
  2.2 26.5 %all-to-all-start = ((f32[16,8,128]{2,1,0:T(8,128)}), f32[16,8,128]{2,1,0:T(8,128)S(1)}, u32[]{:S(2)}, u32[]{:S(2)}) async-start(f32[16,8,128]{2,1,0:T(8,128)} %get-tuple-element.14), calls=%async_computation | async-start | bytes 131072 | tf_op jit(solution)/shard_map/all_to_all | solution.py:396
  17.1 24.1 %collective-permute-start.1 = (bf16[48,512]{1,0:T(8,128)(2,1)}, bf16[48,512]{1,0:T(8,128)(2,1)S(1)}, u32[]{:S(2)}, u32[]{:S(2)}) collective-permute-start(bf16[48,512]{1,0:T(8,128)(2,1)} %get-tuple-element.15), channel_id=1, source_target_pairs={{0,2},{2,4},{3,1},{4,6},{5,3},{6,8},{7,5},{8,10},{9,7},{10,12},{11... | collective-permute-start | bytes 147464 | tf_op jit(solution)/shard_map/ppermute | solution.py:352
  23.7 19.5 %collective-permute-start = (bf16[384,512]{1,0:T(8,128)(2,1)}, bf16[384,512]{1,0:T(8,128)(2,1)S(1)}, u32[]{:S(2)}, u32[]{:S(2)}) collective-permute-start(bf16[384,512]{1,0:T(8,128)(2,1)} %own_in.3), channel_id=1, source_target_pairs={{0,1},{1,0},{2,3},{3,2},{4,5},{5,4},{6,7},{7,6},{8,9},{9,8},{10,11... | collective-permute-start | bytes 1179656 | tf_op jit(solution)/shard_map/ppermute | solution.py:406
  29.6 18.8 %all-to-all-start.1 = ((bf16[16,32,512]{2,1,0:T(8,128)(2,1)}), bf16[16,32,512]{2,1,0:T(8,128)(2,1)S(1)}, u32[]{:S(2)}, u32[]{:S(2)}) async-start(bf16[16,32,512]{2,1,0:T(8,128)(2,1)} %shard_map.185), calls=%async_computation.1 | async-start | bytes 1048576 | tf_op jit(solution)/shard_map/all_to_all | solution.py:403
  43.2 0.7 copy-start.1
  48.4 0.8 copy-start
  60.5 22.4 %copy-start.3 = (bf16[48,512]{1,0:T(8,128)(2,1)S(1)}, bf16[48,512]{1,0:T(8,128)(2,1)}, u32[]{:S(2)}) copy-start(bf16[48,512]{1,0:T(8,128)(2,1)} %get-tuple-element.18) | copy-start | bytes 147460
  77.4 21.0 %all-to-all-start.3 = ((f32[16,8,128]{2,1,0:T(8,128)}), f32[16,8,128]{2,1,0:T(8,128)S(1)}, u32[]{:S(2)}, u32[]{:S(2)}) async-start(f32[16,8,128]{2,1,0:T(8,128)} %bitcast.10), calls=%async_computation.3 | async-start | bytes 131072 | tf_op jit(solution)/shard_map/all_to_all | solution.py:489
  82.8 9.4 %collective-permute-start.2 = (bf16[48,512]{1,0:T(8,128)(2,1)S(1)}, bf16[48,512]{1,0:T(8,128)(2,1)S(1)}, u32[]{:S(2)}, u32[]{:S(2)}) collective-permute-start(bf16[48,512]{1,0:T(8,128)(2,1)S(1)} %copy-done.3), channel_id=1, source_target_pairs={{1,3},{2,0},{3,5},{4,2},{5,7},{6,4},{7,9},{8,6},{9,11},{10,8},{11,... | collective-permute-start | bytes 147464 | tf_op jit(solution)/shard_map/ppermute | solution.py:352
  98.4 0.6 copy-start.2

commit v6 on v5

--- a/solution.py
+++ b/solution.py
@@ -77,7 +77,7 @@
 HB = pl.BlockSpec(memory_space=pltpu.HBM)
 
 
-def call(kernel, ins, outs, scratch=(), copies=0, flops=0, room=0):
+def call(kernel, ins, outs, scratch=(), copies=0, flops=0, room=0, aliases=None):
     shapes = [jax.ShapeDtypeStruct(s, d) for s, d, _ in outs]
     args = [a for a, _ in ins]
     moved = sum(math.prod(o.shape) * o.dtype.itemsize for o in shapes + args)
@@ -90,6 +90,7 @@
         in_specs=[spec for _, spec in ins],
         out_specs=[spec for _, _, spec in outs],
         scratch_shapes=scratch,
+        input_output_aliases=aliases or {},
         compiler_params=pltpu.CompilerParams(vmem_limit_bytes=GRANT - room * 1024),
         cost_estimate=pl.CostEstimate(flops=flops, bytes_accessed=moved, transcendentals=0),
     )(*args)
@@ -156,9 +157,7 @@
         total += buf_ref[p].astype(F32)
     for r in range(HUB_DEV):
         for j in range(4):
-            out_ref[pl.ds(4 * r + j, nz, stride=8), :] = total[
-                r * nz : (r + 1) * nz, j * LANES : (j + 1) * LANES
-            ]
+            out_ref[pl.ds(4 * r + j, nz, stride=8), :] = total[:, j * LANES : (j + 1) * LANES]
 
 
 def near_kernel(
@@ -272,7 +271,7 @@
 
     back += start_copies([(dpre_ref, dpre_out)], sems, done + 2)
     dpre = dpre_ref[...]
-    hub_sums_ref[...] = times(dot(hot_cols(ids_ref[0:1, :], slots, hub_count), dpre), ws_ref)
+    hub_sums_ref[...] = times(dot(hot_cols(ids_ref[2:3, :], 0, hub_count // 2), dpre), ws_ref)
     back += start_copies([(hub_sums_ref, hub_sums_out)], sems, done + 3)
     gathered_ref[...] = dot(hot_cols(ids_ref[0:1, :], 0, slots), dpre)
     back += start_copies([(gathered_ref.at[pl.ds(RIM, node_count)], own_out)], sems, done + 4)
@@ -324,21 +323,29 @@
     base_ref[...] = base
 
 
-def last_kernel(hub_ref, rims_in, base_in, out_ref, rims_ref, base_ref, sems):
+def sum_kernel(rims_in, base_in, out_ref, head_ref, rims_ref, base_ref, sems):
     node_count = base_in.shape[0]
-    copies = start_copies([(rims_in, rims_ref), (base_in, base_ref)], sems)
-    hub = hub_ref[0]
-    for z in range(1, hub_ref.shape[0]):
-        hub += hub_ref[z]
-    for copy in copies:
+    for copy in start_copies([(rims_in, rims_ref), (base_in, base_ref)], sems):
         copy.wait()
     base_ref[:RIM] += rims_ref[RIM:].astype(F32)
     base_ref[node_count - RIM :] += rims_ref[:RIM].astype(F32)
+    head_ref[...] = base_ref[: head_ref.shape[0]]
+    out_ref[...] = base_ref[...].astype(BF)
+
+
+def last_kernel(hub_ref, head_ref, grad_in, out_ref, rows_ref, sum_ref, sems):
+    del grad_in
+    hub = hub_ref[0:8]
+    for z in range(1, hub_ref.shape[0] // 8):
+        hub += hub_ref[8 * z : 8 * z + 8]
+    sum_ref[...] = head_ref[...]
     for r in range(HUB_DEV):
-        base_ref[r : r + 1] += jnp.concatenate(
+        sum_ref[r : r + 1] += jnp.concatenate(
             [hub[4 * r + j : 4 * r + j + 1] for j in range(4)], axis=1
         )
-    out_ref[...] = base_ref[...].astype(BF)
+    rows_ref[...] = sum_ref[...].astype(BF)
+    (copy,) = start_copies([(rows_ref, out_ref.at[pl.ds(0, rows_ref.shape[0])])], sems)
+    copy.wait()
 
 
 def both_ways(x, step):
@@ -410,20 +417,21 @@
     hub_y, hub_zx = block // (nz * nx), block % (nz * nx)
     hub_z, hub_x = hub_zx // nx, hub_zx % nx
     hub_slot = ((hub_y * nx + hub_x) * HUB_DEV + line) * nz + hub_z
+    from_own = block == own_block
+    from_left = (block == own_block - 1) & (line >= node_count - RIM)
+    from_right = (block == own_block + 1) & (line < RIM)
     slot = jnp.where(
-        block == own_block,
+        from_own,
         RIM + line,
         jnp.where(
-            (block == own_block - 1) & (line >= node_count - RIM),
+            from_left,
             line - (node_count - RIM),
-            jnp.where(
-                (block == own_block + 1) & (line < RIM),
-                RIM + node_count + line,
-                slots + hub_slot,
-            ),
+            jnp.where(from_right, RIM + node_count + line, slots + hub_slot),
         ),
     )
-    ids = jnp.stack([slot, ids[1] - own_block * node_count + RIM])
+    near_by = from_own | from_left | from_right
+    hub_sent = jnp.where(near_by | (line != core), -1, (hub_y * nx + hub_x) * nz + hub_z)
+    ids = jnp.stack([slot, ids[1] - own_block * node_count + RIM, hub_sent])
 
     (near,) = call(
         near_kernel,
@@ -447,7 +455,7 @@
         [
             ((node_count, width), BF, VM),
             ((edge_count, width), BF, HB),
-            ((hub_count, width), BF, HB),
+            ((hub_count // 2, width), BF, HB),
             ((RIM, width), BF, VM),
             ((node_count, width), F32, HB),
             ((node_count, width), F32, HB),
@@ -455,7 +463,7 @@
         ],
         [wide(hub_count), wide(edge_count, F32), wide(edge_count)]
         + [wide(node_count)] * 2 + [wide(width)] * 2 + [wide(2 * width), wide(width)]
-        + [wide(edge_count), wide(hub_count), wide(node_count, F32), wide(node_count)]
+        + [wide(edge_count), wide(hub_count // 2), wide(node_count, F32), wide(node_count)]
         + [wide(hub_count), wide(edge_count, F32), pltpu.VMEM((edge_count, LANES), F32)]
         + [wide(slots, F32), wide(slots), wide(slots)],
         copies=14 + steps,
@@ -463,7 +471,7 @@
         room=0,
     )
 
-    hub_back = lax.all_to_all(hub_sums.reshape(plane, HUB_DEV * nz, width), PLANE, 0, 0)
+    hub_back = lax.all_to_all(hub_sums.reshape(plane, nz, width), PLANE, 0, 0)
     rim = both_ways(my_rim, -1)
     edge_grad, base = call(
         late_kernel,
@@ -482,19 +490,27 @@
         gather_kernel,
         [(hub_back, HB)],
         [((nz * 8, LANES), F32, VM)],
-        [pltpu.VMEM((plane, HUB_DEV * nz, width), BF)],
+        [pltpu.VMEM((plane, nz, width), BF)],
         copies=4,
         room=54000,
     )
-    hub_back = lax.all_to_all(by_z.reshape(nz, 8, LANES), "z", 0, 0)
+    hub_back = lax.all_to_all(by_z.reshape(2 * nz, 4, LANES), ("z", "c"), 0, 0)
     rims = lax.all_gather(rim, "c", axis=0, tiled=True)
+    node_grad, head = call(
+        sum_kernel,
+        [(rims, HB), (base, HB)],
+        [((node_count, width), BF, VM), ((16, width), F32, VM)],
+        [wide(2 * RIM), wide(node_count, F32)],
+        copies=2,
+    )
     (node_grad,) = call(
         last_kernel,
-        [(hub_back, VM), (rims, HB), (base, HB)],
-        [((node_count, width), BF, VM)],
-        [wide(2 * RIM), wide(node_count, F32)],
-        copies=2,
-        room=0,
+        [(hub_back.reshape(nz * 8, LANES), VM), (head, VM), (node_grad, HB)],
+        [((node_count, width), BF, HB)],
+        [wide(16), wide(16, F32)],
+        copies=1,
+        room=54000,
+        aliases={2: 0},
     )
     return new_nodes, node_grad, edge_grad
 

time: 103 us -> 99.6 us (0.967)
  the two profiles are of different devices: /device:TPU:9 before, /device:TPU:1 now
where the time goes in v6:
time: 99.6 us; the launch traced here: 98.6 us
  starting transfers between devices  40.2 us (40%)
  Pallas kernels  26.3 us (26%)
  blocking collectives  22.9 us (23%)
  waiting for transfers between devices  4 us (4%)
  local copies, waits for them, and re-layouts  3.67 us (4%)
    pallas_call x8, Pallas kernels, call(): pl.pallas_call(kernel, out_shape=shapes, in_specs=[spec for _, spec in in...  26.3 us
    all_to_all x1, starting transfers between devices, layer(): by_z = lax.all_to_all(my_hub, 'z', 0, 0)  15.7 us
    all_to_all x1, blocking collectives, layer(): hub_back = lax.all_to_all(hub_sums.reshape(plane, nz, width), PLANE, 0, 0)  15.1 us
    all_to_all x1, starting transfers between devices, layer(): hub_back = lax.all_to_all(by_z.reshape(2 * nz, 4, LANES), ('z', 'c'), 0, 0)  9.34 us
    all_to_all x1, starting transfers between devices, layer(): hubs = lax.all_to_all(spread, PLANE, 0, 0).reshape(hub_count, width)  6.75 us
    all_gather x2, blocking collectives, layer(): rims = lax.all_gather(rim, 'c', axis=0, tiled=True)  6 us
    ppermute x1, starting transfers between devices, layer(): other = lax.ppermute(edges, 'c', [(0, 1), (1, 0)])  4.91 us
    ppermute x2, starting transfers between devices, both_ways(): return lax.ppermute(x, ALL, pairs)  3.49 us
  transfers between devices with their start and end apart: 6, of which 2 were waited for; matrix products, arithmetic and copies ran while one was open for 2% of the time, Pallas kernels for 12%

profile of v6, /device:TPU:1, one launch (start us, length us, event | category | flops | bytes accessed | tf_op | source)
XLA Modules:
  0.0 98.6 jit_solution(15141527755451596585)
XLA Ops:
  0.6 1.5 %shard_map.184 = (f32[16,8,128]{2,1,0:T(8,128)}, bf16[48,512]{1,0:T(8,128)(2,1)}) custom-call(s32[1]{0:T(128)} %bitcast.core_ref, bf16[160,512]{1,0:T(8,128)(2,1)} %nodes_in.3), custom_call_target="tpu_custom_call" | custom-call | bytes 278532 | tf_op jit(solution)/shard_map/pallas_call | solution.py:87
  2.2 15.7 %all-to-all-start = ((f32[16,8,128]{2,1,0:T(8,128)}), f32[16,8,128]{2,1,0:T(8,128)S(1)}, u32[]{:S(2)}, u32[]{:S(2)}) async-start(f32[16,8,128]{2,1,0:T(8,128)} %get-tuple-element.16), calls=%async_computation | async-start | bytes 131072 | tf_op jit(solution)/shard_map/all_to_all | solution.py:403
  17.9 1.3 %collective-permute-start.1 = (bf16[48,512]{1,0:T(8,128)(2,1)}, bf16[48,512]{1,0:T(8,128)(2,1)S(1)}, u32[]{:S(2)}, u32[]{:S(2)}) collective-permute-start(bf16[48,512]{1,0:T(8,128)(2,1)} %get-tuple-element.17), channel_id=1, source_target_pairs={{0,2},{2,4},{3,1},{4,6},{5,3},{6,8},{7,5},{8,10},{9,7},{10,12},{11... | collective-permute-start | bytes 147464 | tf_op jit(solution)/shard_map/ppermute | solution.py:359
  19.2 4.9 %collective-permute-start = (bf16[384,512]{1,0:T(8,128)(2,1)}, bf16[384,512]{1,0:T(8,128)(2,1)S(1)}, u32[]{:S(2)}, u32[]{:S(2)}) collective-permute-start(bf16[384,512]{1,0:T(8,128)(2,1)} %own_in.3), channel_id=1, source_target_pairs={{0,1},{1,0},{2,3},{3,2},{4,5},{5,4},{6,7},{7,6},{8,9},{9,8},{10,11... | collective-permute-start | bytes 1179656 | tf_op jit(solution)/shard_map/ppermute | solution.py:413
  24.1 0.7 stack.15
  24.8 0.7 stack.16
  25.5 1.8 %all_gather.9 = s32[2,768]{1,0:T(2,128)S(1)} all-gather(s32[2,384]{1,0:T(2,128)S(1)} %pad_add_fusion.1), channel_id=1, replica_groups=mesh['y'=4,'z'=16,'x'=4,'c'=2] {'c'}, dimensions={1}, use_global_device_ids=true | all-gather | bytes 9216 | tf_op jit(solution)/shard_map/all_gather | solution.py:414
  27.4 2.1 %all-to-all-done = f32[16,8,128]{2,1,0:T(8,128)S(1)} async-done(((f32[16,8,128]{2,1,0:T(8,128)}), f32[16,8,128]{2,1,0:T(8,128)S(1)}, u32[]{:S(2)}, u32[]{:S(2)}) %all-to-all-start) | async-done | bytes 65568 | tf_op jit(solution)/shard_map/all_to_all | solution.py:403
  29.5 0.9 shard_map.185
  30.4 6.8 %all-to-all-start.1 = ((bf16[16,32,512]{2,1,0:T(8,128)(2,1)}), bf16[16,32,512]{2,1,0:T(8,128)(2,1)S(1)}, u32[]{:S(2)}, u32[]{:S(2)}) async-start(bf16[16,32,512]{2,1,0:T(8,128)(2,1)} %shard_map.185), calls=%async_computation.1 | async-start | bytes 1048576 | tf_op jit(solution)/shard_map/all_to_all | solution.py:410
  37.1 0.1 compare_select_fusion.6
  37.2 0.6 pad_add_fusion.ids_ref
  37.9 0.0 collective-permute-done.1
  37.9 4.0 %all_gather.10.rims_in = bf16[96,512]{1,0:T(8,128)(2,1)} all-gather(bf16[48,512]{1,0:T(8,128)(2,1)S(1)} %collective-permute-done.1), channel_id=1, replica_groups=mesh['y'=4,'z'=16,'x'=4,'c'=2] {'c'}, dimensions={0}, use_global_device_ids=true | all-gather | bytes 147456 | tf_op jit(solution)/shard_map/all_gather | solution.py:412
  41.9 0.0 collective-permute-done.other_in
  41.9 0.0 copy-start.2
  41.9 0.7 copy-done.2
  42.6 4.4 %shard_map.186.pre_in = f32[768,512]{1,0:T(8,128)} custom-call(s32[1]{0:T(128)} %bitcast.core_ref, bf16[384,512]{1,0:T(8,128)(2,1)} %own_in.3, bf16[384,512]{1,0:T(8,128)(2,1)} %copy-done.2, s32[3,768]{1,0:T(4,128)} %pad_add_fusion.ids_ref, bf16[160,512]{1,0:T(8,128)(2,1)} %nodes_in.3, bf16[96,512]{1,0:T(8,128)(2,1)} %all_gather.10.rims_in, ...), custom_call_target="tpu_custom_call" | custom-call | flops 1073741824 | bytes 4205572 | tf_op jit(solution)/shard_map/pallas_call | solution.py:87
  47.1 0.0 all-to-all-done.1
  47.1 0.0 copy-start.1
  47.1 0.8 copy-done.1
  47.9 10.9 %shard_map.187 = (bf16[160,512]{1,0:T(8,128)(2,1)}, bf16[768,512]{1,0:T(8,128)(2,1)}, bf16[256,512]{1,0:T(8,128)(2,1)}, bf16[48,512]{1,0:T(8,128)(2,1)}, f32[160...) custom-call(s32[1]{0:T(128)} %bitcast.core_ref, bf16[512,512]{1,0:T(8,128)(2,1)} %bitcast.14, ...), custom_call_target="tpu_custom_call" | custom-call | flops 2684354560 | bytes 7932932 | tf_op jit(solution)/shard_map/pallas_call | solution.py:87
  58.8 15.1 %all_to_all.20.sums_ref = bf16[16,16,512]{2,1,0:T(8,128)(2,1)S(1)} all-to-all(bf16[16,16,512]{2,1,0:T(8,128)(2,1)} %bitcast.15), channel_id=1, replica_groups=mesh['y'=4,'z'=16,'x'=4,'c'=2] {'y','x'}, dimensions={0} | all-to-all | bytes 524288 | tf_op jit(solution)/shard_map/all_to_all | solution.py:474
  73.9 1.0 %shard_map.188 = f32[128,128]{1,0:T(8,128)} custom-call(bf16[16,16,512]{2,1,0:T(8,128)(2,1)S(1)} %all_to_all.20.sums_ref), custom_call_target="tpu_custom_call" | custom-call | bytes 327680 | tf_op jit(solution)/shard_map/pallas_call | solution.py:87
  74.9 9.3 %all-to-all-start.3 = ((f32[32,4,128]{2,1,0:T(4,128)}), f32[32,4,128]{2,1,0:T(4,128)S(1)}, u32[]{:S(2)}, u32[]{:S(2)}) async-start(f32[32,4,128]{2,1,0:T(4,128)} %bitcast.10), calls=%async_computation.3 | async-start | bytes 131072 | tf_op jit(solution)/shard_map/all_to_all | solution.py:497
  84.2 2.2 %collective-permute-start.2 = (bf16[48,512]{1,0:T(8,128)(2,1)}, bf16[48,512]{1,0:T(8,128)(2,1)S(1)}, u32[]{:S(2)}, u32[]{:S(2)}) collective-permute-start(bf16[48,512]{1,0:T(8,128)(2,1)} %get-tuple-element.20), channel_id=1, source_target_pairs={{1,3},{2,0},{3,5},{4,2},{5,7},{6,4},{7,9},{8,6},{9,11},{10,8},{11,... | collective-permute-start | bytes 147464 | tf_op jit(solution)/shard_map/ppermute | solution.py:359
  86.4 5.1 %shard_map.189 = (bf16[384,512]{1,0:T(8,128)(2,1)}, f32[160,512]{1,0:T(8,128)}) custom-call(s32[1]{0:T(128)} %bitcast.core_ref, bf16[768,512]{1,0:T(8,128)(2,1)} %get-tuple-element.21.dpre_in, s32[3,768]{1,0:T(4,128)} %pad_add_fusion.ids_ref, f32[160,512]{1,0:T(8,128)} %get-tuple-element.22.gg_in, bf16[160,512]{1,0:T(8,128)(2,1)} %get-tuple-element.23.ndpre_in, ...), custom_call_target="tpu_custom_call" | custom-call | flops 805306368 | bytes 5121028 | tf_op jit(solution)/shard_map/pallas_call | solution.py:87
  91.6 0.0 collective-permute-done.2
  91.6 2.0 %all_gather.11.rims_in = bf16[96,512]{1,0:T(8,128)(2,1)} all-gather(bf16[48,512]{1,0:T(8,128)(2,1)S(1)} %collective-permute-done.2), channel_id=1, replica_groups=mesh['y'=4,'z'=16,'x'=4,'c'=2] {'c'}, dimensions={0}, use_global_device_ids=true | all-gather | bytes 147456 | tf_op jit(solution)/shard_map/all_gather | solution.py:498
  93.6 1.7 %shard_map.190 = (bf16[160,512]{1,0:T(8,128)(2,1)}, f32[16,512]{1,0:T(8,128)}) custom-call(bf16[96,512]{1,0:T(8,128)(2,1)} %all_gather.11.rims_in, f32[160,512]{1,0:T(8,128)} %get-tuple-element.25.base_in), custom_call_target="tpu_custom_call" | custom-call | bytes 622592 | tf_op jit(solution)/shard_map/pallas_call | solution.py:87
  95.3 1.9 %all-to-all-done.3 = f32[32,4,128]{2,1,0:T(4,128)S(1)} async-done(((f32[32,4,128]{2,1,0:T(4,128)}), f32[32,4,128]{2,1,0:T(4,128)S(1)}, u32[]{:S(2)}, u32[]{:S(2)}) %all-to-all-start.3) | async-done | bytes 65568 | tf_op jit(solution)/shard_map/all_to_all | solution.py:497
  97.2 0.0 copy-start
  97.2 0.8 copy-done
  98.0 0.6 shard_map.191
  (3 shorter events, 0.1 us)
Async XLA Ops:
  2.2 27.3 %all-to-all-start = ((f32[16,8,128]{2,1,0:T(8,128)}), f32[16,8,128]{2,1,0:T(8,128)S(1)}, u32[]{:S(2)}, u32[]{:S(2)}) async-start(f32[16,8,128]{2,1,0:T(8,128)} %get-tuple-element.16), calls=%async_computation | async-start | bytes 131072 | tf_op jit(solution)/shard_map/all_to_all | solution.py:403
  17.9 19.9 %collective-permute-start.1 = (bf16[48,512]{1,0:T(8,128)(2,1)}, bf16[48,512]{1,0:T(8,128)(2,1)S(1)}, u32[]{:S(2)}, u32[]{:S(2)}) collective-permute-start(bf16[48,512]{1,0:T(8,128)(2,1)} %get-tuple-element.17), channel_id=1, source_target_pairs={{0,2},{2,4},{3,1},{4,6},{5,3},{6,8},{7,5},{8,10},{9,7},{10,12},{11... | collective-permute-start | bytes 147464 | tf_op jit(solution)/shard_map/ppermute | solution.py:359
  19.2 22.6 %collective-permute-start = (bf16[384,512]{1,0:T(8,128)(2,1)}, bf16[384,512]{1,0:T(8,128)(2,1)S(1)}, u32[]{:S(2)}, u32[]{:S(2)}) collective-permute-start(bf16[384,512]{1,0:T(8,128)(2,1)} %own_in.3), channel_id=1, source_target_pairs={{0,1},{1,0},{2,3},{3,2},{4,5},{5,4},{6,7},{7,6},{8,9},{9,8},{10,11... | collective-permute-start | bytes 1179656 | tf_op jit(solution)/shard_map/ppermute | solution.py:413
  30.4 16.7 %all-to-all-start.1 = ((bf16[16,32,512]{2,1,0:T(8,128)(2,1)}), bf16[16,32,512]{2,1,0:T(8,128)(2,1)S(1)}, u32[]{:S(2)}, u32[]{:S(2)}) async-start(bf16[16,32,512]{2,1,0:T(8,128)(2,1)} %shard_map.185), calls=%async_computation.1 | async-start | bytes 1048576 | tf_op jit(solution)/shard_map/all_to_all | solution.py:410
  41.9 0.7 copy-start.2
  47.1 0.8 copy-start.1
  74.9 22.4 %all-to-all-start.3 = ((f32[32,4,128]{2,1,0:T(4,128)}), f32[32,4,128]{2,1,0:T(4,128)S(1)}, u32[]{:S(2)}, u32[]{:S(2)}) async-start(f32[32,4,128]{2,1,0:T(4,128)} %bitcast.10), calls=%async_computation.3 | async-start | bytes 131072 | tf_op jit(solution)/shard_map/all_to_all | solution.py:497
  84.2 7.3 %collective-permute-start.2 = (bf16[48,512]{1,0:T(8,128)(2,1)}, bf16[48,512]{1,0:T(8,128)(2,1)S(1)}, u32[]{:S(2)}, u32[]{:S(2)}) collective-permute-start(bf16[48,512]{1,0:T(8,128)(2,1)} %get-tuple-element.20), channel_id=1, source_target_pairs={{1,3},{2,0},{3,5},{4,2},{5,7},{6,4},{7,9},{8,6},{9,11},{10,8},{11,... | collective-permute-start | bytes 147464 | tf_op jit(solution)/shard_map/ppermute | solution.py:359
  97.2 0.8 copy-start

commit v7 on v6

--- a/solution.py
+++ b/solution.py
@@ -18,7 +18,8 @@
 SPACE = ("y", "z", "x")
 PLANE = ("y", "x")
 LANES = 128
-TILE = 256
+NEAR_TILE = 384
+MAIN_TILE = 768
 SHAPE = (4, 16, 4)
 GRANT = 60 * 1024 * 1024
 
@@ -143,7 +144,7 @@
 
 def gather_kernel(sums_ref, out_ref, buf_ref, sems):
     planes = sums_ref.shape[0]
-    nz = out_ref.shape[0] // 8
+    nz = out_ref.shape[0] // 4
     quarter = planes // 4
     pairs = [
         (sums_ref.at[pl.ds(k * quarter, quarter)], buf_ref.at[pl.ds(k * quarter, quarter)])
@@ -155,9 +156,8 @@
         if p % quarter == 0:
             copies[p // quarter].wait()
         total += buf_ref[p].astype(F32)
-    for r in range(HUB_DEV):
-        for j in range(4):
-            out_ref[pl.ds(4 * r + j, nz, stride=8), :] = total[:, j * LANES : (j + 1) * LANES]
+    for j in range(4):
+        out_ref[pl.ds(j, nz, stride=4), :] = total[:, j * LANES : (j + 1) * LANES]
 
 
 def near_kernel(
@@ -187,8 +187,8 @@
     for copy in copies[5:]:
         copy.wait()
     back = []
-    for i in range(edges_ref.shape[0] // TILE):
-        rows = pl.ds(i * TILE, TILE)
+    for i in range(edges_ref.shape[0] // NEAR_TILE):
+        rows = pl.ds(i * NEAR_TILE, NEAR_TILE)
         pre = dot(edges_ref[rows, :], we_ref[...])
         pre += dot(hot_rows(ids_ref[0:1, rows], 0, slots), send_ref[...])
         pre += dot(hot_rows(ids_ref[1:2, rows], 0, slots), recv_ref[...])
@@ -209,10 +209,10 @@
     node_count, width = nodes_in.shape
     hub_count = hubs_in.shape[0]
     edge_count = edges_ref.shape[0]
-    steps = edge_count // TILE
+    steps = edge_count // MAIN_TILE
     slots = 2 * RIM + node_count
     own = slice(RIM, RIM + node_count)
-    tiles = [pl.ds(i * TILE, TILE) for i in range(steps)]
+    tiles = [pl.ds(i * MAIN_TILE, MAIN_TILE) for i in range(steps)]
     hubs, ws, wo, *rest = start_copies(
         [(hubs_in, hubs_ref), (ws_in, ws_ref), (wo_in, wo_ref)]
         + [(pre_in.at[rows], pre_ref.at[rows]) for rows in tiles]
@@ -233,11 +233,12 @@
             rest[steps + 1].wait()
         pre = pre_ref[rows, :] + dot(hot_rows(ids_ref[0:1, rows], slots, hub_count), terms_ref[...])
         gate = jax.nn.sigmoid(pre)
-        pre_ref[rows, :] = gate * (1.0 + pre * (1.0 - gate))
-        edge_sum = dot((pre * gate).astype(BF), wo_ref[...])
+        act = pre * gate
+        pre_ref[rows, :] = gate + act * (1.0 - gate)
+        edge_sum = dot(act.astype(BF), wo_ref[...])
         normed, scale = layer_stats(edge_sum)
         normed_ref[rows, :] = normed
-        scale_ref[rows, :] = jnp.broadcast_to(scale, (TILE, LANES))
+        scale_ref[rows, :] = jnp.broadcast_to(scale, (MAIN_TILE, LANES))
         new_edges = edges_ref[rows, :].astype(F32) + normed * egain_ref[...] + eshift_ref[...]
         gathered_ref[...] += dot(hot_cols(ids_ref[1:2, rows], 0, slots), new_edges.astype(BF))
 
@@ -247,26 +248,29 @@
     gathered = gathered_ref[own].astype(BF)
     node_pre = dot(nodes, win_ref[:width]) + dot(gathered, win_ref[width:]) + nbias_ref[...]
     gate = jax.nn.sigmoid(node_pre)
-    node_mix = dot((node_pre * gate).astype(BF), wout_ref[...])
+    act = node_pre * gate
+    node_mix = dot(act.astype(BF), wout_ref[...])
     normed, scale = layer_stats(node_mix)
     new_nodes = nodes.astype(F32) + normed * ngain_ref[...] + nshift_ref[...]
     new_ref[...] = new_nodes.astype(BF)
     dmix = norm_back(cot_ref[...].astype(F32), normed, scale, ngain_ref[...]).astype(BF)
-    ndpre = dot_t(dmix, wout_ref[...]) * (gate * (1.0 + node_pre * (1.0 - gate)))
+    ndpre = dot_t(dmix, wout_ref[...]) * (gate + act * (1.0 - gate))
     ndpre = ndpre.astype(BF)
     ndpre_ref[...] = ndpre
     gathered_grad = dot_t(ndpre, win_ref[width:])
     gg_ref[...] = gathered_grad
     back = start_copies([(ndpre_ref, ndpre_out), (gg_ref, gg_out)], sems, done)
-    high, low = split2(gathered_grad)
+    scaled = gathered_grad * egain_ref[...]
+    high, low = split2(scaled - row_mean(scaled))
     for ref, part in ((high_ref, high), (low_ref, low)):
         ref[...] = jnp.zeros_like(ref)
         ref[own] = part
 
     for rows in tiles:
         hot = hot_rows(ids_ref[1:2, rows], 0, slots)
-        upstream = dot(hot, high_ref[...]) + dot(hot, low_ref[...])
-        dsum = norm_back(upstream, normed_ref[rows, :], scale_ref[rows, :1], egain_ref[...])
+        scaled = dot(hot, high_ref[...]) + dot(hot, low_ref[...])
+        normed = normed_ref[rows, :]
+        dsum = scale_ref[rows, :1] * (scaled - normed * row_mean(scaled * normed))
         dpre_ref[rows, :] = (dot_t(dsum.astype(BF), wo_ref[...]) * pre_ref[rows, :]).astype(BF)
 
     back += start_copies([(dpre_ref, dpre_out)], sems, done + 2)
@@ -282,31 +286,31 @@
 
 
 def late_kernel(
-    core_ref, dpre_in, ids_ref, gg_in, ndpre_in, own_in, cot_in, we_in, ws_in, wr_in, win_in,
-    egrad_ref, base_ref,
-    dpre_ref, gg_ref, ndpre_ref, own_ref, cot_ref, we_ref, ws_ref, wr_ref, win_ref,
-    high_ref, low_ref, sems,
+    core_ref, dpre_in, ids_ref, gg_in, ndpre_in, own_in, cot_in, we_in, ws_in, wr_in, win_in, rims_in,
+    egrad_ref, grad_ref, head_ref,
+    dpre_ref, gg_ref, ndpre_ref, own_ref, cot_ref, we_ref, ws_ref, wr_ref, win_ref, rims_ref,
+    high_ref, low_ref, base_ref, sems,
 ):
     node_count, width = cot_in.shape
     slots = 2 * RIM + node_count
     own = slice(RIM, RIM + node_count)
     half = egrad_ref.shape[0]
-    copies = start_copies(
+    gg, dpre, we, wr, win, ndpre, ws, sums, cot, rims = start_copies(
         [
             (gg_in, gg_ref),
             (dpre_in, dpre_ref),
             (we_in, we_ref),
+            (wr_in, wr_ref),
+            (win_in.at[pl.ds(0, width)], win_ref),
             (ndpre_in, ndpre_ref),
+            (ws_in, ws_ref),
             (own_in, own_ref),
             (cot_in, cot_ref),
-            (win_in.at[pl.ds(0, width)], win_ref),
-            (ws_in, ws_ref),
-            (wr_in, wr_ref),
+            (rims_in, rims_ref),
         ],
         sems,
     )
-    for copy in copies:
-        copy.wait()
+    gg.wait()
     high, low = split2(gg_ref[...])
     for ref, part in ((high_ref, high), (low_ref, low)):
         ref[...] = jnp.zeros_like(ref)
@@ -314,35 +318,35 @@
     rows = pl.ds(pl.multiple_of(core_ref[0] * half, half), half)
     hot = hot_rows(ids_ref[1:2, rows], 0, slots)
     upstream = dot(hot, high_ref[...]) + dot(hot, low_ref[...])
+    dpre.wait()
+    we.wait()
     egrad_ref[...] = (upstream + dot_t(dpre_ref[rows, :], we_ref[...])).astype(BF)
-    base = cot_ref[...].astype(F32) + dot_t(ndpre_ref[...], win_ref[...])
     recv = dot(hot_cols(ids_ref[1:2, :], RIM, node_count), dpre_ref[...])
-    for sums, weight in ((own_ref[...], ws_ref), (recv, wr_ref)):
-        high, low = split2(sums)
-        base += dot_t(high, weight[...]) + dot_t(low, weight[...])
-    base_ref[...] = base
-
-
-def sum_kernel(rims_in, base_in, out_ref, head_ref, rims_ref, base_ref, sems):
-    node_count = base_in.shape[0]
-    for copy in start_copies([(rims_in, rims_ref), (base_in, base_ref)], sems):
+    high, low = split2(recv)
+    wr.wait()
+    base = dot_t(high, wr_ref[...]) + dot_t(low, wr_ref[...])
+    for copy in (win, ndpre, ws, sums, cot, rims):
         copy.wait()
+    base += dot_t(ndpre_ref[...], win_ref[...])
+    high, low = split2(own_ref[...])
+    base += dot_t(high, ws_ref[...]) + dot_t(low, ws_ref[...])
+    base_ref[...] = base + cot_ref[...].astype(F32)
     base_ref[:RIM] += rims_ref[RIM:].astype(F32)
     base_ref[node_count - RIM :] += rims_ref[:RIM].astype(F32)
     head_ref[...] = base_ref[: head_ref.shape[0]]
-    out_ref[...] = base_ref[...].astype(BF)
+    grad_ref[...] = base_ref[...].astype(BF)
 
 
 def last_kernel(hub_ref, head_ref, grad_in, out_ref, rows_ref, sum_ref, sems):
     del grad_in
-    hub = hub_ref[0:8]
-    for z in range(1, hub_ref.shape[0] // 8):
-        hub += hub_ref[8 * z : 8 * z + 8]
+    count = hub_ref.shape[0] // HUB_DEV
     sum_ref[...] = head_ref[...]
     for r in range(HUB_DEV):
-        sum_ref[r : r + 1] += jnp.concatenate(
-            [hub[4 * r + j : 4 * r + j + 1] for j in range(4)], axis=1
-        )
+        pair = hub_ref[r * count : r * count + 8]
+        for k in range(8, count, 8):
+            pair += hub_ref[r * count + k : r * count + k + 8]
+        hub = pair[:4] + pair[4:]
+        sum_ref[r : r + 1] += jnp.concatenate([hub[j : j + 1] for j in range(4)], axis=1)
     rows_ref[...] = sum_ref[...].astype(BF)
     (copy,) = start_copies([(rows_ref, out_ref.at[pl.ds(0, rows_ref.shape[0])])], sems)
     copy.wait()
@@ -381,7 +385,6 @@
     node_count, width = nodes.shape
     half = edges.shape[0]
     edge_count = 2 * half
-    steps = edge_count // TILE
     ny, nz, nx = (lax.axis_size(a) for a in SPACE)
     plane = ny * nx
     hub_count = plane * HUB_DEV * nz
@@ -442,7 +445,7 @@
         [((edge_count, width), F32, HB)],
         [wide(edge_count)] + [wide(slots)] + [wide(width)] * 3 + [wide(slots)] * 2
         + [wide(edge_count, F32)],
-        copies=8 + steps,
+        copies=8 + edge_count // NEAR_TILE,
         flops=square * (edge_count * 2 + 2 * slots),
     )
     new_nodes, dpre, hub_sums, my_rim, own_sums, gathered_grad, node_dpre = call(
@@ -466,46 +469,41 @@
         + [wide(edge_count), wide(hub_count // 2), wide(node_count, F32), wide(node_count)]
         + [wide(hub_count), wide(edge_count, F32), pltpu.VMEM((edge_count, LANES), F32)]
         + [wide(slots, F32), wide(slots), wide(slots)],
-        copies=14 + steps,
+        copies=14 + edge_count // MAIN_TILE,
         flops=square * (edge_count * 6 + hub_count),
         room=0,
     )
 
     hub_back = lax.all_to_all(hub_sums.reshape(plane, nz, width), PLANE, 0, 0)
     rim = both_ways(my_rim, -1)
-    edge_grad, base = call(
+    (by_z,) = call(
+        gather_kernel,
+        [(hub_back, HB)],
+        [((nz * 4, LANES), F32, VM)],
+        [pltpu.VMEM((plane, nz, width), BF)],
+        copies=4,
+        room=54000,
+    )
+    hub_back = lax.all_to_all(by_z.reshape(nz, 4, LANES), "z", 0, 0)
+    hub_back = lax.all_gather(hub_back.reshape(nz * 4, LANES), "c", axis=0, tiled=True)
+    rims = lax.all_gather(rim, "c", axis=0, tiled=True)
+    edge_grad, node_grad, head = call(
         late_kernel,
         [
             (core.reshape(1), SM), (dpre, HB), (ids, VM), (gathered_grad, HB), (node_dpre, HB),
             (own_sums, HB), (node_cot, HB), (edge_proj, HB), (send_proj, HB), (recv_proj, HB),
-            (node_in, HB),
+            (node_in, HB), (rims, HB),
         ],
-        [((half, width), BF, VM), ((node_count, width), F32, VM)],
+        [((half, width), BF, VM), ((node_count, width), BF, VM), ((16, width), F32, VM)],
         [wide(edge_count), wide(node_count, F32), wide(node_count), wide(node_count, F32)]
-        + [wide(node_count)] + [wide(width)] * 4 + [wide(slots)] * 2,
-        copies=9,
+        + [wide(node_count)] + [wide(width)] * 4 + [wide(2 * RIM)] + [wide(slots)] * 2
+        + [wide(node_count, F32)],
+        copies=10,
         flops=square * edge_count * 2,
-    )
-    (by_z,) = call(
-        gather_kernel,
-        [(hub_back, HB)],
-        [((nz * 8, LANES), F32, VM)],
-        [pltpu.VMEM((plane, nz, width), BF)],
-        copies=4,
-        room=54000,
-    )
-    hub_back = lax.all_to_all(by_z.reshape(2 * nz, 4, LANES), ("z", "c"), 0, 0)
-    rims = lax.all_gather(rim, "c", axis=0, tiled=True)
-    node_grad, head = call(
-        sum_kernel,
-        [(rims, HB), (base, HB)],
-        [((node_count, width), BF, VM), ((16, width), F32, VM)],
-        [wide(2 * RIM), wide(node_count, F32)],
-        copies=2,
     )
     (node_grad,) = call(
         last_kernel,
-        [(hub_back.reshape(nz * 8, LANES), VM), (head, VM), (node_grad, HB)],
+        [(hub_back, VM), (head, VM), (node_grad, HB)],
         [((node_count, width), BF, HB)],
         [wide(16), wide(16, F32)],
         copies=1,

time: 99.6 us -> 99.2 us (level)
  blocking collectives: 22.9 us -> 15 us
  waiting for transfers between devices: 4 us -> 9.93 us
  starting transfers between devices: 40.2 us -> 45.8 us
  Pallas kernels: 26.3 us -> 22.4 us
    all_to_all x1 -> x0, blocking collectives: 15.1 us -> none  [layer(): hub_back = lax.all_to_all(hub_sums.reshape(plane, nz, width), PLANE, 0, 0)]
    all_to_all x1 -> x2, waiting for transfers between devices: 1.9 us -> 7.83 us  [the longest x1 4.88 us: layer(): hub_back = lax.all_to_all(hub_sums.reshape(plane, nz, width), PLANE, 0, 0)]
    all_gather x0 -> x1, blocking collectives: none -> 5.07 us  [layer(): lax.all_gather(hub_back.reshape(nz * 4, LANES), 'c', axis=0, tiled=True)]
    all_to_all x1 -> x2, starting transfers between devices: 9.34 us -> 13.8 us  [the longest x1 6.93 us: layer(): hub_back = lax.all_to_all(hub_sums.reshape(plane, nz, width), PLANE, 0, 0)]
    pallas_call x8 -> x7, Pallas kernels: 26.3 us -> 22.4 us  [call(): pl.pallas_call(kernel, out_shape=shapes, in_specs=[spec for _, spec in in...]
    all_gather x2, blocking collectives: 6 us -> 8.07 us  [layer(): rims = lax.all_gather(rim, 'c', axis=0, tiled=True)]
    ppermute x2, starting transfers between devices: 3.49 us -> 4.55 us  [both_ways(): return lax.ppermute(x, ALL, pairs)]
  transfers between devices with their start and end apart: 6 -> 7, of which waited for: 2 -> 3; matrix products, arithmetic and copies ran while one was open for 2% -> 2% of each run, Pallas kernels for 12% -> 11%
where the time goes in v7:
time: 99.2 us; the launch traced here: 98.3 us
  starting transfers between devices  45.8 us (46%)
  Pallas kernels  22.4 us (23%)
  blocking collectives  15 us (15%)
  waiting for transfers between devices  9.93 us (10%)
  local copies, waits for them, and re-layouts  3.67 us (4%)
    pallas_call x7, Pallas kernels, call(): pl.pallas_call(kernel, out_shape=shapes, in_specs=[spec for _, spec in in...  22.4 us
    all_to_all x1, starting transfers between devices, layer(): by_z = lax.all_to_all(my_hub, 'z', 0, 0)  15.7 us
    all_gather x2, blocking collectives, layer(): rims = lax.all_gather(rim, 'c', axis=0, tiled=True)  8.07 us
    all_to_all x1, starting transfers between devices, layer(): hub_back = lax.all_to_all(hub_sums.reshape(plane, nz, width), PLANE, 0, 0)  6.93 us
    all_to_all x1, starting transfers between devices, layer(): hub_back = lax.all_to_all(by_z.reshape(nz, 4, LANES), 'z', 0, 0)  6.87 us
    all_to_all x1, starting transfers between devices, layer(): hubs = lax.all_to_all(spread, PLANE, 0, 0).reshape(hub_count, width)  6.75 us
    all_gather x1, blocking collectives, layer(): lax.all_gather(hub_back.reshape(nz * 4, LANES), 'c', axis=0, tiled=True)  5.07 us
    ppermute x1, starting transfers between devices, layer(): other = lax.ppermute(edges, 'c', [(0, 1), (1, 0)])  4.91 us
  transfers between devices with their start and end apart: 7, of which 3 were waited for; matrix products, arithmetic and copies ran while one was open for 2% of the time, Pallas kernels for 11%

profile of v7, /device:TPU:1, one launch (start us, length us, event | category | flops | bytes accessed | tf_op | source)
XLA Modules:
  0.0 98.3 jit_solution(8168887924769963823)
XLA Ops:
  0.6 1.5 %shard_map.184 = (f32[16,8,128]{2,1,0:T(8,128)}, bf16[48,512]{1,0:T(8,128)(2,1)}) custom-call(s32[1]{0:T(128)} %bitcast.core_ref, bf16[160,512]{1,0:T(8,128)(2,1)} %nodes_in.3), custom_call_target="tpu_custom_call" | custom-call | bytes 278532 | tf_op jit(solution)/shard_map/pallas_call | solution.py:88
  2.2 15.7 %all-to-all-start = ((f32[16,8,128]{2,1,0:T(8,128)}), f32[16,8,128]{2,1,0:T(8,128)S(1)}, u32[]{:S(2)}, u32[]{:S(2)}) async-start(f32[16,8,128]{2,1,0:T(8,128)} %get-tuple-element.15), calls=%async_computation | async-start | bytes 131072 | tf_op jit(solution)/shard_map/all_to_all | solution.py:406
  17.9 1.3 %collective-permute-start.1 = (bf16[48,512]{1,0:T(8,128)(2,1)}, bf16[48,512]{1,0:T(8,128)(2,1)S(1)}, u32[]{:S(2)}, u32[]{:S(2)}) collective-permute-start(bf16[48,512]{1,0:T(8,128)(2,1)} %get-tuple-element.16), channel_id=1, source_target_pairs={{0,2},{2,4},{3,1},{4,6},{5,3},{6,8},{7,5},{8,10},{9,7},{10,12},{11... | collective-permute-start | bytes 147464 | tf_op jit(solution)/shard_map/ppermute | solution.py:363
  19.2 4.9 %collective-permute-start = (bf16[384,512]{1,0:T(8,128)(2,1)}, bf16[384,512]{1,0:T(8,128)(2,1)S(1)}, u32[]{:S(2)}, u32[]{:S(2)}) collective-permute-start(bf16[384,512]{1,0:T(8,128)(2,1)} %own_in.3), channel_id=1, source_target_pairs={{0,1},{1,0},{2,3},{3,2},{4,5},{5,4},{6,7},{7,6},{8,9},{9,8},{10,11... | collective-permute-start | bytes 1179656 | tf_op jit(solution)/shard_map/ppermute | solution.py:416
  24.1 0.7 stack.15
  24.8 0.7 stack.16
  25.5 1.8 %all_gather.12 = s32[2,768]{1,0:T(2,128)S(1)} all-gather(s32[2,384]{1,0:T(2,128)S(1)} %pad_add_fusion.1), channel_id=1, replica_groups=mesh['y'=4,'z'=16,'x'=4,'c'=2] {'c'}, dimensions={1}, use_global_device_ids=true | all-gather | bytes 9216 | tf_op jit(solution)/shard_map/all_gather | solution.py:417
  27.4 2.1 %all-to-all-done = f32[16,8,128]{2,1,0:T(8,128)S(1)} async-done(((f32[16,8,128]{2,1,0:T(8,128)}), f32[16,8,128]{2,1,0:T(8,128)S(1)}, u32[]{:S(2)}, u32[]{:S(2)}) %all-to-all-start) | async-done | bytes 65568 | tf_op jit(solution)/shard_map/all_to_all | solution.py:406
  29.5 0.9 shard_map.185
  30.4 6.8 %all-to-all-start.1 = ((bf16[16,32,512]{2,1,0:T(8,128)(2,1)}), bf16[16,32,512]{2,1,0:T(8,128)(2,1)S(1)}, u32[]{:S(2)}, u32[]{:S(2)}) async-start(bf16[16,32,512]{2,1,0:T(8,128)(2,1)} %shard_map.185), calls=%async_computation.1 | async-start | bytes 1048576 | tf_op jit(solution)/shard_map/all_to_all | solution.py:413
  37.1 0.1 compare_select_fusion.6
  37.2 0.6 pad_add_fusion.ids_ref
  37.9 0.0 collective-permute-done.1
  37.9 4.0 %all_gather.13.rims_in = bf16[96,512]{1,0:T(8,128)(2,1)} all-gather(bf16[48,512]{1,0:T(8,128)(2,1)S(1)} %collective-permute-done.1), channel_id=1, replica_groups=mesh['y'=4,'z'=16,'x'=4,'c'=2] {'c'}, dimensions={0}, use_global_device_ids=true | all-gather | bytes 147456 | tf_op jit(solution)/shard_map/all_gather | solution.py:415
  41.8 0.0 collective-permute-done.other_in
  41.9 0.0 copy-start.2
  41.9 0.7 copy-done.2
  42.6 4.5 %shard_map.186.pre_in = f32[768,512]{1,0:T(8,128)} custom-call(s32[1]{0:T(128)} %bitcast.core_ref, bf16[384,512]{1,0:T(8,128)(2,1)} %own_in.3, bf16[384,512]{1,0:T(8,128)(2,1)} %copy-done.2, s32[3,768]{1,0:T(4,128)} %pad_add_fusion.ids_ref, bf16[160,512]{1,0:T(8,128)(2,1)} %nodes_in.3, bf16[96,512]{1,0:T(8,128)(2,1)} %all_gather.13.rims_in, ...), custom_call_target="tpu_custom_call" | custom-call | flops 1073741824 | bytes 4205572 | tf_op jit(solution)/shard_map/pallas_call | solution.py:88
  47.1 0.0 all-to-all-done.1
  47.1 0.0 copy-start.1
  47.1 0.8 copy-done.1
  47.9 9.4 %shard_map.187 = (bf16[160,512]{1,0:T(8,128)(2,1)}, bf16[768,512]{1,0:T(8,128)(2,1)}, bf16[256,512]{1,0:T(8,128)(2,1)}, bf16[48,512]{1,0:T(8,128)(2,1)}, f32[160...) custom-call(s32[1]{0:T(128)} %bitcast.core_ref, bf16[512,512]{1,0:T(8,128)(2,1)} %bitcast.13, ...), custom_call_target="tpu_custom_call" | custom-call | flops 2684354560 | bytes 7932932 | tf_op jit(solution)/shard_map/pallas_call | solution.py:88
  57.4 6.9 %all-to-all-start.2 = ((bf16[16,16,512]{2,1,0:T(8,128)(2,1)}), bf16[16,16,512]{2,1,0:T(8,128)(2,1)S(1)}, u32[]{:S(2)}, u32[]{:S(2)}) async-start(bf16[16,16,512]{2,1,0:T(8,128)(2,1)} %bitcast.14), calls=%async_computation.2 | async-start | bytes 524288 | tf_op jit(solution)/shard_map/all_to_all | solution.py:477
  64.3 3.3 %collective-permute-start.2 = (bf16[48,512]{1,0:T(8,128)(2,1)}, bf16[48,512]{1,0:T(8,128)(2,1)S(1)}, u32[]{:S(2)}, u32[]{:S(2)}) collective-permute-start(bf16[48,512]{1,0:T(8,128)(2,1)} %get-tuple-element.23), channel_id=1, source_target_pairs={{1,3},{2,0},{3,5},{4,2},{5,7},{6,4},{7,9},{8,6},{9,11},{10,8},{11,... | collective-permute-start | bytes 147464 | tf_op jit(solution)/shard_map/ppermute | solution.py:363
  67.6 4.9 %all-to-all-done.2.sums_ref = bf16[16,16,512]{2,1,0:T(8,128)(2,1)S(1)} async-done(((bf16[16,16,512]{2,1,0:T(8,128)(2,1)}), bf16[16,16,512]{2,1,0:T(8,128)(2,1)S(1)}, u32[]{:S(2)}, u32[]{:S(2)}) %all-to-all-start.2) | async-done | bytes 262176 | tf_op jit(solution)/shard_map/all_to_all | solution.py:477
  72.5 1.0 %shard_map.188 = f32[64,128]{1,0:T(8,128)} custom-call(bf16[16,16,512]{2,1,0:T(8,128)(2,1)S(1)} %all-to-all-done.2.sums_ref), custom_call_target="tpu_custom_call" | custom-call | bytes 294912 | tf_op jit(solution)/shard_map/pallas_call | solution.py:88
  73.5 6.9 %all-to-all-start.3 = ((f32[16,4,128]{2,1,0:T(4,128)}), f32[16,4,128]{2,1,0:T(4,128)S(1)}, u32[]{:S(2)}, u32[]{:S(2)}) async-start(f32[16,4,128]{2,1,0:T(4,128)} %bitcast.10), calls=%async_computation.3 | async-start | bytes 65536 | tf_op jit(solution)/shard_map/all_to_all | solution.py:487
  80.3 0.0 collective-permute-done.2
  80.3 4.1 %all_gather.15.rims_in = bf16[96,512]{1,0:T(8,128)(2,1)} all-gather(bf16[48,512]{1,0:T(8,128)(2,1)S(1)} %collective-permute-done.2), channel_id=1, replica_groups=mesh['y'=4,'z'=16,'x'=4,'c'=2] {'c'}, dimensions={0}, use_global_device_ids=true | all-gather | bytes 147456 | tf_op jit(solution)/shard_map/all_gather | solution.py:489
  84.4 4.4 %shard_map.189 = (bf16[384,512]{1,0:T(8,128)(2,1)}, bf16[160,512]{1,0:T(8,128)(2,1)}, f32[16,512]{1,0:T(8,128)}) custom-call(s32[1]{0:T(128)} %bitcast.core_ref, bf16[768,512]{1,0:T(8,128)(2,1)} %get-tuple-element.19.dpre_in, s32[3,768]{1,0:T(4,128)} %pad_add_fusion.ids_ref, f32[160,512]{1,0:T(8,128)} %get-tuple-element.20.gg_in, ...), custom_call_target="tpu_custom_call" | custom-call | flops 805306368 | bytes 5088260 | tf_op jit(solution)/shard_map/pallas_call | solution.py:88
  88.9 2.9 %all-to-all-done.3 = f32[16,4,128]{2,1,0:T(4,128)S(1)} async-done(((f32[16,4,128]{2,1,0:T(4,128)}), f32[16,4,128]{2,1,0:T(4,128)S(1)}, u32[]{:S(2)}, u32[]{:S(2)}) %all-to-all-start.3) | async-done | bytes 32800 | tf_op jit(solution)/shard_map/all_to_all | solution.py:487
  91.8 5.1 %all_gather.14.hub_ref = f32[128,128]{1,0:T(8,128)S(1)} all-gather(f32[64,128]{1,0:T(8,128)S(1)} %bitcast.15), channel_id=1, replica_groups=mesh['y'=4,'z'=16,'x'=4,'c'=2] {'c'}, dimensions={0}, use_global_device_ids=true | all-gather | bytes 98304 | tf_op jit(solution)/shard_map/all_gather | solution.py:488
  96.9 0.0 copy-start
  96.9 0.8 copy-done
  97.6 0.6 shard_map.190
  (3 shorter events, 0.1 us)
Async XLA Ops:
  2.2 27.3 %all-to-all-start = ((f32[16,8,128]{2,1,0:T(8,128)}), f32[16,8,128]{2,1,0:T(8,128)S(1)}, u32[]{:S(2)}, u32[]{:S(2)}) async-start(f32[16,8,128]{2,1,0:T(8,128)} %get-tuple-element.15), calls=%async_computation | async-start | bytes 131072 | tf_op jit(solution)/shard_map/all_to_all | solution.py:406
  17.9 19.9 %collective-permute-start.1 = (bf16[48,512]{1,0:T(8,128)(2,1)}, bf16[48,512]{1,0:T(8,128)(2,1)S(1)}, u32[]{:S(2)}, u32[]{:S(2)}) collective-permute-start(bf16[48,512]{1,0:T(8,128)(2,1)} %get-tuple-element.16), channel_id=1, source_target_pairs={{0,2},{2,4},{3,1},{4,6},{5,3},{6,8},{7,5},{8,10},{9,7},{10,12},{11... | collective-permute-start | bytes 147464 | tf_op jit(solution)/shard_map/ppermute | solution.py:363
  19.2 22.6 %collective-permute-start = (bf16[384,512]{1,0:T(8,128)(2,1)}, bf16[384,512]{1,0:T(8,128)(2,1)S(1)}, u32[]{:S(2)}, u32[]{:S(2)}) collective-permute-start(bf16[384,512]{1,0:T(8,128)(2,1)} %own_in.3), channel_id=1, source_target_pairs={{0,1},{1,0},{2,3},{3,2},{4,5},{5,4},{6,7},{7,6},{8,9},{9,8},{10,11... | collective-permute-start | bytes 1179656 | tf_op jit(solution)/shard_map/ppermute | solution.py:416
  30.4 16.8 %all-to-all-start.1 = ((bf16[16,32,512]{2,1,0:T(8,128)(2,1)}), bf16[16,32,512]{2,1,0:T(8,128)(2,1)S(1)}, u32[]{:S(2)}, u32[]{:S(2)}) async-start(bf16[16,32,512]{2,1,0:T(8,128)(2,1)} %shard_map.185), calls=%async_computation.1 | async-start | bytes 1048576 | tf_op jit(solution)/shard_map/all_to_all | solution.py:413
  41.9 0.7 copy-start.2
  47.1 0.8 copy-start.1
  57.4 15.1 %all-to-all-start.2 = ((bf16[16,16,512]{2,1,0:T(8,128)(2,1)}), bf16[16,16,512]{2,1,0:T(8,128)(2,1)S(1)}, u32[]{:S(2)}, u32[]{:S(2)}) async-start(bf16[16,16,512]{2,1,0:T(8,128)(2,1)} %bitcast.14), calls=%async_computation.2 | async-start | bytes 524288 | tf_op jit(solution)/shard_map/all_to_all | solution.py:477
  64.3 16.0 %collective-permute-start.2 = (bf16[48,512]{1,0:T(8,128)(2,1)}, bf16[48,512]{1,0:T(8,128)(2,1)S(1)}, u32[]{:S(2)}, u32[]{:S(2)}) collective-permute-start(bf16[48,512]{1,0:T(8,128)(2,1)} %get-tuple-element.23), channel_id=1, source_target_pairs={{1,3},{2,0},{3,5},{4,2},{5,7},{6,4},{7,9},{8,6},{9,11},{10,8},{11,... | collective-permute-start | bytes 147464 | tf_op jit(solution)/shard_map/ppermute | solution.py:363
  73.5 18.4 %all-to-all-start.3 = ((f32[16,4,128]{2,1,0:T(4,128)}), f32[16,4,128]{2,1,0:T(4,128)S(1)}, u32[]{:S(2)}, u32[]{:S(2)}) async-start(f32[16,4,128]{2,1,0:T(4,128)} %bitcast.10), calls=%async_computation.3 | async-start | bytes 65536 | tf_op jit(solution)/shard_map/all_to_all | solution.py:487
  96.9 0.8 copy-start

commit v8 on v7

--- a/solution.py
+++ b/solution.py
@@ -18,7 +18,6 @@
 SPACE = ("y", "z", "x")
 PLANE = ("y", "x")
 LANES = 128
-NEAR_TILE = 384
 MAIN_TILE = 768
 SHAPE = (4, 16, 4)
 GRANT = 60 * 1024 * 1024
@@ -161,41 +160,24 @@
 
 
 def near_kernel(
-    core_ref, own_in, other_in, ids_ref, nodes_in, rims_in, we_in, ws_in, wr_in, bias_ref,
-    pre_out,
-    edges_ref, frame_ref, we_ref, ws_ref, wr_ref, send_ref, recv_ref, pre_ref, sems,
+    core_ref, own_ref, other_ref, ids_ref, nodes_ref, rims_ref, we_ref, ws_ref, wr_ref, bias_ref,
+    pre_ref,
+    frame_ref, send_ref, recv_ref,
 ):
-    node_count = nodes_in.shape[0]
+    node_count = nodes_ref.shape[0]
+    half = own_ref.shape[0]
     slots = 2 * RIM + node_count
-    copies = start_copies(
-        [
-            (nodes_in, frame_ref.at[pl.ds(RIM, node_count)]),
-            (rims_in.at[pl.ds(0, RIM)], frame_ref.at[pl.ds(0, RIM)]),
-            (rims_in.at[pl.ds(RIM, RIM)], frame_ref.at[pl.ds(RIM + node_count, RIM)]),
-            (ws_in, ws_ref),
-            (wr_in, wr_ref),
-            (we_in, we_ref),
-        ]
-        + edge_pairs(core_ref, own_in, other_in, edges_ref),
-        sems,
-    )
-    for copy in copies[:4]:
-        copy.wait()
+    frame_ref[:RIM] = rims_ref[:RIM]
+    frame_ref[RIM : RIM + node_count] = nodes_ref[...]
+    frame_ref[RIM + node_count :] = rims_ref[RIM:]
     send_ref[...] = dot(frame_ref[...], ws_ref[...]).astype(BF)
-    copies[4].wait()
     recv_ref[...] = dot(frame_ref[...], wr_ref[...]).astype(BF)
-    for copy in copies[5:]:
-        copy.wait()
-    back = []
-    for i in range(edges_ref.shape[0] // NEAR_TILE):
-        rows = pl.ds(i * NEAR_TILE, NEAR_TILE)
-        pre = dot(edges_ref[rows, :], we_ref[...])
+    for edges_ref, at in ((own_ref, core_ref[0]), (other_ref, 1 - core_ref[0])):
+        rows = pl.ds(pl.multiple_of(at * half, half), half)
+        pre = dot(edges_ref[...], we_ref[...])
         pre += dot(hot_rows(ids_ref[0:1, rows], 0, slots), send_ref[...])
         pre += dot(hot_rows(ids_ref[1:2, rows], 0, slots), recv_ref[...])
         pre_ref[rows, :] = pre + bias_ref[...]
-        back += start_copies([(pre_ref.at[rows], pre_out.at[rows])], sems, len(copies) + i)
-    for copy in back:
-        copy.wait()
 
 
 def main_kernel(
@@ -213,14 +195,15 @@
     slots = 2 * RIM + node_count
     own = slice(RIM, RIM + node_count)
     tiles = [pl.ds(i * MAIN_TILE, MAIN_TILE) for i in range(steps)]
-    hubs, ws, wo, *rest = start_copies(
-        [(hubs_in, hubs_ref), (ws_in, ws_ref), (wo_in, wo_ref)]
+    hubs, ws, *rest = start_copies(
+        [(hubs_in, hubs_ref), (ws_in, ws_ref)]
         + [(pre_in.at[rows], pre_ref.at[rows]) for rows in tiles]
+        + [(wo_in, wo_ref)]
         + edge_pairs(core_ref, own_in, other_in, edges_ref)
         + [(nodes_in, nodes_ref), (cot_in, cot_ref), (win_in, win_ref), (wout_in, wout_ref)],
         sems,
     )
-    done = 3 + len(rest)
+    done = 2 + len(rest)
     gathered_ref[...] = jnp.zeros_like(gathered_ref)
     hubs.wait()
     ws.wait()
@@ -228,9 +211,8 @@
     for i, rows in enumerate(tiles):
         rest[i].wait()
         if i == 0:
-            wo.wait()
-            rest[steps].wait()
-            rest[steps + 1].wait()
+            for copy in rest[steps : steps + 3]:
+                copy.wait()
         pre = pre_ref[rows, :] + dot(hot_rows(ids_ref[0:1, rows], slots, hub_count), terms_ref[...])
         gate = jax.nn.sigmoid(pre)
         act = pre * gate
@@ -242,7 +224,7 @@
         new_edges = edges_ref[rows, :].astype(F32) + normed * egain_ref[...] + eshift_ref[...]
         gathered_ref[...] += dot(hot_cols(ids_ref[1:2, rows], 0, slots), new_edges.astype(BF))
 
-    for copy in rest[steps + 2 :]:
+    for copy in rest[steps + 3 :]:
         copy.wait()
     nodes = nodes_ref[...]
     gathered = gathered_ref[own].astype(BF)
@@ -414,7 +396,8 @@
 
     rims = lax.all_gather(rim, "c", axis=0, tiled=True)
     other = lax.ppermute(edges, "c", [(0, 1), (1, 0)])
-    ids = lax.all_gather(jnp.stack([senders, receivers]), "c", axis=1, tiled=True)
+    ids = jnp.stack([senders, receivers])
+    ids = lax.all_gather(ids, "c", axis=1, tiled=True)
     block = ids[0] // node_count
     line = ids[0] - block * node_count
     hub_y, hub_zx = block // (nz * nx), block % (nz * nx)
@@ -439,14 +422,13 @@
     (near,) = call(
         near_kernel,
         [
-            (core.reshape(1), SM), (edges, HB), (other, HB), (ids, VM), (nodes, HB), (rims, HB),
-            (edge_proj, HB), (send_proj, HB), (recv_proj, HB), row(edge_bias),
+            (core.reshape(1), SM), (edges, VM), (other, VM), (ids, VM), (nodes, VM), (rims, VM),
+            (edge_proj, VM), (send_proj, VM), (recv_proj, VM), row(edge_bias),
         ],
-        [((edge_count, width), F32, HB)],
-        [wide(edge_count)] + [wide(slots)] + [wide(width)] * 3 + [wide(slots)] * 2
-        + [wide(edge_count, F32)],
-        copies=8 + edge_count // NEAR_TILE,
+        [((edge_count, width), F32, VM)],
+        [wide(slots)] * 3,
         flops=square * (edge_count * 2 + 2 * slots),
+        room=46000,
     )
     new_nodes, dpre, hub_sums, my_rim, own_sums, gathered_grad, node_dpre = call(
         main_kernel,

time: 99.2 us -> 99.8 us (level)
  Pallas kernels: 22.4 us -> 19.2 us
  blocking collectives: 15 us -> 17.1 us
    all_to_all x1, starting transfers between devices: 6.87 us -> 10.3 us  [layer(): hub_back = lax.all_to_all(by_z.reshape(nz, 4, LANES), 'z', 0, 0)]
    pallas_call x7, Pallas kernels: 22.4 us -> 19.2 us  [call(): pl.pallas_call(kernel, out_shape=shapes, in_specs=[spec for _, spec in in...]
    all_to_all x1, starting transfers between devices: 6.93 us -> 4.21 us  [layer(): hub_back = lax.all_to_all(hub_sums.reshape(plane, nz, width), PLANE, 0, 0)]
    all_to_all x1, waiting for transfers between devices: 0.01 us -> 2.72 us  [layer(): hubs = lax.all_to_all(spread, PLANE, 0, 0).reshape(hub_count, width)]
    all_gather x1, blocking collectives: 5.07 us -> 6.22 us  [layer(): lax.all_gather(hub_back.reshape(nz * 4, LANES), 'c', axis=0, tiled=True)]
    all_to_all x1, waiting for transfers between devices: 2.95 us -> 1.84 us  [layer(): hub_back = lax.all_to_all(by_z.reshape(nz, 4, LANES), 'z', 0, 0)]
    all_gather x2, blocking collectives: 8.07 us -> 9.11 us  [layer(): rims = lax.all_gather(rim, 'c', axis=0, tiled=True)]
    unnamed x6 -> x22, local copies, waits for them, and re-layouts: 2.3 us -> 2.78 us
  transfers between devices with their start and end apart: 7 -> 7, of which waited for: 3 -> 4; matrix products, arithmetic and copies ran while one was open for 2% -> 2% of each run, Pallas kernels for 11% -> 8%
where the time goes in v8:
time: 99.8 us; the launch traced here: 99 us
  starting transfers between devices  46.5 us (47%)
  Pallas kernels  19.2 us (19%)
  blocking collectives  17.1 us (17%)
  waiting for transfers between devices  10.9 us (11%)
  local copies, waits for them, and re-layouts  4.14 us (4%)
    pallas_call x7, Pallas kernels, call(): pl.pallas_call(kernel, out_shape=shapes, in_specs=[spec for _, spec in in...  19.2 us
    all_to_all x1, starting transfers between devices, layer(): by_z = lax.all_to_all(my_hub, 'z', 0, 0)  15.7 us
    all_to_all x1, starting transfers between devices, layer(): hub_back = lax.all_to_all(by_z.reshape(nz, 4, LANES), 'z', 0, 0)  10.3 us
    all_gather x2, blocking collectives, layer(): rims = lax.all_gather(rim, 'c', axis=0, tiled=True)  9.11 us
    all_to_all x1, starting transfers between devices, layer(): hubs = lax.all_to_all(spread, PLANE, 0, 0).reshape(hub_count, width)  6.75 us
    all_gather x1, blocking collectives, layer(): lax.all_gather(hub_back.reshape(nz * 4, LANES), 'c', axis=0, tiled=True)  6.22 us
    ppermute x1, starting transfers between devices, layer(): other = lax.ppermute(edges, 'c', [(0, 1), (1, 0)])  4.97 us
    ppermute x2, starting transfers between devices, both_ways(): return lax.ppermute(x, ALL, pairs)  4.55 us
  transfers between devices with their start and end apart: 7, of which 4 were waited for; matrix products, arithmetic and copies ran while one was open for 2% of the time, Pallas kernels for 8%

profile of v8, /device:TPU:1, one launch (start us, length us, event | category | flops | bytes accessed | tf_op | source)
XLA Modules:
  0.0 99.0 jit_solution(13129359243550875304)
XLA Ops:
  0.6 0.0 copy-start.4
  0.6 0.0 copy-start.5
  0.7 0.0 copy-start.1
  0.7 0.0 copy-start.2
  0.7 0.0 copy-start
  0.7 0.0 copy-start.9
  0.7 1.6 %shard_map.184 = (f32[16,8,128]{2,1,0:T(8,128)}, bf16[48,512]{1,0:T(8,128)(2,1)}) custom-call(s32[1]{0:T(128)} %bitcast.core_ref, bf16[160,512]{1,0:T(8,128)(2,1)} %nodes_in.1), custom_call_target="tpu_custom_call" | custom-call | bytes 278532 | tf_op jit(solution)/shard_map/pallas_call | solution.py:87
  2.3 15.7 %all-to-all-start = ((f32[16,8,128]{2,1,0:T(8,128)}), f32[16,8,128]{2,1,0:T(8,128)S(1)}, u32[]{:S(2)}, u32[]{:S(2)}) async-start(f32[16,8,128]{2,1,0:T(8,128)} %get-tuple-element.15), calls=%async_computation | async-start | bytes 131072 | tf_op jit(solution)/shard_map/all_to_all | solution.py:388
  18.1 1.3 %collective-permute-start.1 = (bf16[48,512]{1,0:T(8,128)(2,1)}, bf16[48,512]{1,0:T(8,128)(2,1)S(1)}, u32[]{:S(2)}, u32[]{:S(2)}) collective-permute-start(bf16[48,512]{1,0:T(8,128)(2,1)} %get-tuple-element.16), channel_id=1, source_target_pairs={{0,2},{2,4},{3,1},{4,6},{5,3},{6,8},{7,5},{8,10},{9,7},{10,12},{11... | collective-permute-start | bytes 147464 | tf_op jit(solution)/shard_map/ppermute | solution.py:345
  19.4 5.0 %collective-permute-start = (bf16[384,512]{1,0:T(8,128)(2,1)}, bf16[384,512]{1,0:T(8,128)(2,1)S(1)}, u32[]{:S(2)}, u32[]{:S(2)}) collective-permute-start(bf16[384,512]{1,0:T(8,128)(2,1)} %own_in.1), channel_id=1, source_target_pairs={{0,1},{1,0},{2,3},{3,2},{4,5},{5,4},{6,7},{7,6},{8,9},{9,8},{10,11... | collective-permute-start | bytes 1179656 | tf_op jit(solution)/shard_map/ppermute | solution.py:398
  24.4 0.7 stack.15
  25.0 0.7 stack.16
  25.7 1.8 %all_gather.12 = s32[2,768]{1,0:T(2,128)S(1)} all-gather(s32[2,384]{1,0:T(2,128)S(1)} %pad_add_fusion.1), channel_id=1, replica_groups=mesh['y'=4,'z'=16,'x'=4,'c'=2] {'c'}, dimensions={1}, use_global_device_ids=true | all-gather | bytes 9216 | tf_op jit(solution)/shard_map/all_gather | solution.py:400
  27.6 2.0 %all-to-all-done = f32[16,8,128]{2,1,0:T(8,128)S(1)} async-done(((f32[16,8,128]{2,1,0:T(8,128)}), f32[16,8,128]{2,1,0:T(8,128)S(1)}, u32[]{:S(2)}, u32[]{:S(2)}) %all-to-all-start) | async-done | bytes 65568 | tf_op jit(solution)/shard_map/all_to_all | solution.py:388
  29.6 0.8 shard_map.185
  30.5 6.8 %all-to-all-start.1 = ((bf16[16,32,512]{2,1,0:T(8,128)(2,1)}), bf16[16,32,512]{2,1,0:T(8,128)(2,1)S(1)}, u32[]{:S(2)}, u32[]{:S(2)}) async-start(bf16[16,32,512]{2,1,0:T(8,128)(2,1)} %shard_map.185), calls=%async_computation.1 | async-start | bytes 1048576 | tf_op jit(solution)/shard_map/all_to_all | solution.py:395
  37.3 0.1 compare_select_fusion.6
  37.4 0.0 copy-start.7
  37.4 0.0 collective-permute-done.1
  37.4 3.9 %all_gather.13.rims_ref = bf16[96,512]{1,0:T(8,128)(2,1)S(1)} all-gather(bf16[48,512]{1,0:T(8,128)(2,1)S(1)} %collective-permute-done.1), channel_id=1, replica_groups=mesh['y'=4,'z'=16,'x'=4,'c'=2] {'c'}, dimensions={0}, use_global_device_ids=true | all-gather | bytes 147456 | tf_op jit(solution)/shard_map/all_gather | solution.py:397
  41.3 0.0 collective-permute-done.other_ref.other_in
  41.3 0.0 copy-start.6
  41.3 0.0 copy-done.4
  41.3 0.0 copy-done.5
  41.3 0.0 copy-done.1
  41.4 0.0 copy-done.2
  41.4 0.0 copy-done
  41.4 0.0 copy-done.9
  41.4 1.3 %shard_map.186.pre_in = f32[768,512]{1,0:T(8,128)S(1)} custom-call(s32[1]{0:T(128)} %bitcast.core_ref, bf16[384,512]{1,0:T(8,128)(2,1)S(1)} %copy-done.5, bf16[384,512]{1,0:T(8,128)(2,1)S(1)} %collective-permute-done.other_ref.other_in, s32[3,768]{1,0:T(4,128)S(1)} %pad_add_fusion.ids_ref, bf16[160,512]{1,0:T(8,128)(2,1)S(1)} %copy-done.4, ...), custom_call_target="tpu_custom_call" | custom-call | flops 1073741824 | bytes 4205572 | tf_op jit(solution)/shard_map/pallas_call | solution.py:87
  42.7 0.0 copy-done.7
  42.7 0.0 copy-done.6
  42.7 0.0 copy-start.3
  42.7 1.2 %copy-done.3 = f32[768,512]{1,0:T(8,128)} copy-done((f32[768,512]{1,0:T(8,128)}, f32[768,512]{1,0:T(8,128)S(1)}, u32[]{:S(2)}) %copy-start.3) | copy-done | bytes 1572888
  43.9 2.7 %all-to-all-done.1 = bf16[16,32,512]{2,1,0:T(8,128)(2,1)S(1)} async-done(((bf16[16,32,512]{2,1,0:T(8,128)(2,1)}), bf16[16,32,512]{2,1,0:T(8,128)(2,1)S(1)}, u32[]{:S(2)}, u32[]{:S(2)}) %all-to-all-start.1) | async-done | bytes 524320 | tf_op jit(solution)/shard_map/all_to_all | solution.py:395
  46.6 0.8 copy-done.10
  47.4 9.4 %shard_map.187 = (bf16[160,512]{1,0:T(8,128)(2,1)}, bf16[768,512]{1,0:T(8,128)(2,1)}, bf16[256,512]{1,0:T(8,128)(2,1)}, bf16[48,512]{1,0:T(8,128)(2,1)}, f32[160...) custom-call(s32[1]{0:T(128)} %bitcast.core_ref, bf16[512,512]{1,0:T(8,128)(2,1)} %bitcast.14, ...), custom_call_target="tpu_custom_call" | custom-call | flops 2684354560 | bytes 7932932 | tf_op jit(solution)/shard_map/pallas_call | solution.py:87
  56.8 4.2 %all-to-all-start.2 = ((bf16[16,16,512]{2,1,0:T(8,128)(2,1)}), bf16[16,16,512]{2,1,0:T(8,128)(2,1)S(1)}, u32[]{:S(2)}, u32[]{:S(2)}) async-start(bf16[16,16,512]{2,1,0:T(8,128)(2,1)} %bitcast.15), calls=%async_computation.2 | async-start | bytes 524288 | tf_op jit(solution)/shard_map/all_to_all | solution.py:459
  61.0 3.3 %collective-permute-start.2 = (bf16[48,512]{1,0:T(8,128)(2,1)}, bf16[48,512]{1,0:T(8,128)(2,1)S(1)}, u32[]{:S(2)}, u32[]{:S(2)}) collective-permute-start(bf16[48,512]{1,0:T(8,128)(2,1)} %get-tuple-element.23), channel_id=1, source_target_pairs={{1,3},{2,0},{3,5},{4,2},{5,7},{6,4},{7,9},{8,6},{9,11},{10,8},{11,... | collective-permute-start | bytes 147464 | tf_op jit(solution)/shard_map/ppermute | solution.py:345
  64.3 4.3 %all-to-all-done.2.sums_ref = bf16[16,16,512]{2,1,0:T(8,128)(2,1)S(1)} async-done(((bf16[16,16,512]{2,1,0:T(8,128)(2,1)}), bf16[16,16,512]{2,1,0:T(8,128)(2,1)S(1)}, u32[]{:S(2)}, u32[]{:S(2)}) %all-to-all-start.2) | async-done | bytes 262176 | tf_op jit(solution)/shard_map/all_to_all | solution.py:459
  68.6 1.0 %shard_map.188 = f32[64,128]{1,0:T(8,128)} custom-call(bf16[16,16,512]{2,1,0:T(8,128)(2,1)S(1)} %all-to-all-done.2.sums_ref), custom_call_target="tpu_custom_call" | custom-call | bytes 294912 | tf_op jit(solution)/shard_map/pallas_call | solution.py:87
  69.6 10.3 %all-to-all-start.3 = ((f32[16,4,128]{2,1,0:T(4,128)}), f32[16,4,128]{2,1,0:T(4,128)S(1)}, u32[]{:S(2)}, u32[]{:S(2)}) async-start(f32[16,4,128]{2,1,0:T(4,128)} %bitcast.10), calls=%async_computation.3 | async-start | bytes 65536 | tf_op jit(solution)/shard_map/all_to_all | solution.py:469
  79.9 0.0 collective-permute-done.2
  79.9 5.2 %all_gather.15.rims_in = bf16[96,512]{1,0:T(8,128)(2,1)} all-gather(bf16[48,512]{1,0:T(8,128)(2,1)S(1)} %collective-permute-done.2), channel_id=1, replica_groups=mesh['y'=4,'z'=16,'x'=4,'c'=2] {'c'}, dimensions={0}, use_global_device_ids=true | all-gather | bytes 147456 | tf_op jit(solution)/shard_map/all_gather | solution.py:471
  85.1 4.4 %shard_map.189 = (bf16[384,512]{1,0:T(8,128)(2,1)}, bf16[160,512]{1,0:T(8,128)(2,1)}, f32[16,512]{1,0:T(8,128)}) custom-call(s32[1]{0:T(128)} %bitcast.core_ref, bf16[768,512]{1,0:T(8,128)(2,1)} %get-tuple-element.19.dpre_in, s32[3,768]{1,0:T(4,128)} %copy-done.7, f32[160,512]{1,0:T(8,128)} %get-tuple-element.20.gg_in, ...), custom_call_target="tpu_custom_call" | custom-call | flops 805306368 | bytes 5088260 | tf_op jit(solution)/shard_map/pallas_call | solution.py:87
  89.5 1.8 %all-to-all-done.3 = f32[16,4,128]{2,1,0:T(4,128)S(1)} async-done(((f32[16,4,128]{2,1,0:T(4,128)}), f32[16,4,128]{2,1,0:T(4,128)S(1)}, u32[]{:S(2)}, u32[]{:S(2)}) %all-to-all-start.3) | async-done | bytes 32800 | tf_op jit(solution)/shard_map/all_to_all | solution.py:469
  91.4 6.2 %all_gather.14.hub_ref = f32[128,128]{1,0:T(8,128)S(1)} all-gather(f32[64,128]{1,0:T(8,128)S(1)} %bitcast.16), channel_id=1, replica_groups=mesh['y'=4,'z'=16,'x'=4,'c'=2] {'c'}, dimensions={0}, use_global_device_ids=true | all-gather | bytes 98304 | tf_op jit(solution)/shard_map/all_gather | solution.py:470
  97.6 0.8 copy-done.8
  98.4 0.6 shard_map.190
  (6 shorter events, 0.1 us)
Async XLA Ops:
  0.6 40.7 %copy-start.4 = (bf16[160,512]{1,0:T(8,128)(2,1)S(1)}, bf16[160,512]{1,0:T(8,128)(2,1)}, u32[]{:S(2)}) copy-start(bf16[160,512]{1,0:T(8,128)(2,1)} %nodes_in.1) | copy-start | bytes 491524
  0.6 40.7 %copy-start.5 = (bf16[384,512]{1,0:T(8,128)(2,1)S(1)}, bf16[384,512]{1,0:T(8,128)(2,1)}, u32[]{:S(2)}) copy-start(bf16[384,512]{1,0:T(8,128)(2,1)} %own_in.1) | copy-start | bytes 1179652
  0.7 40.7 %copy-start.1 = (bf16[512,512]{1,0:T(8,128)(2,1)S(1)}, bf16[512,512]{1,0:T(8,128)(2,1)}, u32[]{:S(2)}) copy-start(bf16[512,512]{1,0:T(8,128)(2,1)} %ws_in.3) | copy-start | bytes 1572868
  0.7 40.7 %copy-start.2 = (bf16[512,512]{1,0:T(8,128)(2,1)S(1)}, bf16[512,512]{1,0:T(8,128)(2,1)}, u32[]{:S(2)}) copy-start(bf16[512,512]{1,0:T(8,128)(2,1)} %wr_in.1) | copy-start | bytes 1572868
  0.7 40.7 %copy-start = (bf16[512,512]{1,0:T(8,128)(2,1)S(1)}, bf16[512,512]{1,0:T(8,128)(2,1)}, u32[]{:S(2)}) copy-start(bf16[512,512]{1,0:T(8,128)(2,1)} %we_in.1) | copy-start | bytes 1572868
  0.7 40.7 %copy-start.9 = (f32[512]{0:T(512)S(1)}, f32[512]{0:T(512)}, u32[]{:S(2)}) copy-start(f32[512]{0:T(512)} %param.24) | copy-start | bytes 6148
  2.3 27.3 %all-to-all-start = ((f32[16,8,128]{2,1,0:T(8,128)}), f32[16,8,128]{2,1,0:T(8,128)S(1)}, u32[]{:S(2)}, u32[]{:S(2)}) async-start(f32[16,8,128]{2,1,0:T(8,128)} %get-tuple-element.15), calls=%async_computation | async-start | bytes 131072 | tf_op jit(solution)/shard_map/all_to_all | solution.py:388
  18.1 19.3 %collective-permute-start.1 = (bf16[48,512]{1,0:T(8,128)(2,1)}, bf16[48,512]{1,0:T(8,128)(2,1)S(1)}, u32[]{:S(2)}, u32[]{:S(2)}) collective-permute-start(bf16[48,512]{1,0:T(8,128)(2,1)} %get-tuple-element.16), channel_id=1, source_target_pairs={{0,2},{2,4},{3,1},{4,6},{5,3},{6,8},{7,5},{8,10},{9,7},{10,12},{11... | collective-permute-start | bytes 147464 | tf_op jit(solution)/shard_map/ppermute | solution.py:345
  19.4 22.0 %collective-permute-start = (bf16[384,512]{1,0:T(8,128)(2,1)}, bf16[384,512]{1,0:T(8,128)(2,1)S(1)}, u32[]{:S(2)}, u32[]{:S(2)}) collective-permute-start(bf16[384,512]{1,0:T(8,128)(2,1)} %own_in.1), channel_id=1, source_target_pairs={{0,1},{1,0},{2,3},{3,2},{4,5},{5,4},{6,7},{7,6},{8,9},{9,8},{10,11... | collective-permute-start | bytes 1179656 | tf_op jit(solution)/shard_map/ppermute | solution.py:398
  30.5 16.1 %all-to-all-start.1 = ((bf16[16,32,512]{2,1,0:T(8,128)(2,1)}), bf16[16,32,512]{2,1,0:T(8,128)(2,1)S(1)}, u32[]{:S(2)}, u32[]{:S(2)}) async-start(bf16[16,32,512]{2,1,0:T(8,128)(2,1)} %shard_map.185), calls=%async_computation.1 | async-start | bytes 1048576 | tf_op jit(solution)/shard_map/all_to_all | solution.py:395
  37.4 5.3 %copy-start.7 = (s32[3,768]{1,0:T(4,128)}, s32[3,768]{1,0:T(4,128)S(1)}, u32[]{:S(2)}) copy-start(s32[3,768]{1,0:T(4,128)S(1)} %pad_add_fusion.ids_ref) | copy-start | bytes 27652
  41.3 1.3 %copy-start.6 = (bf16[384,512]{1,0:T(8,128)(2,1)}, bf16[384,512]{1,0:T(8,128)(2,1)S(1)}, u32[]{:S(2)}) copy-start(bf16[384,512]{1,0:T(8,128)(2,1)S(1)} %collective-permute-done.other_ref.other_in) | copy-start | bytes 1179652
  42.7 1.2 %copy-start.3 = (f32[768,512]{1,0:T(8,128)}, f32[768,512]{1,0:T(8,128)S(1)}, u32[]{:S(2)}) copy-start(f32[768,512]{1,0:T(8,128)S(1)} %shard_map.186.pre_in) | copy-start | bytes 4718596
  46.6 0.8 copy-start.10
  56.8 11.8 %all-to-all-start.2 = ((bf16[16,16,512]{2,1,0:T(8,128)(2,1)}), bf16[16,16,512]{2,1,0:T(8,128)(2,1)S(1)}, u32[]{:S(2)}, u32[]{:S(2)}) async-start(bf16[16,16,512]{2,1,0:T(8,128)(2,1)} %bitcast.15), calls=%async_computation.2 | async-start | bytes 524288 | tf_op jit(solution)/shard_map/all_to_all | solution.py:459
  61.0 18.9 %collective-permute-start.2 = (bf16[48,512]{1,0:T(8,128)(2,1)}, bf16[48,512]{1,0:T(8,128)(2,1)S(1)}, u32[]{:S(2)}, u32[]{:S(2)}) collective-permute-start(bf16[48,512]{1,0:T(8,128)(2,1)} %get-tuple-element.23), channel_id=1, source_target_pairs={{1,3},{2,0},{3,5},{4,2},{5,7},{6,4},{7,9},{8,6},{9,11},{10,8},{11,... | collective-permute-start | bytes 147464 | tf_op jit(solution)/shard_map/ppermute | solution.py:345
  69.6 21.8 %all-to-all-start.3 = ((f32[16,4,128]{2,1,0:T(4,128)}), f32[16,4,128]{2,1,0:T(4,128)S(1)}, u32[]{:S(2)}, u32[]{:S(2)}) async-start(f32[16,4,128]{2,1,0:T(4,128)} %bitcast.10), calls=%async_computation.3 | async-start | bytes 65536 | tf_op jit(solution)/shard_map/all_to_all | solution.py:469
  97.6 0.8 copy-start.8
